TPU v7x, 512 devices: a whole 4x4x16 slice. The times are simulated.
512 devices in a mesh: blk: 128 (over z, y, core), grp: 4 (over x).
Axes of the slice: x: 4, y: 4, z: 16, core: 2. Of those that a mesh axis runs over, the one named last changes fastest.
Arguments:
- voxels: bfloat16 [1024, 64, 64, 128], P('blk', 'grp'), may hold values from -6 to 6
- shell_lo: int32 [1024, 64], P('blk', 'grp'), may hold values from 0 to 127, as said below
- shell_hi: int32 [1024, 64], P('blk', 'grp'), may hold values from 1 to 128, as said below
- conv_weight: bfloat16 [3, 3, 3, 64, 64], replicated, may hold values from -0.15625 to 0.15625
- conv_bias: float32 [64], replicated, may hold values from -3 to 3
- down_weight: bfloat16 [8, 64, 128], replicated, may hold values from -0.25 to 0.25
- down_bias: float32 [128], replicated, may hold values from -3 to 3
- coarse_owner: int32 [64, 4, 8], P(None, 'grp'), may hold values from 0 to 127, as said below
Outputs:
- coarse_out: bfloat16 [128, 4, 4, 128, 512], P('blk', 'grp')
Inputs may be any that keep to these rules, and one draw needn't show every extreme that they name: shell_lo is below shell_hi in every voxel column. shell_hi is above shell_lo in every voxel column. `coarse_owner`: for each coarse column X and each index g of grp, the 8 coarse blocks have the owners (2 * X + k) mod the size of blk, for every whole k from -(3) up to 4, each k once.
All inputs are finite; a program needn't handle non-finite values.
Results may differ from a plain program's by a relative error of at most 0.0043.
Values may be sent and summed in bfloat16 or wider, within the bound.
No kernel may reach another device: no remote copies, remote signals or barrier semaphores. Data moves between devices by JAX's collectives and lax.ppermute only.
A program may use at most 64 MiB of HBM per device.

v0:
```python
import jax
import jax.numpy as jnp
from jax import lax
from jax.sharding import PartitionSpec as P


def with_halo(block, sides, width):
    for axis, dim in sides:
        count = lax.axis_size(axis)
        forward = [(i, i + 1) for i in range(count - 1)]
        backward = [(target, source) for source, target in forward]
        low = lax.ppermute(
            lax.slice_in_dim(block, block.shape[dim] - width, None, axis=dim), axis, forward
        )
        high = lax.ppermute(lax.slice_in_dim(block, 0, width, axis=dim), axis, backward)
        block = jnp.concatenate([low, block, high], axis=dim)
    return block


def shifted(value, axis, steps):
    count = lax.axis_size(axis)
    pairs = [(source, (source + steps) % count) for source in range(count)]
    return lax.ppermute(value, axis, pairs)


def select_piece(pieces, owners, target):
    chosen = owners == target
    level = jnp.sum(jnp.where(chosen, lax.iota(jnp.int32, owners.shape[0]), 0))
    present = jnp.any(chosen).astype(pieces.dtype)
    return lax.dynamic_index_in_dim(pieces, level, 0, keepdims=False) * present


def local(voxels, shell_lo, shell_hi, conv_weight, conv_bias, down_weight, down_bias, coarse_owner):
    rows_x, rows_y, channels, rows_z = voxels.shape
    heights = lax.broadcasted_iota(jnp.int32, (rows_x, rows_y, rows_z), 2)
    inside = (heights >= shell_lo[:, :, None]) & (heights < shell_hi[:, :, None])
    masked = voxels * inside.astype(jnp.bfloat16)[:, :, None, :]
    padded = with_halo(masked, (("blk", 0), ("grp", 1)), 1)
    padded = jnp.pad(padded, ((0, 0), (0, 0), (0, 0), (1, 1)))
    summed = lax.conv_general_dilated(
        padded[None],
        conv_weight,
        (1, 1, 1),
        "VALID",
        dimension_numbers=("NXYCZ", "XYZIO", "NXYCZ"),
        preferred_element_type=jnp.float32,
    )[0]
    occupied = inside.astype(jnp.float32)
    hidden = (
        jax.nn.silu(summed + conv_bias[None, None, :, None]) * occupied[:, :, None, :]
    ).astype(jnp.bfloat16)
    half_x, half_y, half_z = (rows_x // 2, rows_y // 2, rows_z // 2)
    cout = down_weight.shape[2]
    children = hidden.reshape(half_x, 2, half_y, 2, channels, half_z, 2)
    weights = down_weight.reshape(2, 2, 2, channels, cout)
    coarse = jnp.einsum(
        "aibjcdk,ijkco->abod", children, weights, preferred_element_type=jnp.float32
    )
    coarse_mask = jnp.max(occupied.reshape(half_x, 2, half_y, 2, half_z, 2), axis=(1, 3, 5))
    coarse = ((coarse + down_bias[None, None, :, None]) * coarse_mask[:, :, None, :]).astype(
        jnp.bfloat16
    )
    levels_z = rows_z // (2 * rows_x)
    cells = half_x * half_y * rows_x
    pieces = (
        coarse.reshape(half_x, half_y, cout, levels_z, rows_x)
        .transpose(3, 2, 0, 1, 4)
        .reshape(levels_z, cout, cells)
    )
    position = lax.axis_index("blk")
    peer_count = lax.axis_size("blk")
    owners = lax.dynamic_index_in_dim(coarse_owner[:, 0, :], position // 2, 0, keepdims=False)
    slot_count = levels_z // 2
    first_col = (position - slot_count + 1) // 2
    slot_cols = first_col + lax.iota(jnp.int32, slot_count)
    received = []
    for offset in range(-slot_count, slot_count + 1):
        one_piece = select_piece(pieces, owners, (position + offset) % peer_count)
        if offset == 0:
            arrived = one_piece
        else:
            arrived = shifted(one_piece, "blk", offset)
        received.append(arrived)
    received = jnp.stack(received, axis=0)
    steps_back = position - 2 * slot_cols
    sources = jnp.stack([steps_back + slot_count, steps_back - 1 + slot_count], axis=1)
    picked = jnp.take(received, sources.reshape(-1), axis=0)
    blocks = (
        picked.reshape(slot_count, 2, cout, cells)
        .transpose(0, 2, 1, 3)
        .reshape(slot_count, cout, 2 * cells)
    )
    return blocks[None, None]


def solution(mesh):
    placed = (
        P("blk", "grp", None, None),
        P("blk", "grp"),
        P("blk", "grp"),
        P(),
        P(),
        P(),
        P(),
        P(None, "grp", None),
    )
    return jax.shard_map(
        local,
        mesh=mesh,
        in_specs=placed,
        out_specs=P("blk", "grp", None, None, None),
        check_vma=False,
    )
```

profile of v0, /device:TPU:1, one launch (start us, length us, event | category | flops | bytes accessed | tf_op | source)
XLA Modules:
  0.0 190.3 jit_solution(264442949779808840)
XLA Ops:
  0.0 0.9 fusion.24
  0.9 1.8 broadcast_multiply_fusion
  2.6 0.7 fusion.41
  3.4 8.7 %collective-permute-start.1 = (bf16[1,16,64,128]{3,2,1,0:T(8,128)(2,1)}, bf16[1,16,64,128]{3,2,1,0:T(8,128)(2,1)S(1)}, u32[]{:S(2)}, u32[]{:S(2)}) collective-permute-start(bf16[1,16,64,128]{3,2,1,0:T(8,128)(2,1)} %get-tuple-element.30), channel_id=1, source_target_pairs={{4,0},{8,4},{12,8},{16,12},{20,16},{24,20},{28,24},{32,28},{36,32}... | collective-permute-start | bytes 786440 | tf_op jit(solution)/shard_map/ppermute | solution.py:15
  12.1 1.9 %collective-permute-start = (bf16[1,16,64,128]{3,2,1,0:T(8,128)(2,1)S(1)}, bf16[1,16,64,128]{3,2,1,0:T(8,128)(2,1)S(1)}, u32[]{:S(2)}, u32[]{:S(2)}) collective-permute-start(bf16[1,16,64,128]{3,2,1,0:T(8,128)(2,1)S(1)} %get-tuple-element.29), channel_id=1, source_target_pairs={{0,4},{4,8},{8,12},{12,16},{16,20},{20,24},{24,28},{28,32},{32,36}... | collective-permute-start | bytes 786440 | tf_op jit(solution)/shard_map/ppermute | solution.py:12
  14.2 1.3 broadcast_compare_fusion
  15.5 0.6 fusion.31
  16.2 0.7 fusion.32
  16.8 0.7 fusion.33
  17.6 0.7 fusion.34
  18.2 0.7 fusion.36
  18.9 0.7 fusion.37
  19.6 0.7 fusion.38
  20.3 0.7 fusion.39
  21.1 0.7 compare_and_fusion
  21.7 0.1 reshape.136
  21.8 0.6 fusion.27
  22.4 0.7 select_reduce_fusion
  23.1 0.7 select_reduce_fusion.2
  23.8 0.7 select_reduce_fusion.5
  24.4 0.8 lt.111
  25.2 0.8 ge.33
  25.9 1.6 fusion.40
  27.5 0.0 collective-permute-done.1
  27.5 0.0 collective-permute-done
  27.6 1.3 collective-permute-start.3
  28.9 4.6 %collective-permute-start.2 = (bf16[10,1,64,128]{3,2,1,0:T(8,128)(2,1)S(1)}, bf16[10,1,64,128]{3,2,1,0:T(8,128)(2,1)}, u32[]{:S(2)}, u32[]{:S(2)}) collective-permute-start(bf16[10,1,64,128]{3,2,1,0:T(8,128)(2,1)S(1)} %get-tuple-element.27), channel_id=1, source_target_pairs={{0,1},{1,2},{2,3},{4,5},{5,6},{6,7},{8,9},{9,10},{10,11},{12,13},{... | collective-permute-start | bytes 491528 | tf_op jit(solution)/shard_map/ppermute | solution.py:12
  33.5 1.4 select_reduce_fusion.7
  49.9 1.3 fusion.35
  51.2 7.5 %fusion.9 = bf16[10,18,64,1,130]{4,2,1,0,3:T(8,128)(2,1)} fusion(bf16[10,1,64,128]{3,2,1,0:T(8,128)(2,1)S(1)} %collective-permute-done.3, bf16[10,1,64,128]{3,2,1,0:T(8,128)(2,1)} %collective-permute-done.2, bf16[1,16,64,128]{3,2,1,0:T(8,128)(2,1)S(1)} %collective-permute-done.1, bf16[8,16,64,128]{3,2,1,0:T(8,128)(2,1)S(1)} %broadcast_multiply_fusion, ...), kind=kLoop, calls=%fused_computation.14 | loop fusion | flops 26956800 | bytes 5944320 | tf_op jit(solution)/shard_map/broadcast_in_dim | solution.py:41
  58.7 9.4 %copy.46 = bf16[10,18,64,1,130]{2,4,1,0,3:T(8,128)(2,1)} copy(bf16[10,18,64,1,130]{4,2,1,0,3:T(8,128)(2,1)} %fusion.9) | data formatting | bytes 5990400
  68.1 6.7 %pad.5.clone = bf16[10,18,64,1,136]{2,4,1,0,3:T(8,128)(2,1)} pad(bf16[10,18,64,1,130]{2,4,1,0,3:T(8,128)(2,1)} %copy.46, bf16[]{:T(256)} %constant.136.clone.1), padding=0_0x0_0x0_0x0_0x0_6 | pad | bytes 6128642 | tf_op jit(solution)/shard_map/broadcast_in_dim | solution.py:41
  74.8 11.8 %reshape.139 = bf16[10,18,64,1,8,17]{2,5,4,1,0,3:T(8,128)(2,1)} reshape(bf16[10,18,64,1,136]{2,4,1,0,3:T(8,128)(2,1)} %pad.5.clone) | data formatting | bytes 6266880 | tf_op jit(solution)/shard_map/conv_general_dilated | solution.py:40
  86.6 5.0 %copy.31 = bf16[10,18,64,1,8,17]{2,4,5,1,0,3:T(8,128)(2,1)S(1)} copy(bf16[10,18,64,1,8,17]{2,5,4,1,0,3:T(8,128)(2,1)} %reshape.139) | data formatting | bytes 6266880 | tf_op jit(solution)/shard_map/conv_general_dilated | solution.py:40
  91.7 2.6 %copy-done.2 = bf16[10,18,64,1,8,17]{2,4,5,1,0,3:T(8,128)(2,1)} copy-done((bf16[10,18,64,1,8,17]{2,4,5,1,0,3:T(8,128)(2,1)}, bf16[10,18,64,1,8,17]{2,4,5,1,0,3:T(8,128)(2,1)S(1)}, u32[]{:S(2)}) %copy-start.2) | copy-done | bytes 3133464
  94.3 0.2 slice.22
  94.5 19.8 %broadcast_select_fusion = f32[8,16,8,17,64]{4,2,3,1,0:T(8,128)S(1)} fusion(pred[8,17]{0,1:T(8,128)(4,1)S(1)} %copy-done.11, bf16[3,3,3,64,64]{4,3,2,1,0:T(8,128)(2,1)S(1)} %copy-done, bf16[10,18,64,1,7,2]{2,4,5,1,0,3:T(8,128)(2,1)S(1)} %slice.22, bf16[10,18,64,1,8,17]{2,4,5,1,0,3:T(8,128)(2,1)} %copy-done.2), kind=kOutput, calls=%fused_computation.21 | convolution fusion | flops 3861991424 | bytes 8133768 | tf_op jit(solution)/shard_map/conv_general_dilated | solution.py:40
  114.3 1.6 copy.32
  115.9 4.0 %slice.23 = f32[8,16,1,128,64]{4,1,3,0,2:T(8,128)} slice(f32[8,16,1,136,64]{4,1,3,0,2:T(8,128)S(1)} %bitcast.75), slice={[0:8], [0:16], [0:1], [0:128], [0:64]} | slice | bytes 8388608 | tf_op jit(solution)/shard_map/conv_general_dilated | solution.py:40
  120.0 13.5 %copy.34 = f32[4,2,8,2,64,64,2]{5,4,6,3,2,1,0:T(8,128)} copy(f32[4,2,8,2,64,64,2]{4,3,2,6,5,1,0:T(2,128)} %bitcast.76) | data formatting | bytes 8388608 | tf_op jit(solution)/shard_map/squeeze | solution.py:40
  133.5 0.0 copy-start.6
  133.6 0.0 copy-start.1
  133.6 5.3 %fusion.15 = f32[4,8,64,128,1,1,1]{3,2,6,5,0,1,4:T(8,128)S(1)} fusion(bf16[2,2,2,64,128,1,1]{4,3,2,1,5,6,0:T(8,128)(2,1)S(1)} %bitcast.81, f32[4,2,8,2,64,64,2]{5,4,6,3,2,1,0:T(8,128)} %copy.34, f32[4,2,8,2,64,2]{4,5,3,2,1,0:T(2,128)S(1)} %copy-done.3, f32[64]{0:T(128)S(1)} %copy-done.10), kind=kOutput, calls=%fused_computation.22 | convolution fusion | flops 275775488 | bytes 5439744 | tf_op jit(solution)/shard_map/aibjcdk,ijkco->abod/dot_general | solution.py:56
  138.9 0.3 fusion.22
  139.3 0.1 copy.36
  139.5 9.5 %collective-permute-start.4 = (bf16[128,256]{0,1:T(8,128)(2,1)S(1)}, bf16[128,256]{0,1:T(8,128)(2,1)S(1)}, u32[]{:S(2)}, u32[]{:S(2)}) collective-permute-start(bf16[128,256]{0,1:T(8,128)(2,1)S(1)} %get-tuple-element.39), channel_id=1, source_target_pairs={{0,496},{4,500},{8,504},{12,508},{16,0},{20,4},{24,8},{28,12},{32,... | collective-permute-start | bytes 196616 | tf_op jit(solution)/shard_map/ppermute | solution.py:23
  149.0 0.7 select_reduce_fusion.4
  157.3 2.8 %collective-permute-start.5 = (bf16[128,256]{0,1:T(8,128)(2,1)S(1)}, bf16[128,256]{0,1:T(8,128)(2,1)S(1)}, u32[]{:S(2)}, u32[]{:S(2)}) collective-permute-start(bf16[128,256]{0,1:T(8,128)(2,1)S(1)} %get-tuple-element.38), channel_id=1, source_target_pairs={{0,500},{4,504},{8,508},{12,0},{16,4},{20,8},{24,12},{28,16},{32,2... | collective-permute-start | bytes 196616 | tf_op jit(solution)/shard_map/ppermute | solution.py:23
  160.2 3.9 %collective-permute-start.6 = (bf16[128,256]{0,1:T(8,128)(2,1)S(1)}, bf16[128,256]{0,1:T(8,128)(2,1)S(1)}, u32[]{:S(2)}, u32[]{:S(2)}) collective-permute-start(bf16[128,256]{0,1:T(8,128)(2,1)S(1)} %get-tuple-element.37), channel_id=1, source_target_pairs={{0,504},{4,508},{8,0},{12,4},{16,8},{20,12},{24,16},{28,20},{32,24... | collective-permute-start | bytes 196616 | tf_op jit(solution)/shard_map/ppermute | solution.py:23
  164.1 5.0 %collective-permute-start.7 = (bf16[128,256]{0,1:T(8,128)(2,1)S(1)}, bf16[128,256]{0,1:T(8,128)(2,1)S(1)}, u32[]{:S(2)}, u32[]{:S(2)}) collective-permute-start(bf16[128,256]{0,1:T(8,128)(2,1)S(1)} %get-tuple-element.36), channel_id=1, source_target_pairs={{0,508},{4,0},{8,4},{12,8},{16,12},{20,16},{24,20},{28,24},{32,28}... | collective-permute-start | bytes 196616 | tf_op jit(solution)/shard_map/ppermute | solution.py:23
  169.2 0.8 collective-permute-done.7
  170.0 0.1 multiply_bitcast_fusion
  170.1 1.9 %collective-permute-start.8 = (bf16[128,256]{0,1:T(8,128)(2,1)S(1)}, bf16[128,256]{0,1:T(8,128)(2,1)S(1)}, u32[]{:S(2)}, u32[]{:S(2)}) collective-permute-start(bf16[128,256]{0,1:T(8,128)(2,1)S(1)} %get-tuple-element.34), channel_id=1, source_target_pairs={{0,4},{4,8},{8,12},{12,16},{16,20},{20,24},{24,28},{28,32},{32,36}... | collective-permute-start | bytes 196616 | tf_op jit(solution)/shard_map/ppermute | solution.py:23
  172.0 1.9 %collective-permute-start.9 = (bf16[128,256]{0,1:T(8,128)(2,1)S(1)}, bf16[128,256]{0,1:T(8,128)(2,1)S(1)}, u32[]{:S(2)}, u32[]{:S(2)}) collective-permute-start(bf16[128,256]{0,1:T(8,128)(2,1)S(1)} %get-tuple-element.33), channel_id=1, source_target_pairs={{0,8},{4,12},{8,16},{12,20},{16,24},{20,28},{24,32},{28,36},{32,40... | collective-permute-start | bytes 196616 | tf_op jit(solution)/shard_map/ppermute | solution.py:23
  174.0 5.3 %collective-permute-start.10 = (bf16[128,256]{0,1:T(8,128)(2,1)S(1)}, bf16[128,256]{0,1:T(8,128)(2,1)S(1)}, u32[]{:S(2)}, u32[]{:S(2)}) collective-permute-start(bf16[128,256]{0,1:T(8,128)(2,1)S(1)} %get-tuple-element.32), channel_id=1, source_target_pairs={{0,12},{4,16},{8,20},{12,24},{16,28},{20,32},{24,36},{28,40},{32,4... | collective-permute-start | bytes 196616 | tf_op jit(solution)/shard_map/ppermute | solution.py:23
  179.3 1.9 %collective-permute-start.11 = (bf16[128,256]{0,1:T(8,128)(2,1)S(1)}, bf16[128,256]{0,1:T(8,128)(2,1)S(1)}, u32[]{:S(2)}, u32[]{:S(2)}) collective-permute-start(bf16[128,256]{0,1:T(8,128)(2,1)S(1)} %get-tuple-element.31), channel_id=1, source_target_pairs={{0,16},{4,20},{8,24},{12,28},{16,32},{20,36},{24,40},{28,44},{32,4... | collective-permute-start | bytes 196616 | tf_op jit(solution)/shard_map/ppermute | solution.py:23
  181.2 0.4 collective-permute-done.9
  181.7 2.6 %collective-permute-done.10 = bf16[128,256]{0,1:T(8,128)(2,1)S(1)} collective-permute-done((bf16[128,256]{0,1:T(8,128)(2,1)S(1)}, bf16[128,256]{0,1:T(8,128)(2,1)S(1)}, u32[]{:S(2)}, u32[]{:S(2)}) %collective-permute-start.10) | collective-permute-done | bytes 65568 | tf_op jit(solution)/shard_map/ppermute | solution.py:23
  184.3 3.7 %collective-permute-done.11 = bf16[128,256]{0,1:T(8,128)(2,1)S(1)} collective-permute-done((bf16[128,256]{0,1:T(8,128)(2,1)S(1)}, bf16[128,256]{0,1:T(8,128)(2,1)S(1)}, u32[]{:S(2)}, u32[]{:S(2)}) %collective-permute-start.11) | collective-permute-done | bytes 65568 | tf_op jit(solution)/shard_map/ppermute | solution.py:23
  188.0 0.6 gather_fusion
  188.7 0.2 copy.37
  188.9 0.1 select_bitcast_fusion
  189.0 0.3 copy.38
  189.3 1.0 copy.39
  (40 shorter events, 0.2 us)
Async XLA Ops:
  0.0 94.5 %copy-start = (bf16[3,3,3,64,64]{4,3,2,1,0:T(8,128)(2,1)S(1)}, bf16[3,3,3,64,64]{4,3,2,1,0:T(8,128)(2,1)}, u32[]{:S(2)}) copy-start(bf16[3,3,3,64,64]{4,3,2,1,0:T(8,128)(2,1)} %param.11) | copy-start | bytes 663556
  3.4 24.1 %collective-permute-start.1 = (bf16[1,16,64,128]{3,2,1,0:T(8,128)(2,1)}, bf16[1,16,64,128]{3,2,1,0:T(8,128)(2,1)S(1)}, u32[]{:S(2)}, u32[]{:S(2)}) collective-permute-start(bf16[1,16,64,128]{3,2,1,0:T(8,128)(2,1)} %get-tuple-element.30), channel_id=1, source_target_pairs={{4,0},{8,4},{12,8},{16,12},{20,16},{24,20},{28,24},{32,28},{36,32}... | collective-permute-start | bytes 786440 | tf_op jit(solution)/shard_map/ppermute | solution.py:15
  12.1 15.4 %collective-permute-start = (bf16[1,16,64,128]{3,2,1,0:T(8,128)(2,1)S(1)}, bf16[1,16,64,128]{3,2,1,0:T(8,128)(2,1)S(1)}, u32[]{:S(2)}, u32[]{:S(2)}) collective-permute-start(bf16[1,16,64,128]{3,2,1,0:T(8,128)(2,1)S(1)} %get-tuple-element.29), channel_id=1, source_target_pairs={{0,4},{4,8},{8,12},{12,16},{16,20},{20,24},{24,28},{28,32},{32,36}... | collective-permute-start | bytes 786440 | tf_op jit(solution)/shard_map/ppermute | solution.py:12
  27.6 23.7 %collective-permute-start.3 = (bf16[10,1,64,128]{3,2,1,0:T(8,128)(2,1)S(1)}, bf16[10,1,64,128]{3,2,1,0:T(8,128)(2,1)S(1)}, u32[]{:S(2)}, u32[]{:S(2)}) collective-permute-start(bf16[10,1,64,128]{3,2,1,0:T(8,128)(2,1)S(1)} %get-tuple-element.28), channel_id=1, source_target_pairs={{1,0},{2,1},{3,2},{5,4},{6,5},{7,6},{9,8},{10,9},{11,10},{13,12},{... | collective-permute-start | bytes 491528 | tf_op jit(solution)/shard_map/ppermute | solution.py:15
  28.9 22.4 %collective-permute-start.2 = (bf16[10,1,64,128]{3,2,1,0:T(8,128)(2,1)S(1)}, bf16[10,1,64,128]{3,2,1,0:T(8,128)(2,1)}, u32[]{:S(2)}, u32[]{:S(2)}) collective-permute-start(bf16[10,1,64,128]{3,2,1,0:T(8,128)(2,1)S(1)} %get-tuple-element.27), channel_id=1, source_target_pairs={{0,1},{1,2},{2,3},{4,5},{5,6},{6,7},{8,9},{9,10},{10,11},{12,13},{... | collective-permute-start | bytes 491528 | tf_op jit(solution)/shard_map/ppermute | solution.py:12
  86.6 7.9 %copy-start.11 = (pred[8,17]{0,1:T(8,128)(4,1)S(1)}, pred[8,17]{0,1:T(8,128)(4,1)}, u32[]{:S(2)}) copy-start(pred[8,17]{0,1:T(8,128)(4,1)} %constant.156) | copy-start | bytes 412
  91.7 2.6 %copy-start.2 = (bf16[10,18,64,1,8,17]{2,4,5,1,0,3:T(8,128)(2,1)}, bf16[10,18,64,1,8,17]{2,4,5,1,0,3:T(8,128)(2,1)S(1)}, u32[]{:S(2)}) copy-start(bf16[10,18,64,1,8,17]{2,4,5,1,0,3:T(8,128)(2,1)S(1)} %copy.31) | copy-start | bytes 9400324
  120.0 13.5 %copy-start.3 = (f32[4,2,8,2,64,2]{4,5,3,2,1,0:T(2,128)S(1)}, f32[4,2,8,2,64,2]{4,5,3,2,1,0:T(2,128)}, u32[]{:S(2)}) copy-start(f32[4,2,8,2,64,2]{4,5,3,2,1,0:T(2,128)} %get-tuple-element.26) | copy-start | bytes 196612
  120.0 13.5 %copy-start.9 = (bf16[8,64,128]{2,1,0:T(8,128)(2,1)S(1)}, bf16[8,64,128]{2,1,0:T(8,128)(2,1)}, u32[]{:S(2)}) copy-start(bf16[8,64,128]{2,1,0:T(8,128)(2,1)} %param.13) | copy-start | bytes 393220
  120.0 13.5 %copy-start.10 = (f32[64]{0:T(128)S(1)}, f32[64]{0:T(128)}, u32[]{:S(2)}) copy-start(f32[64]{0:T(128)} %param.12) | copy-start | bytes 772
  133.5 5.4 %copy-start.4 = (f32[4,8,64]{2,1,0:T(8,128)S(1)}, f32[4,8,64]{2,1,0:T(8,128)}, u32[]{:S(2)}) copy-start(f32[4,8,64]{2,1,0:T(8,128)} %get-tuple-element.25) | copy-start | bytes 24580
  133.5 5.4 %copy-start.6 = (f32[128]{0:T(128)S(1)}, f32[128]{0:T(128)}, u32[]{:S(2)}) copy-start(f32[128]{0:T(128)} %param.14) | copy-start | bytes 1540
  133.5 15.4 %copy-start.8 = (pred[8]{0:T(512)(128)(4,1)S(1)}, pred[8]{0:T(512)(128)(4,1)}, u32[]{:S(2)}) copy-start(pred[8]{0:T(512)(128)(4,1)} %get-tuple-element.14) | copy-start | bytes 28
  133.5 38.5 %copy-start.7 = (s32[8]{0:T(128)S(1)}, s32[8]{0:T(128)}, u32[]{:S(2)}) copy-start(s32[8]{0:T(128)} %fusion.27) | copy-start | bytes 100
  133.6 56.8 %copy-start.1 = (bf16[3,3,3,64,64]{4,3,2,1,0:T(8,128)(2,1)S(1)}, bf16[3,3,3,64,64]{4,3,2,1,0:T(8,128)(2,1)}, u32[]{:S(2)}) copy-start(bf16[3,3,3,64,64]{4,3,2,1,0:T(8,128)(2,1)} %param.11) | copy-start | bytes 663556
  138.9 50.0 %copy-start.5 = (pred[4,2]{1,0:T(4,128)(4,1)S(1)}, pred[4,2]{1,0:T(4,128)(4,1)}, u32[]{:S(2)}) copy-start(pred[4,2]{1,0:T(4,128)(4,1)} %get-tuple-element.23) | copy-start | bytes 28
  139.5 29.6 %collective-permute-start.4 = (bf16[128,256]{0,1:T(8,128)(2,1)S(1)}, bf16[128,256]{0,1:T(8,128)(2,1)S(1)}, u32[]{:S(2)}, u32[]{:S(2)}) collective-permute-start(bf16[128,256]{0,1:T(8,128)(2,1)S(1)} %get-tuple-element.39), channel_id=1, source_target_pairs={{0,496},{4,500},{8,504},{12,508},{16,0},{20,4},{24,8},{28,12},{32,... | collective-permute-start | bytes 196616 | tf_op jit(solution)/shard_map/ppermute | solution.py:23
  157.3 11.8 %collective-permute-start.5 = (bf16[128,256]{0,1:T(8,128)(2,1)S(1)}, bf16[128,256]{0,1:T(8,128)(2,1)S(1)}, u32[]{:S(2)}, u32[]{:S(2)}) collective-permute-start(bf16[128,256]{0,1:T(8,128)(2,1)S(1)} %get-tuple-element.38), channel_id=1, source_target_pairs={{0,500},{4,504},{8,508},{12,0},{16,4},{20,8},{24,12},{28,16},{32,2... | collective-permute-start | bytes 196616 | tf_op jit(solution)/shard_map/ppermute | solution.py:23
  160.2 9.0 %collective-permute-start.6 = (bf16[128,256]{0,1:T(8,128)(2,1)S(1)}, bf16[128,256]{0,1:T(8,128)(2,1)S(1)}, u32[]{:S(2)}, u32[]{:S(2)}) collective-permute-start(bf16[128,256]{0,1:T(8,128)(2,1)S(1)} %get-tuple-element.37), channel_id=1, source_target_pairs={{0,504},{4,508},{8,0},{12,4},{16,8},{20,12},{24,16},{28,20},{32,24... | collective-permute-start | bytes 196616 | tf_op jit(solution)/shard_map/ppermute | solution.py:23
  164.1 5.9 %collective-permute-start.7 = (bf16[128,256]{0,1:T(8,128)(2,1)S(1)}, bf16[128,256]{0,1:T(8,128)(2,1)S(1)}, u32[]{:S(2)}, u32[]{:S(2)}) collective-permute-start(bf16[128,256]{0,1:T(8,128)(2,1)S(1)} %get-tuple-element.36), channel_id=1, source_target_pairs={{0,508},{4,0},{8,4},{12,8},{16,12},{20,16},{24,20},{28,24},{32,28}... | collective-permute-start | bytes 196616 | tf_op jit(solution)/shard_map/ppermute | solution.py:23
  170.1 11.1 %collective-permute-start.8 = (bf16[128,256]{0,1:T(8,128)(2,1)S(1)}, bf16[128,256]{0,1:T(8,128)(2,1)S(1)}, u32[]{:S(2)}, u32[]{:S(2)}) collective-permute-start(bf16[128,256]{0,1:T(8,128)(2,1)S(1)} %get-tuple-element.34), channel_id=1, source_target_pairs={{0,4},{4,8},{8,12},{12,16},{16,20},{20,24},{24,28},{28,32},{32,36}... | collective-permute-start | bytes 196616 | tf_op jit(solution)/shard_map/ppermute | solution.py:23
  172.0 9.6 %collective-permute-start.9 = (bf16[128,256]{0,1:T(8,128)(2,1)S(1)}, bf16[128,256]{0,1:T(8,128)(2,1)S(1)}, u32[]{:S(2)}, u32[]{:S(2)}) collective-permute-start(bf16[128,256]{0,1:T(8,128)(2,1)S(1)} %get-tuple-element.33), channel_id=1, source_target_pairs={{0,8},{4,12},{8,16},{12,20},{16,24},{20,28},{24,32},{28,36},{32,40... | collective-permute-start | bytes 196616 | tf_op jit(solution)/shard_map/ppermute | solution.py:23
  174.0 10.3 %collective-permute-start.10 = (bf16[128,256]{0,1:T(8,128)(2,1)S(1)}, bf16[128,256]{0,1:T(8,128)(2,1)S(1)}, u32[]{:S(2)}, u32[]{:S(2)}) collective-permute-start(bf16[128,256]{0,1:T(8,128)(2,1)S(1)} %get-tuple-element.32), channel_id=1, source_target_pairs={{0,12},{4,16},{8,20},{12,24},{16,28},{20,32},{24,36},{28,40},{32,4... | collective-permute-start | bytes 196616 | tf_op jit(solution)/shard_map/ppermute | solution.py:23
  179.3 8.8 %collective-permute-start.11 = (bf16[128,256]{0,1:T(8,128)(2,1)S(1)}, bf16[128,256]{0,1:T(8,128)(2,1)S(1)}, u32[]{:S(2)}, u32[]{:S(2)}) collective-permute-start(bf16[128,256]{0,1:T(8,128)(2,1)S(1)} %get-tuple-element.31), channel_id=1, source_target_pairs={{0,16},{4,20},{8,24},{12,28},{16,32},{20,36},{24,40},{28,44},{32,4... | collective-permute-start | bytes 196616 | tf_op jit(solution)/shard_map/ppermute | solution.py:23
where the time goes:
time: 192 us; the launch traced here: 190 us
  local copies, waits for them, and re-layouts  59.7 us (31%)
  starting transfers between devices  48.8 us (25%)
  other arithmetic  25.8 us (13%)
  matrix products  25.1 us (13%)
  between operations  23.2 us (12%)
  waiting for transfers between devices  7.59 us (4%)
    ppermute x8, starting transfers between devices, shifted(): return lax.ppermute(value, axis, pairs)  32.2 us
    conv_general_dilated x5, local copies, waits for them, and re-layouts, local(): lax.conv_general_dilated(padded[None], conv_weight, (1, 1, 1), 'VALID', d...  22.7 us
    conv_general_dilated x1, matrix products, local(): lax.conv_general_dilated(padded[None], conv_weight, (1, 1, 1), 'VALID', d...  19.8 us
    squeeze x1, local copies, waits for them, and re-layouts, local(): lax.conv_general_dilated(padded[None], conv_weight, (1, 1, 1), 'VALID', d...  13.5 us
    unnamed x32, local copies, waits for them, and re-layouts  12.2 us
    ppermute x2, starting transfers between devices, with_halo(): lax.ppermute(lax.slice_in_dim(block, 0, width, axis=dim), axis, backward)  10 us
    ppermute x8, waiting for transfers between devices, shifted(): return lax.ppermute(value, axis, pairs)  7.58 us
    broadcast_in_dim x1, other arithmetic, local(): padded[None]  7.47 us
  transfers between devices with their start and end apart: 12, of which 4 were waited for; matrix products, arithmetic and copies ran while one was open for 9% of the time, Pallas kernels for 0%

commit v1 on v0

v1 whole, which is shorter than its diff:
```python
import jax
import jax.numpy as jnp
from jax import lax
from jax.experimental import pallas as pl
from jax.experimental.pallas import tpu as pltpu
from jax.sharding import PartitionSpec as P

BF = jnp.bfloat16
F32 = jnp.float32
VMEM = pltpu.VMEM
SMEM = pltpu.SMEM


def prep_kernel(cw, cb, dw, db, w_out, d_out, cb_out, db_out, sel_out):
    zero = jnp.zeros((64, 64), F32)
    for dx in range(3):
        for dz in range(3):
            taps = [cw[dx, dy, dz].astype(F32) for dy in range(3)]
            for yo in range(2):
                line = ([zero] if yo else []) + taps + ([] if yo else [zero])
                for half in range(2):
                    pair = jnp.concatenate(line[2 * half : 2 * half + 2], axis=0)
                    row = (dz * 2 + yo) * 64
                    col = (dx * 4 + half * 2) * 64
                    w_out[row : row + 64, col : col + 128] = pair.T.astype(BF)
    for k in range(2):
        for i in range(2):
            pair = jnp.concatenate([dw[4 * i + k], dw[4 * i + 2 + k]], axis=0).astype(F32)
            d_out[k * 128 : k * 128 + 128, i * 128 : i * 128 + 128] = pair.T.astype(BF)
    cb_out[...] = jnp.broadcast_to(cb[...], (128, 128)).T
    db_out[...] = jnp.broadcast_to(db[...], (128, 128)).T
    for q in range(8):
        z = lax.broadcasted_iota(jnp.int32, (128, 512), 0)
        lane = lax.broadcasted_iota(jnp.int32, (128, 512), 1)
        want = jnp.where(((lane >> 3) & 7) == q, 16 * (lane >> 6) + 2 * (lane & 7), -1)
        sel_out[q * 128 : q * 128 + 128, :] = jnp.where(z == want, 1.0, 0.0).astype(BF)


def prep(conv_weight, conv_bias, down_weight, down_bias):
    return pl.pallas_call(
        prep_kernel,
        out_shape=(
            jax.ShapeDtypeStruct((384, 768), BF),
            jax.ShapeDtypeStruct((256, 256), BF),
            jax.ShapeDtypeStruct((128, 128), F32),
            jax.ShapeDtypeStruct((128, 128), F32),
            jax.ShapeDtypeStruct((1024, 512), BF),
        ),
        name="prep",
    )(
        conv_weight,
        jnp.tile(conv_bias, 2)[None],
        down_weight,
        down_bias[None],
    )


def main_kernel(
    lo, hi, slots, vox, ylo, yhi, xlo, xhi, w, d, cb, db, sel, keep, give, pad, cells, pieces
):
    lane8 = lax.broadcasted_iota(jnp.int32, (8, 128), 1)

    def occupied(x, y):
        return jnp.where((lane8 >= lo[x, y]) & (lane8 < hi[x, y]), 1.0, 0.0)

    pad[0] = xlo[...]
    pad[9] = xhi[...]
    for x in range(8):
        pad[x + 1, 0] = ylo[x]
        pad[x + 1, 17] = yhi[x]

    @pl.loop(0, 8)
    def _(x):
        for y in range(16):
            mask = jnp.concatenate([occupied(x, y)] * 2, axis=0).astype(BF)
            pad[x + 1, y + 1] = (vox[x, y].reshape(4, 16, 128) * mask[None]).reshape(64, 128)

    lane = lax.broadcasted_iota(jnp.int32, (128, 128), 1)

    def conv_cell(p, yp):
        rows = [pad[2 * p + r, pl.ds(2 * yp, 4)].reshape(256, 128) for r in range(4)]
        window = jnp.concatenate(
            [jnp.concatenate([rows[t], rows[t + 1]], axis=1) for t in range(3)], axis=0
        )
        summed = jnp.dot(w[...], window, preferred_element_type=F32)
        parts = []
        for xi in range(2):
            part = summed[:, xi * 128 : xi * 128 + 128]
            below = jnp.where(lane == 0, 0.0, pltpu.roll(part[0:128], 1, 1))
            above = jnp.where(lane == 127, 0.0, pltpu.roll(part[256:384], 127, 1))
            half = (below + above + part[128:256] + cb[...]) * 0.5
            act = half + half * jnp.tanh(half)
            masks = [occupied(2 * p + xi, 2 * yp + yo) for yo in range(2)]
            mask = jnp.stack(masks)[:, None]
            act = act.reshape(2, 8, 8, 128) * mask
            parts.append(act.reshape(128, 128).astype(BF))
        return jnp.concatenate(parts, axis=0)

    def coarse_mask(p, yp):
        found = None
        for xi in range(2):
            for yo in range(2):
                x, y = 2 * p + xi, 2 * yp + yo
                here = (lane8 + 1 >= lo[x, y]) & (lane8 < hi[x, y])
                found = here if found is None else found | here
        return jnp.where(found, 1.0, 0.0)

    @pl.loop(0, 4)
    def _(p):
        for ypp in range(4):
            hidden = jnp.concatenate([conv_cell(p, 2 * ypp), conv_cell(p, 2 * ypp + 1)], axis=1)
            down = jnp.dot(d[...], hidden, preferred_element_type=F32)
            for e in range(2):
                part = down[:, e * 128 : e * 128 + 128]
                total = part[0:128] + pltpu.roll(part[128:256], 127, 1) + db[...]
                total = total.reshape(16, 8, 128) * coarse_mask(p, 2 * ypp + e)[None]
                q = 2 * ypp + e
                cells[pl.ds(p * 128, 128), q * 128 : q * 128 + 128] = total.reshape(
                    128, 128
                ).astype(BF)

    for pair in range(2):
        picked = jnp.dot(
            cells[pair * 256 : pair * 256 + 256], sel[...], preferred_element_type=F32
        )
        for level in range(8):
            at = slice(level * 64, level * 64 + 64)
            both = jnp.concatenate([picked[0:128, at], picked[128:256, at]], axis=1)
            pieces[slots[level], :, pair * 128 : pair * 128 + 128] = both.astype(BF)
    keep[...] = pieces[0:4]
    give[...] = pieces[4:8]


def main(lo, hi, slots, vox, ylo, yhi, xlo, xhi, tables):
    half = jax.ShapeDtypeStruct((4, 128, 256), BF)
    smem = pl.BlockSpec(memory_space=SMEM)
    vmem = pl.BlockSpec(memory_space=VMEM)
    return pl.pallas_call(
        main_kernel,
        out_shape=(half, half),
        in_specs=[smem] * 3 + [vmem] * 10,
        out_specs=(vmem, vmem),
        scratch_shapes=[
            VMEM((10, 18, 64, 128), BF),
            VMEM((512, 1024), BF),
            VMEM((8, 128, 256), BF),
        ],
        compiler_params=pltpu.CompilerParams(vmem_limit_bytes=48 * 1024 * 1024),
        name="scene",
    )(lo, hi, slots, vox, ylo, yhi, xlo, xhi, *tables)


def ring(count, step):
    return [(i, step(i) % count) for i in range(count)]


def local(voxels, shell_lo, shell_hi, conv_weight, conv_bias, down_weight, down_bias, coarse_owner):
    blk_n = lax.axis_size("blk")
    grp_n = lax.axis_size("grp")
    me = lax.axis_index("blk")
    core = me % 2

    def masked(block, lo, hi):
        heights = lax.broadcasted_iota(jnp.int32, block.shape[:1] + block.shape[2:], 1)
        inside = (heights >= lo[:, None]) & (heights < hi[:, None])
        return block * inside.astype(BF)[:, None, :]

    up = [(i, i + 1) for i in range(grp_n - 1)]
    down = [(b, a) for a, b in up]
    ylo = lax.ppermute(masked(voxels[:, 15], shell_lo[:, 15], shell_hi[:, 15]), "grp", up)
    yhi = lax.ppermute(masked(voxels[:, 0], shell_lo[:, 0], shell_hi[:, 0]), "grp", down)
    tables = prep(conv_weight, conv_bias, down_weight, down_bias)

    def x_face(x):
        face = masked(voxels[x], shell_lo[x], shell_hi[x])
        return jnp.concatenate([ylo[x : x + 1], face, yhi[x : x + 1]], axis=0)

    ahead = [(i, i + 1) for i in range(blk_n - 1)]
    behind = [(b, a) for a, b in ahead]
    xlo = lax.ppermute(x_face(7), "blk", ahead)
    xhi = lax.ppermute(x_face(0), "blk", behind)

    column = me // 2
    owners = lax.dynamic_index_in_dim(coarse_owner[:, 0, :], column, 0, keepdims=False)
    offset = (owners - 2 * column + 3) % blk_n
    slots = (offset + 4 * core) % 8

    keep, give = main(shell_lo, shell_hi, slots, voxels, ylo, yhi, xlo, xhi, tables)
    got = lax.ppermute(give, "blk", ring(blk_n, lambda i: i ^ 1))
    even = core == 0
    whole = jnp.where(
        even, jnp.concatenate([keep, got], axis=2), jnp.concatenate([got, keep], axis=2)
    )
    def mine(a, b):
        return jnp.where(even, whole[a], whole[b])

    one = lax.ppermute(mine(2, 1), "blk", ring(blk_n, lambda i: i + 1 if i % 2 else i - 1))
    two = lax.ppermute(mine(1, 2), "blk", ring(blk_n, lambda i: i + 2 if i % 2 else i - 2))
    three = lax.ppermute(mine(0, 3), "blk", ring(blk_n, lambda i: i + 3 if i % 2 else i - 3))
    stay = mine(3, 0)
    result = jnp.stack(
        [
            jnp.where(even, three, two),
            jnp.where(even, one, stay),
            jnp.where(even, stay, one),
            jnp.where(even, two, three),
        ]
    )
    return result[None, None]


def solution(mesh):
    placed = (
        P("blk", "grp", None, None),
        P("blk", "grp"),
        P("blk", "grp"),
        P(),
        P(),
        P(),
        P(),
        P(None, "grp", None),
    )
    return jax.shard_map(
        local,
        mesh=mesh,
        in_specs=placed,
        out_specs=P("blk", "grp", None, None, None),
        check_vma=False,
    )
```

time: 192 us -> 73.7 us (0.38)
  the two profiles are of different devices: /device:TPU:1 before, /device:TPU:6 now
where the time goes in v1:
time: 73.7 us; the launch traced here: 73.1 us
  starting transfers between devices  31.7 us (43%)
  Pallas kernels  15.4 us (21%)
  waiting for transfers between devices  12.4 us (17%)
  local copies, waits for them, and re-layouts  9.13 us (12%)
  other arithmetic  4.31 us (6%)
    pallas_call x1, Pallas kernels, main(): pl.pallas_call(main_kernel, out_shape=(half, half), in_specs=[smem] * 3 +...  12.6 us
    ppermute x1, starting transfers between devices, local(): lax.ppermute(mine(2, 1), 'blk', ring(blk_n, lambda i: i + 1 if i % 2 else...  12.2 us
    ppermute x1, waiting for transfers between devices, local(): lax.ppermute(mine(0, 3), 'blk', ring(blk_n, lambda i: i + 3 if i % 2 else...  7.01 us
    ppermute x1, starting transfers between devices, local(): got = lax.ppermute(give, 'blk', ring(blk_n, lambda i: i ^ 1))  6.97 us
    unnamed x20, local copies, waits for them, and re-layouts  4.88 us
    ppermute x1, starting transfers between devices, local(): lax.ppermute(mine(1, 2), 'blk', ring(blk_n, lambda i: i + 2 if i % 2 else...  3.97 us
    ppermute x1, waiting for transfers between devices, local(): lax.ppermute(masked(voxels[:, 15], shell_lo[:, 15], shell_hi[:, 15]), 'gr...  2.85 us
    pallas_call x1, Pallas kernels, prep(): pl.pallas_call(prep_kernel, out_shape=(jax.ShapeDtypeStruct((384, 768), B...  2.79 us
  transfers between devices with their start and end apart: 8, of which 5 were waited for; matrix products, arithmetic and copies ran while one was open for 6% of the time, Pallas kernels for 4%

profile of v1, /device:TPU:6, one launch (start us, length us, event | category | flops | bytes accessed | tf_op | source)
XLA Modules:
  0.0 73.1 jit_solution(3781989656267184526)
XLA Ops:
  0.0 0.0 copy-start.6
  0.0 0.0 copy-start.7
  0.0 0.0 copy-start
  0.0 0.0 copy-start.9
  0.0 0.0 copy-start.8
  0.0 1.1 %slice_reduce_fusion.1 = (s32[8]{0:T(128)S(1)}, s32[8]{0:T(128)S(1)}) fusion(s32[8,16]{1,0:T(8,128)} %lo.1), kind=kLoop, calls=%fused_computation.28 | loop fusion | bytes 128 | tf_op jit(solution)/shard_map/slice | solution.py:171
  1.1 1.0 %slice_reduce_fusion = (s32[8]{0:T(128)S(1)}, s32[8]{0:T(128)S(1)}) fusion(s32[8,16]{1,0:T(8,128)} %hi.1), kind=kLoop, calls=%fused_computation.26 | loop fusion | bytes 128 | tf_op jit(solution)/shard_map/slice | solution.py:171
  2.1 0.1 fusion.7
  2.2 1.0 %bitcast_multiply_fusion.2 = (bf16[8,64,128]{2,1,0:T(8,128)(2,1)S(1)}, bf16[8,64,128]{2,1,0:T(8,128)(2,1)S(1)}) fusion(bf16[8,16,64,128]{3,2,1,0:T(8,128)(2,1)} %vox.1, bf16[8,128]{1,0:T(8,128)(2,1)S(1)} %get-tuple-element.43, bf16[8,128]{1,0:T(8,128)(2,1)S(1)} %get-tuple-element.42), kind=kLoop, calls=%fused_computation.6 | loop fusion | flops 131072 | bytes 528384 | tf_op jit(solution)/shard_map/mul | solution.py:166
  3.2 2.7 %collective-permute-start.1 = (bf16[8,64,128]{2,1,0:T(8,128)(2,1)S(1)}, bf16[8,64,128]{2,1,0:T(8,128)(2,1)S(1)}, u32[]{:S(2)}, u32[]{:S(2)}) collective-permute-start(bf16[8,64,128]{2,1,0:T(8,128)(2,1)S(1)} %get-tuple-element.25), channel_id=1, source_target_pairs={{1,0},{2,1},{3,2},{5,4},{6,5},{7,6},{9,8},{10,9},{11,10},{13,12},{... | collective-permute-start | bytes 393224 | tf_op jit(solution)/shard_map/ppermute | solution.py:171
  5.9 1.3 %collective-permute-start = (bf16[8,64,128]{2,1,0:T(8,128)(2,1)S(1)}, bf16[8,64,128]{2,1,0:T(8,128)(2,1)S(1)}, u32[]{:S(2)}, u32[]{:S(2)}) collective-permute-start(bf16[8,64,128]{2,1,0:T(8,128)(2,1)S(1)} %get-tuple-element.26), channel_id=1, source_target_pairs={{0,1},{1,2},{2,3},{4,5},{5,6},{6,7},{8,9},{9,10},{10,11},{12,13},{... | collective-permute-start | bytes 393224 | tf_op jit(solution)/shard_map/ppermute | solution.py:170
  7.2 0.8 %slice_bitcast_fusion.1 = (s32[16]{0:T(128)S(1)}, s32[16]{0:T(128)S(1)}) fusion(s32[8,16]{1,0:T(8,128)} %lo.1), kind=kLoop, calls=%fused_computation.49 | loop fusion | bytes 256 | tf_op jit(solution)/shard_map/ge | solution.py:165
  8.0 0.8 %slice_bitcast_fusion = (s32[16]{0:T(128)S(1)}, s32[16]{0:T(128)S(1)}) fusion(s32[8,16]{1,0:T(8,128)} %hi.1), kind=kLoop, calls=%fused_computation.48 | loop fusion | bytes 256 | tf_op jit(solution)/shard_map/lt | solution.py:165
  8.7 0.1 fusion.3
  8.8 1.1 %bitcast_multiply_fusion = (bf16[16,64,128]{2,1,0:T(8,128)(2,1)S(1)}, bf16[16,64,128]{2,1,0:T(8,128)(2,1)S(1)}) fusion(bf16[8,16,64,128]{3,2,1,0:T(8,128)(2,1)} %vox.1, bf16[16,128]{1,0:T(8,128)(2,1)S(1)} %get-tuple-element.45, bf16[16,128]{1,0:T(8,128)(2,1)S(1)} %get-tuple-element.44), kind=kLoop, calls=%fused_computation.4 | loop fusion | flops 262144 | bytes 1056768 | tf_op jit(solution)/shard_map/mul | solution.py:166
  9.9 0.0 collective-permute-done.1.yhi
  9.9 2.9 %collective-permute-done.ylo = bf16[8,64,128]{2,1,0:T(8,128)(2,1)S(1)} collective-permute-done((bf16[8,64,128]{2,1,0:T(8,128)(2,1)S(1)}, bf16[8,64,128]{2,1,0:T(8,128)(2,1)S(1)}, u32[]{:S(2)}, u32[]{:S(2)}) %collective-permute-start) | collective-permute-done | bytes 131104 | tf_op jit(solution)/shard_map/ppermute | solution.py:170
  12.8 1.3 %collective-permute-start.2 = (bf16[18,64,128]{2,1,0:T(8,128)(2,1)S(1)}, bf16[18,64,128]{2,1,0:T(8,128)(2,1)S(1)}, u32[]{:S(2)}, u32[]{:S(2)}) collective-permute-start(bf16[18,64,128]{2,1,0:T(8,128)(2,1)S(1)} %pad_maximum_fusion), channel_id=1, source_target_pairs={{0,4},{4,8},{8,12},{12,16},{16,20},{20,24},{24,28},{28,32},{32,36}... | collective-permute-start | bytes 884744 | tf_op jit(solution)/shard_map/ppermute | solution.py:180
  14.1 0.8 %pad_maximum_fusion.1 = bf16[18,64,128]{2,1,0:T(8,128)(2,1)} fusion(bf16[1,64,128]{2,1,0:T(8,128)(2,1)S(1)} %get-tuple-element.36, bf16[16,64,128]{2,1,0:T(8,128)(2,1)S(1)} %get-tuple-element.23, bf16[1,64,128]{2,1,0:T(8,128)(2,1)S(1)} %get-tuple-element.34), kind=kLoop, calls=%fused_computation.3 | loop fusion | flops 294912 | bytes 589824 | tf_op jit(solution)/shard_map/concatenate | solution.py:176
  14.9 1.3 %collective-permute-start.3 = (bf16[18,64,128]{2,1,0:T(8,128)(2,1)}, bf16[18,64,128]{2,1,0:T(8,128)(2,1)S(1)}, u32[]{:S(2)}, u32[]{:S(2)}) collective-permute-start(bf16[18,64,128]{2,1,0:T(8,128)(2,1)} %pad_maximum_fusion.1), channel_id=1, source_target_pairs={{4,0},{8,4},{12,8},{16,12},{20,16},{24,20},{28,24},{32,28},{36,32}... | collective-permute-start | bytes 884744 | tf_op jit(solution)/shard_map/ppermute | solution.py:181
  16.2 0.0 copy-done.9
  16.2 0.7 broadcast_in_dim_tile.3.cb
  16.9 2.8 %prep.1 = (bf16[384,768]{1,0:T(8,128)(2,1)}, bf16[256,256]{1,0:T(8,128)(2,1)}, f32[128,128]{1,0:T(8,128)}, f32[128,128]{1,0:T(8,128)}, bf16[1024,512]{1,0:T(8,128)(2,1)}) custom-call(bf16[3,3,3,64,64]{4,3,2,1,0:T(8,128)(2,1)} %cw.1, f32[1,128]{1,0:T(1,128)} %broadcast_in_dim_tile.3.cb, bf16[8,64,128]{2,1,0:T(8,128)(2,1)} %dw.1, f32[1,128]{1,0:T(1,128)} %bitcast.44), custom_call_target="tpu_custom_call" | custom-call | tf_op jit(solution)/shard_map/prep/pallas_call | solution.py:40
  19.7 0.0 copy-done.8
  19.7 0.2 add_reduce_fusion
  19.9 0.0 collective-permute-done.2.xlo
  19.9 0.5 collective-permute-done.3.xhi
  20.4 0.0 copy-done.6
  20.4 0.0 copy-done.7
  20.4 0.0 copy-done
  20.4 0.0 copy-start.1
  20.4 1.2 %copy-done.1 = bf16[1024,512]{1,0:T(8,128)(2,1)S(1)} copy-done((bf16[1024,512]{1,0:T(8,128)(2,1)S(1)}, bf16[1024,512]{1,0:T(8,128)(2,1)}, u32[]{:S(2)}) %copy-start.1) | copy-done | bytes 1048600
  21.6 0.0 copy-start.2
  21.6 1.1 %copy-done.2 = bf16[384,768]{1,0:T(8,128)(2,1)S(1)} copy-done((bf16[384,768]{1,0:T(8,128)(2,1)S(1)}, bf16[384,768]{1,0:T(8,128)(2,1)}, u32[]{:S(2)}) %copy-start.2) | copy-done | bytes 589848
  22.7 0.0 copy-start.3
  22.7 0.9 %copy-done.3 = bf16[256,256]{1,0:T(8,128)(2,1)S(1)} copy-done((bf16[256,256]{1,0:T(8,128)(2,1)S(1)}, bf16[256,256]{1,0:T(8,128)(2,1)}, u32[]{:S(2)}) %copy-start.3) | copy-done | bytes 131096
  23.6 0.0 copy-start.4
  23.6 0.8 %copy-done.4 = f32[128,128]{1,0:T(8,128)S(1)} copy-done((f32[128,128]{1,0:T(8,128)S(1)}, f32[128,128]{1,0:T(8,128)}, u32[]{:S(2)}) %copy-start.4) | copy-done | bytes 65560
  24.4 0.0 copy-start.5
  24.4 0.8 %copy-done.5 = f32[128,128]{1,0:T(8,128)S(1)} copy-done((f32[128,128]{1,0:T(8,128)S(1)}, f32[128,128]{1,0:T(8,128)}, u32[]{:S(2)}) %copy-start.5) | copy-done | bytes 65560
  25.2 12.6 %scene.1 = (bf16[4,128,256]{2,1,0:T(8,128)(2,1)S(1)}, bf16[4,128,256]{2,1,0:T(8,128)(2,1)S(1)}) custom-call(s32[8,16]{1,0:T(8,128)S(1)} %copy-done.6, s32[8,16]{1,0:T(8,128)S(1)} %copy-done.7, s32[8]{0:T(128)S(1)} %and_select_fusion.slots, bf16[8,16,64,128]{3,2,1,0:T(8,128)(2,1)S(1)} %copy-done, bf16[8,64,128]{2,1,0:T(8,128)(2,1)S(1)} %collective-permute-done.ylo, ...), custom_call_target="tpu_custom_call" | custom-call | tf_op jit(solution)/shard_map/scene/pallas_call | solution.py:138
  37.8 7.0 %collective-permute-start.4 = (bf16[4,128,256]{2,1,0:T(8,128)(2,1)S(1)}, bf16[4,128,256]{2,1,0:T(8,128)(2,1)S(1)}, u32[]{:S(2)}, u32[]{:S(2)}) collective-permute-start(bf16[4,128,256]{2,1,0:T(8,128)(2,1)S(1)} %get-tuple-element.18), channel_id=1, source_target_pairs={{0,4},{4,0},{8,12},{12,8},{16,20},{20,16},{24,28},{28,24},{32,36},... | collective-permute-start | bytes 786440 | tf_op jit(solution)/shard_map/ppermute | solution.py:189
  44.8 1.1 %collective-permute-done.4 = bf16[4,128,256]{2,1,0:T(8,128)(2,1)S(1)} collective-permute-done((bf16[4,128,256]{2,1,0:T(8,128)(2,1)S(1)}, bf16[4,128,256]{2,1,0:T(8,128)(2,1)S(1)}, u32[]{:S(2)}, u32[]{:S(2)}) %collective-permute-start.4) | collective-permute-done | bytes 262176 | tf_op jit(solution)/shard_map/ppermute | solution.py:189
  45.9 0.1 maximum_select_fusion
  46.1 12.2 %collective-permute-start.7 = (bf16[128,512]{1,0:T(8,128)(2,1)S(1)}, bf16[128,512]{1,0:T(8,128)(2,1)S(1)}, u32[]{:S(2)}, u32[]{:S(2)}) collective-permute-start(bf16[128,512]{1,0:T(8,128)(2,1)S(1)} %get-tuple-element.29), channel_id=1, source_target_pairs={{0,508},{4,8},{8,4},{12,16},{16,12},{20,24},{24,20},{28,32},{32,28... | collective-permute-start | bytes 393224 | tf_op jit(solution)/shard_map/ppermute | solution.py:197
  58.3 4.0 %collective-permute-start.6 = (bf16[128,512]{1,0:T(8,128)(2,1)S(1)}, bf16[128,512]{1,0:T(8,128)(2,1)S(1)}, u32[]{:S(2)}, u32[]{:S(2)}) collective-permute-start(bf16[128,512]{1,0:T(8,128)(2,1)S(1)} %get-tuple-element.30), channel_id=1, source_target_pairs={{0,504},{4,12},{8,0},{12,20},{16,8},{20,28},{24,16},{28,36},{32,24... | collective-permute-start | bytes 393224 | tf_op jit(solution)/shard_map/ppermute | solution.py:198
  62.3 1.9 %collective-permute-start.5 = (bf16[128,512]{1,0:T(8,128)(2,1)S(1)}, bf16[128,512]{1,0:T(8,128)(2,1)S(1)}, u32[]{:S(2)}, u32[]{:S(2)}) collective-permute-start(bf16[128,512]{1,0:T(8,128)(2,1)S(1)} %get-tuple-element.31), channel_id=1, source_target_pairs={{0,500},{4,16},{8,508},{12,24},{16,4},{20,32},{24,12},{28,40},{32,... | collective-permute-start | bytes 393224 | tf_op jit(solution)/shard_map/ppermute | solution.py:199
  64.2 0.0 collective-permute-done.7
  64.3 0.9 %collective-permute-done.6 = bf16[128,512]{1,0:T(8,128)(2,1)S(1)} collective-permute-done((bf16[128,512]{1,0:T(8,128)(2,1)S(1)}, bf16[128,512]{1,0:T(8,128)(2,1)S(1)}, u32[]{:S(2)}, u32[]{:S(2)}) %collective-permute-start.6) | collective-permute-done | bytes 131104 | tf_op jit(solution)/shard_map/ppermute | solution.py:198
  65.2 7.0 %collective-permute-done.5 = bf16[128,512]{1,0:T(8,128)(2,1)S(1)} collective-permute-done((bf16[128,512]{1,0:T(8,128)(2,1)S(1)}, bf16[128,512]{1,0:T(8,128)(2,1)S(1)}, u32[]{:S(2)}, u32[]{:S(2)}) %collective-permute-start.5) | collective-permute-done | bytes 131104 | tf_op jit(solution)/shard_map/ppermute | solution.py:199
  72.2 0.9 %maximum_bitcast_fusion = bf16[1,1,4,128,512]{4,3,2,1,0:T(8,128)(2,1)} fusion(bf16[1,128,512]{2,1,0:T(8,128)(2,1)S(1)} %get-tuple-element.33, bf16[1,128,512]{2,1,0:T(8,128)(2,1)S(1)} %get-tuple-element.28, bf16[1,128,512]{2,1,0:T(8,128)(2,1)S(1)} %get-tuple-element.27, bf16[1,128,512]{2,1,0:T(8,128)(2,1)S(1)} %get-tuple-element.32), kind=kLoop, calls=%fused_computation.1 | loop fusion | flops 786432 | bytes 1048576 | tf_op jit(solution)/shard_map/broadcast_in_dim | solution.py:209
  (8 shorter events, 0.2 us)
Async XLA Ops:
  0.0 20.4 %copy-start.6 = (s32[8,16]{1,0:T(8,128)S(1)}, s32[8,16]{1,0:T(8,128)}, u32[]{:S(2)}) copy-start(s32[8,16]{1,0:T(8,128)} %lo.1) | copy-start | bytes 1540
  0.0 20.4 %copy-start.7 = (s32[8,16]{1,0:T(8,128)S(1)}, s32[8,16]{1,0:T(8,128)}, u32[]{:S(2)}) copy-start(s32[8,16]{1,0:T(8,128)} %hi.1) | copy-start | bytes 1540
  0.0 20.4 %copy-start = (bf16[8,16,64,128]{3,2,1,0:T(8,128)(2,1)S(1)}, bf16[8,16,64,128]{3,2,1,0:T(8,128)(2,1)}, u32[]{:S(2)}) copy-start(bf16[8,16,64,128]{3,2,1,0:T(8,128)(2,1)} %vox.1) | copy-start | bytes 6291460
  0.0 16.2 %copy-start.9 = (f32[64]{0:T(128)S(1)}, f32[64]{0:T(128)}, u32[]{:S(2)}) copy-start(f32[64]{0:T(128)} %param.12) | copy-start | bytes 772
  0.0 19.7 %copy-start.8 = (s32[64,1,8]{0,2,1:T(8,128)S(1)}, s32[64,1,8]{0,2,1:T(8,128)}, u32[]{:S(2)}) copy-start(s32[64,1,8]{0,2,1:T(8,128)} %param.15) | copy-start | bytes 6148
  3.2 6.7 %collective-permute-start.1 = (bf16[8,64,128]{2,1,0:T(8,128)(2,1)S(1)}, bf16[8,64,128]{2,1,0:T(8,128)(2,1)S(1)}, u32[]{:S(2)}, u32[]{:S(2)}) collective-permute-start(bf16[8,64,128]{2,1,0:T(8,128)(2,1)S(1)} %get-tuple-element.25), channel_id=1, source_target_pairs={{1,0},{2,1},{3,2},{5,4},{6,5},{7,6},{9,8},{10,9},{11,10},{13,12},{... | collective-permute-start | bytes 393224 | tf_op jit(solution)/shard_map/ppermute | solution.py:171
  5.9 6.9 %collective-permute-start = (bf16[8,64,128]{2,1,0:T(8,128)(2,1)S(1)}, bf16[8,64,128]{2,1,0:T(8,128)(2,1)S(1)}, u32[]{:S(2)}, u32[]{:S(2)}) collective-permute-start(bf16[8,64,128]{2,1,0:T(8,128)(2,1)S(1)} %get-tuple-element.26), channel_id=1, source_target_pairs={{0,1},{1,2},{2,3},{4,5},{5,6},{6,7},{8,9},{9,10},{10,11},{12,13},{... | collective-permute-start | bytes 393224 | tf_op jit(solution)/shard_map/ppermute | solution.py:170
  12.8 7.1 %collective-permute-start.2 = (bf16[18,64,128]{2,1,0:T(8,128)(2,1)S(1)}, bf16[18,64,128]{2,1,0:T(8,128)(2,1)S(1)}, u32[]{:S(2)}, u32[]{:S(2)}) collective-permute-start(bf16[18,64,128]{2,1,0:T(8,128)(2,1)S(1)} %pad_maximum_fusion), channel_id=1, source_target_pairs={{0,4},{4,8},{8,12},{12,16},{16,20},{20,24},{24,28},{28,32},{32,36}... | collective-permute-start | bytes 884744 | tf_op jit(solution)/shard_map/ppermute | solution.py:180
  14.9 5.5 %collective-permute-start.3 = (bf16[18,64,128]{2,1,0:T(8,128)(2,1)}, bf16[18,64,128]{2,1,0:T(8,128)(2,1)S(1)}, u32[]{:S(2)}, u32[]{:S(2)}) collective-permute-start(bf16[18,64,128]{2,1,0:T(8,128)(2,1)} %pad_maximum_fusion.1), channel_id=1, source_target_pairs={{4,0},{8,4},{12,8},{16,12},{20,16},{24,20},{28,24},{32,28},{36,32}... | collective-permute-start | bytes 884744 | tf_op jit(solution)/shard_map/ppermute | solution.py:181
  20.4 1.2 %copy-start.1 = (bf16[1024,512]{1,0:T(8,128)(2,1)S(1)}, bf16[1024,512]{1,0:T(8,128)(2,1)}, u32[]{:S(2)}) copy-start(bf16[1024,512]{1,0:T(8,128)(2,1)} %get-tuple-element.16.sel) | copy-start | bytes 3145732
  21.6 1.1 %copy-start.2 = (bf16[384,768]{1,0:T(8,128)(2,1)S(1)}, bf16[384,768]{1,0:T(8,128)(2,1)}, u32[]{:S(2)}) copy-start(bf16[384,768]{1,0:T(8,128)(2,1)} %get-tuple-element.12.w) | copy-start | bytes 1769476
  22.7 0.9 %copy-start.3 = (bf16[256,256]{1,0:T(8,128)(2,1)S(1)}, bf16[256,256]{1,0:T(8,128)(2,1)}, u32[]{:S(2)}) copy-start(bf16[256,256]{1,0:T(8,128)(2,1)} %get-tuple-element.13.d) | copy-start | bytes 393220
  23.6 0.8 %copy-start.4 = (f32[128,128]{1,0:T(8,128)S(1)}, f32[128,128]{1,0:T(8,128)}, u32[]{:S(2)}) copy-start(f32[128,128]{1,0:T(8,128)} %get-tuple-element.14.cb) | copy-start | bytes 196612
  24.4 0.8 %copy-start.5 = (f32[128,128]{1,0:T(8,128)S(1)}, f32[128,128]{1,0:T(8,128)}, u32[]{:S(2)}) copy-start(f32[128,128]{1,0:T(8,128)} %get-tuple-element.15.db) | copy-start | bytes 196612
  37.8 8.1 %collective-permute-start.4 = (bf16[4,128,256]{2,1,0:T(8,128)(2,1)S(1)}, bf16[4,128,256]{2,1,0:T(8,128)(2,1)S(1)}, u32[]{:S(2)}, u32[]{:S(2)}) collective-permute-start(bf16[4,128,256]{2,1,0:T(8,128)(2,1)S(1)} %get-tuple-element.18), channel_id=1, source_target_pairs={{0,4},{4,0},{8,12},{12,8},{16,20},{20,16},{24,28},{28,24},{32,36},... | collective-permute-start | bytes 786440 | tf_op jit(solution)/shard_map/ppermute | solution.py:189
  46.1 18.1 %collective-permute-start.7 = (bf16[128,512]{1,0:T(8,128)(2,1)S(1)}, bf16[128,512]{1,0:T(8,128)(2,1)S(1)}, u32[]{:S(2)}, u32[]{:S(2)}) collective-permute-start(bf16[128,512]{1,0:T(8,128)(2,1)S(1)} %get-tuple-element.29), channel_id=1, source_target_pairs={{0,508},{4,8},{8,4},{12,16},{16,12},{20,24},{24,20},{28,32},{32,28... | collective-permute-start | bytes 393224 | tf_op jit(solution)/shard_map/ppermute | solution.py:197
  58.3 6.9 %collective-permute-start.6 = (bf16[128,512]{1,0:T(8,128)(2,1)S(1)}, bf16[128,512]{1,0:T(8,128)(2,1)S(1)}, u32[]{:S(2)}, u32[]{:S(2)}) collective-permute-start(bf16[128,512]{1,0:T(8,128)(2,1)S(1)} %get-tuple-element.30), channel_id=1, source_target_pairs={{0,504},{4,12},{8,0},{12,20},{16,8},{20,28},{24,16},{28,36},{32,24... | collective-permute-start | bytes 393224 | tf_op jit(solution)/shard_map/ppermute | solution.py:198
  62.3 9.9 %collective-permute-start.5 = (bf16[128,512]{1,0:T(8,128)(2,1)S(1)}, bf16[128,512]{1,0:T(8,128)(2,1)S(1)}, u32[]{:S(2)}, u32[]{:S(2)}) collective-permute-start(bf16[128,512]{1,0:T(8,128)(2,1)S(1)} %get-tuple-element.31), channel_id=1, source_target_pairs={{0,500},{4,16},{8,508},{12,24},{16,4},{20,32},{24,12},{28,40},{32,... | collective-permute-start | bytes 393224 | tf_op jit(solution)/shard_map/ppermute | solution.py:199

commit v2 on v1

v2 whole, which is shorter than its diff:
```python
import jax
import jax.numpy as jnp
from jax import lax
from jax.experimental import pallas as pl
from jax.experimental.pallas import tpu as pltpu
from jax.sharding import PartitionSpec as P

BF = jnp.bfloat16
F32 = jnp.float32
VMEM = pltpu.VMEM
SMEM = pltpu.SMEM


def small_vmem(mib):
    return pltpu.CompilerParams(vmem_limit_bytes=mib * 1024 * 1024)


def prep_kernel(cw, cb, dw, db, w_out, d_out, cb_out, db_out, sel_out):
    zero = jnp.zeros((64, 64), F32)
    for dx in range(3):
        for dz in range(3):
            taps = [cw[dx, dy, dz].astype(F32) for dy in range(3)]
            for yo in range(2):
                line = ([zero] if yo else []) + taps + ([] if yo else [zero])
                for half in range(2):
                    pair = jnp.concatenate(line[2 * half : 2 * half + 2], axis=0)
                    row = (dz * 2 + yo) * 64
                    col = (dx * 4 + half * 2) * 64
                    w_out[row : row + 64, col : col + 128] = pair.T.astype(BF)
    for k in range(2):
        for i in range(2):
            pair = jnp.concatenate([dw[4 * i + k], dw[4 * i + 2 + k]], axis=0).astype(F32)
            d_out[k * 128 : k * 128 + 128, i * 128 : i * 128 + 128] = pair.T.astype(BF)
    cb_out[...] = jnp.broadcast_to(cb[...], (128, 128)).T
    db_out[...] = jnp.broadcast_to(db[...], (128, 128)).T
    for q in range(8):
        z = lax.broadcasted_iota(jnp.int32, (128, 512), 0)
        lane = lax.broadcasted_iota(jnp.int32, (128, 512), 1)
        want = jnp.where(((lane >> 3) & 7) == q, 16 * (lane >> 6) + 2 * (lane & 7), -1)
        sel_out[q * 128 : q * 128 + 128, :] = jnp.where(z == want, 1.0, 0.0).astype(BF)


def prep(conv_weight, conv_bias, down_weight, down_bias):
    return pl.pallas_call(
        prep_kernel,
        out_shape=(
            jax.ShapeDtypeStruct((384, 768), BF),
            jax.ShapeDtypeStruct((256, 256), BF),
            jax.ShapeDtypeStruct((128, 128), F32),
            jax.ShapeDtypeStruct((128, 128), F32),
            jax.ShapeDtypeStruct((1024, 512), BF),
        ),
        compiler_params=small_vmem(8),
        cost_estimate=pl.CostEstimate(flops=10**9, bytes_accessed=4 * 10**6, transcendentals=0),
        name="prep",
    )(
        conv_weight,
        jnp.tile(conv_bias, 2)[None],
        down_weight,
        down_bias[None],
    )


def occupancy(lo, hi, x, y):
    lane = lax.broadcasted_iota(jnp.int32, (8, 128), 1)
    return jnp.where((lane >= lo[x, y]) & (lane < hi[x, y]), 1.0, 0.0)


def masked_column(column, lo, hi, x, y):
    mask = jnp.concatenate([occupancy(lo, hi, x, y)] * 2, axis=0).astype(BF)
    return (column.reshape(4, 16, 128) * mask[None]).reshape(64, 128)


def faces_kernel(lo, hi, vox, y_first, y_last, x_first, x_last, sems):
    copies = [
        pltpu.make_async_copy(vox.at[:, 0], y_first, sems.at[0]),
        pltpu.make_async_copy(vox.at[:, 15], y_last, sems.at[1]),
        pltpu.make_async_copy(vox.at[0], x_first, sems.at[2]),
        pltpu.make_async_copy(vox.at[7], x_last, sems.at[3]),
    ]
    for copy in copies:
        copy.start()
    for copy, ref, y in ((copies[0], y_first, 0), (copies[1], y_last, 15)):
        copy.wait()
        for x in range(8):
            ref[x] = masked_column(ref[x], lo, hi, x, y)
    for copy, ref, x in ((copies[2], x_first, 0), (copies[3], x_last, 7)):
        copy.wait()
        for y in range(16):
            ref[y] = masked_column(ref[y], lo, hi, x, y)


def faces(lo, hi, vox):
    y_face = jax.ShapeDtypeStruct((8, 64, 128), BF)
    x_face = jax.ShapeDtypeStruct((16, 64, 128), BF)
    smem = pl.BlockSpec(memory_space=SMEM)
    vmem = pl.BlockSpec(memory_space=VMEM)
    return pl.pallas_call(
        faces_kernel,
        out_shape=(y_face, y_face, x_face, x_face),
        in_specs=[smem, smem, pl.BlockSpec(memory_space=pltpu.HBM)],
        out_specs=(vmem,) * 4,
        scratch_shapes=[pltpu.SemaphoreType.DMA((4,))],
        compiler_params=small_vmem(4),
        name="faces",
    )(lo, hi, vox)


def scene_rows(starts, columns, lo, hi, pad, w, d, cb, db, sel, cells):
    lane8 = lax.broadcasted_iota(jnp.int32, (8, 128), 1)
    lane = lax.broadcasted_iota(jnp.int32, (128, 128), 1)

    def conv_cell(row, x, yp):
        rows = [pad[row + r, pl.ds(2 * yp, 4)].reshape(256, 128) for r in range(4)]
        window = jnp.concatenate(
            [jnp.concatenate([rows[t], rows[t + 1]], axis=1) for t in range(3)], axis=0
        )
        summed = jnp.dot(w[...], window, preferred_element_type=F32)
        parts = []
        for xi in range(2):
            part = summed[:, xi * 128 : xi * 128 + 128]
            below = jnp.where(lane == 0, 0.0, pltpu.roll(part[0:128], 1, 1))
            above = jnp.where(lane == 127, 0.0, pltpu.roll(part[256:384], 127, 1))
            half = (below + above + part[128:256] + cb[...]) * 0.5
            act = half + half * jnp.tanh(half)
            masks = [occupancy(lo, hi, x + xi, 2 * yp + yo) for yo in range(2)]
            act = act.reshape(2, 8, 8, 128) * jnp.stack(masks)[:, None]
            parts.append(act.reshape(128, 128).astype(BF))
        return jnp.concatenate(parts, axis=0)

    def coarse_mask(x0, yp):
        found = None
        for xi in range(2):
            for yo in range(2):
                x, y = x0 + xi, 2 * yp + yo
                here = (lane8 + 1 >= lo[x, y]) & (lane8 < hi[x, y])
                found = here if found is None else found | here
        return jnp.where(found, 1.0, 0.0)

    (row0, x0), (row1, x1) = starts

    @pl.loop(0, 2)
    def _(t):
        row = row0 + t * (row1 - row0)
        x = x0 + t * (x1 - x0)
        for ypp in range(4):
            hidden = jnp.concatenate(
                [conv_cell(row, x, 2 * ypp), conv_cell(row, x, 2 * ypp + 1)], axis=1
            )
            down = jnp.dot(d[...], hidden, preferred_element_type=F32)
            for e in range(2):
                q = 2 * ypp + e
                part = down[:, e * 128 : e * 128 + 128]
                total = part[0:128] + pltpu.roll(part[128:256], 127, 1) + db[...]
                total = total.reshape(16, 8, 128) * coarse_mask(x, q)[None]
                cells[pl.ds(t * 128, 128), q * 128 : q * 128 + 128] = total.reshape(
                    128, 128
                ).astype(BF)

    return jnp.dot(cells[...], sel[...], preferred_element_type=F32)


def inner_kernel(lo, hi, vox, ylo, yhi, w, d, cb, db, sel, out, pad, cells):
    for r in range(6):
        pad[r, 0] = ylo[r + 1]
        pad[r, 17] = yhi[r + 1]

    @pl.loop(0, 6)
    def _(r):
        for y in range(16):
            pad[r, y + 1] = masked_column(vox[r + 1, y], lo, hi, r + 1, y)

    out[...] = scene_rows(((0, 2), (2, 4)), None, lo, hi, pad, w, d, cb, db, sel, cells)


def outer_kernel(
    lo, hi, slots, vox, ylo, yhi, xlo, xhi, inner, w, d, cb, db, sel, keep, give, pad, cells, pieces
):
    pad[0] = xlo[...]
    pad[7] = xhi[...]
    for r in range(3):
        pad[r + 1, 0] = ylo[r]
        pad[r + 1, 17] = yhi[r]
        pad[r + 4, 0] = ylo[r + 5]
        pad[r + 4, 17] = yhi[r + 5]

    @pl.loop(0, 3)
    def _(r):
        for y in range(16):
            pad[r + 1, y + 1] = masked_column(vox[r, y], lo, hi, r, y)
            pad[r + 4, y + 1] = masked_column(vox[r + 5, y], lo, hi, r + 5, y)

    ends = scene_rows(((0, 0), (4, 6)), None, lo, hi, pad, w, d, cb, db, sel, cells)
    rows = (ends[0:128], inner[0:128], inner[128:256], ends[128:256])
    for pair in range(2):
        for level in range(8):
            at = slice(level * 64, level * 64 + 64)
            both = jnp.concatenate([rows[2 * pair][:, at], rows[2 * pair + 1][:, at]], axis=1)
            pieces[slots[level], :, pair * 128 : pair * 128 + 128] = both.astype(BF)
    keep[...] = pieces[0:4]
    give[...] = pieces[4:8]


def inner_rows(lo, hi, vox, ylo, yhi, tables):
    smem = pl.BlockSpec(memory_space=SMEM)
    vmem = pl.BlockSpec(memory_space=VMEM)
    return pl.pallas_call(
        inner_kernel,
        out_shape=jax.ShapeDtypeStruct((256, 512), F32),
        in_specs=[smem] * 2 + [vmem] * 8,
        out_specs=vmem,
        scratch_shapes=[VMEM((6, 18, 64, 128), BF), VMEM((256, 1024), BF)],
        compiler_params=small_vmem(12),
        cost_estimate=pl.CostEstimate(flops=5 * 10**9, bytes_accessed=4 * 10**6, transcendentals=0),
        name="inner",
    )(lo, hi, vox, ylo, yhi, *tables)


def outer_rows(lo, hi, slots, vox, ylo, yhi, xlo, xhi, inner, tables):
    half = jax.ShapeDtypeStruct((4, 128, 256), BF)
    smem = pl.BlockSpec(memory_space=SMEM)
    vmem = pl.BlockSpec(memory_space=VMEM)
    return pl.pallas_call(
        outer_kernel,
        out_shape=(half, half),
        in_specs=[smem] * 3 + [vmem] * 11,
        out_specs=(vmem, vmem),
        scratch_shapes=[
            VMEM((8, 18, 64, 128), BF),
            VMEM((256, 1024), BF),
            VMEM((8, 128, 256), BF),
        ],
        compiler_params=small_vmem(12),
        name="outer",
    )(lo, hi, slots, vox, ylo, yhi, xlo, xhi, inner, *tables)


def ring(count, step):
    return [(i, step(i) % count) for i in range(count)]


def local(voxels, shell_lo, shell_hi, conv_weight, conv_bias, down_weight, down_bias, coarse_owner):
    blk_n = lax.axis_size("blk")
    grp_n = lax.axis_size("grp")
    me = lax.axis_index("blk")
    core = me % 2

    up = [(i, i + 1) for i in range(grp_n - 1)]
    down = [(b, a) for a, b in up]
    y_first, y_last, x_first, x_last = faces(shell_lo, shell_hi, voxels)
    ylo = lax.ppermute(y_last, "grp", up)
    yhi = lax.ppermute(y_first, "grp", down)
    tables = prep(conv_weight, conv_bias, down_weight, down_bias)
    ylo, yhi, tables = lax.optimization_barrier((ylo, yhi, tables))

    ahead = [(i, i + 1) for i in range(blk_n - 1)]
    behind = [(b, a) for a, b in ahead]
    xlo = lax.ppermute(jnp.concatenate([ylo[7:8], x_last, yhi[7:8]]), "blk", ahead)
    xhi = lax.ppermute(jnp.concatenate([ylo[0:1], x_first, yhi[0:1]]), "blk", behind)
    inner = inner_rows(shell_lo, shell_hi, voxels, ylo, yhi, tables)

    column = me // 2
    owners = lax.dynamic_index_in_dim(coarse_owner[:, 0, :], column, 0, keepdims=False)
    offset = (owners - 2 * column + 3) % blk_n - 3
    place = jnp.where(offset <= 0, offset + 3, 4 - offset)
    slots = jnp.where((offset <= 0) == (core == 0), place, place + 4)

    keep, give = outer_rows(
        shell_lo, shell_hi, slots, voxels, ylo, yhi, xlo, xhi, inner, tables
    )
    got = lax.ppermute(give, "blk", ring(blk_n, lambda i: i ^ 1))
    even = core == 0
    whole = jnp.where(
        even, jnp.concatenate([keep, got], axis=2), jnp.concatenate([got, keep], axis=2)
    )
    near = lax.ppermute(whole[0:2], "blk", ring(blk_n, lambda i: i + 2 if i % 2 else i - 2))
    far = lax.ppermute(
        jnp.concatenate([near[0:1], whole[2:3]]),
        "blk",
        ring(blk_n, lambda i: i + 1 if i % 2 else i - 1),
    )
    result = jnp.where(
        even,
        jnp.stack([far[0], far[1], whole[3], near[1]]),
        jnp.stack([near[1], whole[3], far[1], far[0]]),
    )
    return result[None, None]


def solution(mesh):
    placed = (
        P("blk", "grp", None, None),
        P("blk", "grp"),
        P("blk", "grp"),
        P(),
        P(),
        P(),
        P(),
        P(None, "grp", None),
    )
    return jax.shard_map(
        local,
        mesh=mesh,
        in_specs=placed,
        out_specs=P("blk", "grp", None, None, None),
        check_vma=False,
    )
```

time: 73.7 us -> 67.4 us (0.915)
  the two profiles are of different devices: /device:TPU:6 before, /device:TPU:2 now
where the time goes in v2:
time: 67.4 us; the launch traced here: 67.1 us
  starting transfers between devices  32.4 us (48%)
  Pallas kernels  15.5 us (23%)
  waiting for transfers between devices  14.3 us (21%)
  local copies, waits for them, and re-layouts  3.16 us (5%)
  other arithmetic  1.34 us (2%)
    ppermute x1, starting transfers between devices, local(): lax.ppermute(whole[0:2], 'blk', ring(blk_n, lambda i: i + 2 if i % 2 else...  14.3 us
    ppermute x1, waiting for transfers between devices, local(): lax.ppermute(jnp.concatenate([near[0:1], whole[2:3]]), 'blk', ring(blk_n,...  8.02 us
    pallas_call x1, Pallas kernels, outer_rows(): pl.pallas_call(outer_kernel, out_shape=(half, half), in_specs=[smem] * 3...  7.01 us
    pallas_call x1, Pallas kernels, inner_rows(): pl.pallas_call(inner_kernel, out_shape=jax.ShapeDtypeStruct((256, 512), F...  6.82 us
    ppermute x1, starting transfers between devices, local(): yhi = lax.ppermute(y_first, 'grp', down)  5.69 us
    ppermute x1, waiting for transfers between devices, local(): lax.ppermute(whole[0:2], 'blk', ring(blk_n, lambda i: i + 2 if i % 2 else...  3.84 us
    ppermute x1, starting transfers between devices, local(): got = lax.ppermute(give, 'blk', ring(blk_n, lambda i: i ^ 1))  3.5 us
    ppermute x1, starting transfers between devices, local(): ylo = lax.ppermute(y_last, 'grp', up)  3.4 us
  transfers between devices with their start and end apart: 7, of which 4 were waited for; matrix products, arithmetic and copies ran while one was open for 1% of the time, Pallas kernels for 11%

profile of v2, /device:TPU:2, one launch (start us, length us, event | category | flops | bytes accessed | tf_op | source)
XLA Modules:
  0.0 67.1 jit_solution(3005298548353956458)
XLA Ops:
  0.0 0.0 copy-start
  0.0 1.6 %copy-done = bf16[8,16,64,128]{3,2,1,0:T(8,128)(2,1)S(1)} copy-done((bf16[8,16,64,128]{3,2,1,0:T(8,128)(2,1)S(1)}, bf16[8,16,64,128]{3,2,1,0:T(8,128)(2,1)}, u32[]{:S(2)}) %copy-start) | copy-done | bytes 2097176
  1.6 0.0 copy-start.2
  1.6 0.7 %copy-done.2 = s32[8,16]{1,0:T(8,128)S(1)} copy-done((s32[8,16]{1,0:T(8,128)S(1)}, s32[8,16]{1,0:T(8,128)}, u32[]{:S(2)}) %copy-start.2) | copy-done | bytes 536
  2.3 0.0 copy-start.4
  2.3 0.7 %copy-done.4 = s32[8,16]{1,0:T(8,128)S(1)} copy-done((s32[8,16]{1,0:T(8,128)S(1)}, s32[8,16]{1,0:T(8,128)}, u32[]{:S(2)}) %copy-start.4) | copy-done | bytes 536
  3.0 0.0 copy-start.9
  3.0 0.0 copy-start.10
  3.0 0.0 copy-start.6
  3.0 0.0 copy-start.7
  3.0 0.0 copy-start.8
  3.0 0.9 %faces.1 = (bf16[8,64,128]{2,1,0:T(8,128)(2,1)S(1)}, bf16[8,64,128]{2,1,0:T(8,128)(2,1)S(1)}, bf16[16,64,128]{2,1,0:T(8,128)(2,1)S(1)}, bf16[16,64,128]{2,1,0:T(8,128)(2,1)S(1)}) custom-call(s32[8,16]{1,0:T(8,128)S(1)} %copy-done.2, s32[8,16]{1,0:T(8,128)S(1)} %copy-done.4, bf16[8,16,64,128]{3,2,1,0:T(8,128)(2,1)S(1)} %copy-done), custom_call_target="tpu_custom_call" | custom-call | tf_op jit(solution)/shard_map/faces/pallas_call | solution.py:98
  3.9 3.4 %collective-permute-start = (bf16[8,64,128]{2,1,0:T(8,128)(2,1)S(1)}, bf16[8,64,128]{2,1,0:T(8,128)(2,1)S(1)}, u32[]{:S(2)}, u32[]{:S(2)}) collective-permute-start(bf16[8,64,128]{2,1,0:T(8,128)(2,1)S(1)} %get-tuple-element.23), channel_id=1, source_target_pairs={{0,1},{1,2},{2,3},{4,5},{5,6},{6,7},{8,9},{9,10},{10,11},{12,13},{... | collective-permute-start | bytes 393224 | tf_op jit(solution)/shard_map/ppermute | solution.py:251
  7.3 5.7 %collective-permute-start.1 = (bf16[8,64,128]{2,1,0:T(8,128)(2,1)S(1)}, bf16[8,64,128]{2,1,0:T(8,128)(2,1)S(1)}, u32[]{:S(2)}, u32[]{:S(2)}) collective-permute-start(bf16[8,64,128]{2,1,0:T(8,128)(2,1)S(1)} %get-tuple-element.24), channel_id=1, source_target_pairs={{1,0},{2,1},{3,2},{5,4},{6,5},{7,6},{9,8},{10,9},{11,10},{13,12},{... | collective-permute-start | bytes 393224 | tf_op jit(solution)/shard_map/ppermute | solution.py:252
  13.1 0.0 copy-done.9
  13.1 0.2 add_reduce_fusion
  13.3 0.0 copy-done.10
  13.3 0.1 broadcast_in_dim_tile.3.cb
  13.4 0.0 copy-done.6
  13.4 0.0 copy-done.7
  13.4 0.0 copy-done.8
  13.4 0.0 copy-start.1
  13.4 0.0 copy-start.3
  13.4 0.0 copy-start.5
  13.4 0.8 %prep.1 = (bf16[384,768]{1,0:T(8,128)(2,1)S(1)}, bf16[256,256]{1,0:T(8,128)(2,1)S(1)}, f32[128,128]{1,0:T(8,128)S(1)}, f32[128,128]{1,0:T(8,128)S(1)}, bf16[1024,512]{1,0:T(8,128)(2,1)S(1)}) custom-call(bf16[3,3,3,64,64]{4,3,2,1,0:T(8,128)(2,1)S(1)} %copy-done.6, f32[1,128]{1,0:T(1,128)S(1)} %broadcast_in_dim_tile.3.cb, bf16[8,64,128]{2,1,0:T(8,128)(2,1)S(1)} %copy-done.7, ...), custom_call_target="tpu_custom_call" | custom-call | flops 1000000000 | bytes 4000000 | tf_op jit(solution)/shard_map/prep/pallas_call | solution.py:44
  14.2 0.0 collective-permute-done.ylo
  14.2 1.3 %collective-permute-done.1.yhi = bf16[8,64,128]{2,1,0:T(8,128)(2,1)S(1)} collective-permute-done((bf16[8,64,128]{2,1,0:T(8,128)(2,1)S(1)}, bf16[8,64,128]{2,1,0:T(8,128)(2,1)S(1)}, u32[]{:S(2)}, u32[]{:S(2)}) %collective-permute-start.1) | collective-permute-done | bytes 131104 | tf_op jit(solution)/shard_map/ppermute | solution.py:252
  15.6 1.3 %collective-permute-start.2 = (bf16[18,64,128]{2,1,0:T(8,128)(2,1)S(1)}, bf16[18,64,128]{2,1,0:T(8,128)(2,1)S(1)}, u32[]{:S(2)}, u32[]{:S(2)}) collective-permute-start(bf16[18,64,128]{2,1,0:T(8,128)(2,1)S(1)} %pad_maximum_fusion), channel_id=1, source_target_pairs={{0,4},{4,8},{8,12},{12,16},{16,20},{20,24},{24,28},{28,32},{32,36}... | collective-permute-start | bytes 884744 | tf_op jit(solution)/shard_map/ppermute | solution.py:258
  16.9 1.3 %collective-permute-start.3 = (bf16[18,64,128]{2,1,0:T(8,128)(2,1)S(1)}, bf16[18,64,128]{2,1,0:T(8,128)(2,1)S(1)}, u32[]{:S(2)}, u32[]{:S(2)}) collective-permute-start(bf16[18,64,128]{2,1,0:T(8,128)(2,1)S(1)} %pad_maximum_fusion.1), channel_id=1, source_target_pairs={{4,0},{8,4},{12,8},{16,12},{20,16},{24,20},{28,24},{32,28},{36,32}... | collective-permute-start | bytes 884744 | tf_op jit(solution)/shard_map/ppermute | solution.py:259
  18.2 0.0 copy-done.1
  18.3 0.0 copy-done.3
  18.3 0.0 copy-done.5
  18.3 6.8 %inner.1 = f32[256,512]{1,0:T(8,128)S(1)} custom-call(s32[8,16]{1,0:T(8,128)S(1)} %copy-done.3, s32[8,16]{1,0:T(8,128)S(1)} %copy-done.5, bf16[8,16,64,128]{3,2,1,0:T(8,128)(2,1)S(1)} %copy-done.1, bf16[8,64,128]{2,1,0:T(8,128)(2,1)S(1)} %collective-permute-done.ylo, bf16[8,64,128]{2,1,0:T(8,128)(2,1)S(1)} %collective-permute-done.1.yhi, ...), custom_call_target="tpu_custom_call" | custom-call | flops 5000000000 | bytes 4000000 | tf_op jit(solution)/shard_map/inner/pallas_call | solution.py:207
  25.1 0.0 collective-permute-done.2.xlo
  25.1 0.0 collective-permute-done.3.xhi
  25.1 7.0 %outer.1 = (bf16[4,128,256]{2,1,0:T(8,128)(2,1)S(1)}, bf16[4,128,256]{2,1,0:T(8,128)(2,1)S(1)}) custom-call(s32[8,16]{1,0:T(8,128)S(1)} %copy-done.3, s32[8,16]{1,0:T(8,128)S(1)} %copy-done.5, s32[8]{0:T(128)S(1)} %compare_select_fusion.2.slots, bf16[8,16,64,128]{3,2,1,0:T(8,128)(2,1)S(1)} %copy-done.1, bf16[8,64,128]{2,1,0:T(8,128)(2,1)S(1)} %collective-permute-done.ylo, ...), custom_call_target="tpu_custom_call" | custom-call | tf_op jit(solution)/shard_map/outer/pallas_call | solution.py:223
  32.1 3.5 %collective-permute-start.4 = (bf16[4,128,256]{2,1,0:T(8,128)(2,1)S(1)}, bf16[4,128,256]{2,1,0:T(8,128)(2,1)S(1)}, u32[]{:S(2)}, u32[]{:S(2)}) collective-permute-start(bf16[4,128,256]{2,1,0:T(8,128)(2,1)S(1)} %get-tuple-element.40), channel_id=1, source_target_pairs={{0,4},{4,0},{8,12},{12,8},{16,20},{20,16},{24,28},{28,24},{32,36},... | collective-permute-start | bytes 786440 | tf_op jit(solution)/shard_map/ppermute | solution.py:271
  35.7 1.1 %collective-permute-done.4 = bf16[4,128,256]{2,1,0:T(8,128)(2,1)S(1)} collective-permute-done((bf16[4,128,256]{2,1,0:T(8,128)(2,1)S(1)}, bf16[4,128,256]{2,1,0:T(8,128)(2,1)S(1)}, u32[]{:S(2)}, u32[]{:S(2)}) %collective-permute-start.4) | collective-permute-done | bytes 262176 | tf_op jit(solution)/shard_map/ppermute | solution.py:271
  36.8 0.1 maximum_select_fusion
  37.0 14.3 %collective-permute-start.5 = (bf16[2,128,512]{2,1,0:T(8,128)(2,1)S(1)}, bf16[2,128,512]{2,1,0:T(8,128)(2,1)S(1)}, u32[]{:S(2)}, u32[]{:S(2)}) collective-permute-start(bf16[2,128,512]{2,1,0:T(8,128)(2,1)S(1)} %slice.49), channel_id=1, source_target_pairs={{0,504},{4,12},{8,0},{12,20},{16,8},{20,28},{24,16},{28,36},{32,24... | collective-permute-start | bytes 786440 | tf_op jit(solution)/shard_map/ppermute | solution.py:276
  51.3 3.8 %collective-permute-done.5 = bf16[2,128,512]{2,1,0:T(8,128)(2,1)S(1)} collective-permute-done((bf16[2,128,512]{2,1,0:T(8,128)(2,1)S(1)}, bf16[2,128,512]{2,1,0:T(8,128)(2,1)S(1)}, u32[]{:S(2)}, u32[]{:S(2)}) %collective-permute-start.5) | collective-permute-done | bytes 262176 | tf_op jit(solution)/shard_map/ppermute | solution.py:276
  55.2 3.0 %collective-permute-start.6 = (bf16[2,128,512]{2,1,0:T(8,128)(2,1)S(1)}, bf16[2,128,512]{2,1,0:T(8,128)(2,1)S(1)}, u32[]{:S(2)}, u32[]{:S(2)}) collective-permute-start(bf16[2,128,512]{2,1,0:T(8,128)(2,1)S(1)} %pad_maximum_fusion.2), channel_id=1, source_target_pairs={{0,508},{4,8},{8,4},{12,16},{16,12},{20,24},{24,20},{28,32},{32,28... | collective-permute-start | bytes 786440 | tf_op jit(solution)/shard_map/ppermute | solution.py:277
  58.1 8.0 %collective-permute-done.6 = bf16[2,128,512]{2,1,0:T(8,128)(2,1)S(1)} collective-permute-done((bf16[2,128,512]{2,1,0:T(8,128)(2,1)S(1)}, bf16[2,128,512]{2,1,0:T(8,128)(2,1)S(1)}, u32[]{:S(2)}, u32[]{:S(2)}) %collective-permute-start.6) | collective-permute-done | bytes 262176 | tf_op jit(solution)/shard_map/ppermute | solution.py:277
  66.2 0.9 %maximum_select_fusion.1 = bf16[1,1,4,128,512]{4,3,2,1,0:T(8,128)(2,1)} fusion(bf16[1,1,1,128,512]{4,3,2,1,0:T(8,128)(2,1)S(1)} %get-tuple-element.46, bf16[1,1,1,128,512]{4,3,2,1,0:T(8,128)(2,1)S(1)} %get-tuple-element.42, bf16[1,1,2,128,512]{4,3,2,1,0:T(8,128)(2,1)S(1)} %bitcast.11, bf16[1,1,1,128,512]{4,3,2,1,0:T(8,128)(2,1)S(1)} %get-tuple-element.44, ...), kind=kLoop, calls=%fused_computation.1 | loop fusion | flops 1572864 | bytes 1310721 | tf_op jit(solution)/shard_map/jit(_where)/select_n | solution.py:282
  (10 shorter events, 0.2 us)
Async XLA Ops:
  0.0 1.6 %copy-start = (bf16[8,16,64,128]{3,2,1,0:T(8,128)(2,1)S(1)}, bf16[8,16,64,128]{3,2,1,0:T(8,128)(2,1)}, u32[]{:S(2)}) copy-start(bf16[8,16,64,128]{3,2,1,0:T(8,128)(2,1)} %vox.5) | copy-start | bytes 6291460
  1.6 0.7 %copy-start.2 = (s32[8,16]{1,0:T(8,128)S(1)}, s32[8,16]{1,0:T(8,128)}, u32[]{:S(2)}) copy-start(s32[8,16]{1,0:T(8,128)} %lo.5) | copy-start | bytes 1540
  2.3 0.7 %copy-start.4 = (s32[8,16]{1,0:T(8,128)S(1)}, s32[8,16]{1,0:T(8,128)}, u32[]{:S(2)}) copy-start(s32[8,16]{1,0:T(8,128)} %hi.5) | copy-start | bytes 1540
  3.0 10.1 %copy-start.9 = (s32[64,1,8]{0,2,1:T(8,128)S(1)}, s32[64,1,8]{0,2,1:T(8,128)}, u32[]{:S(2)}) copy-start(s32[64,1,8]{0,2,1:T(8,128)} %param.15) | copy-start | bytes 6148
  3.0 10.3 %copy-start.10 = (f32[64]{0:T(128)S(1)}, f32[64]{0:T(128)}, u32[]{:S(2)}) copy-start(f32[64]{0:T(128)} %param.12) | copy-start | bytes 772
  3.0 10.4 %copy-start.6 = (bf16[3,3,3,64,64]{4,3,2,1,0:T(8,128)(2,1)S(1)}, bf16[3,3,3,64,64]{4,3,2,1,0:T(8,128)(2,1)}, u32[]{:S(2)}) copy-start(bf16[3,3,3,64,64]{4,3,2,1,0:T(8,128)(2,1)} %cw.1) | copy-start | bytes 663556
  3.0 10.4 %copy-start.7 = (bf16[8,64,128]{2,1,0:T(8,128)(2,1)S(1)}, bf16[8,64,128]{2,1,0:T(8,128)(2,1)}, u32[]{:S(2)}) copy-start(bf16[8,64,128]{2,1,0:T(8,128)(2,1)} %dw.1) | copy-start | bytes 393220
  3.0 10.4 %copy-start.8 = (f32[128]{0:T(128)S(1)}, f32[128]{0:T(128)}, u32[]{:S(2)}) copy-start(f32[128]{0:T(128)} %param.14) | copy-start | bytes 1540
  3.9 10.3 %collective-permute-start = (bf16[8,64,128]{2,1,0:T(8,128)(2,1)S(1)}, bf16[8,64,128]{2,1,0:T(8,128)(2,1)S(1)}, u32[]{:S(2)}, u32[]{:S(2)}) collective-permute-start(bf16[8,64,128]{2,1,0:T(8,128)(2,1)S(1)} %get-tuple-element.23), channel_id=1, source_target_pairs={{0,1},{1,2},{2,3},{4,5},{5,6},{6,7},{8,9},{9,10},{10,11},{12,13},{... | collective-permute-start | bytes 393224 | tf_op jit(solution)/shard_map/ppermute | solution.py:251
  7.3 8.2 %collective-permute-start.1 = (bf16[8,64,128]{2,1,0:T(8,128)(2,1)S(1)}, bf16[8,64,128]{2,1,0:T(8,128)(2,1)S(1)}, u32[]{:S(2)}, u32[]{:S(2)}) collective-permute-start(bf16[8,64,128]{2,1,0:T(8,128)(2,1)S(1)} %get-tuple-element.24), channel_id=1, source_target_pairs={{1,0},{2,1},{3,2},{5,4},{6,5},{7,6},{9,8},{10,9},{11,10},{13,12},{... | collective-permute-start | bytes 393224 | tf_op jit(solution)/shard_map/ppermute | solution.py:252
  13.4 4.9 %copy-start.1 = (bf16[8,16,64,128]{3,2,1,0:T(8,128)(2,1)S(1)}, bf16[8,16,64,128]{3,2,1,0:T(8,128)(2,1)}, u32[]{:S(2)}) copy-start(bf16[8,16,64,128]{3,2,1,0:T(8,128)(2,1)} %vox.5) | copy-start | bytes 6291460
  13.4 4.9 %copy-start.3 = (s32[8,16]{1,0:T(8,128)S(1)}, s32[8,16]{1,0:T(8,128)}, u32[]{:S(2)}) copy-start(s32[8,16]{1,0:T(8,128)} %lo.5) | copy-start | bytes 1540
  13.4 4.9 %copy-start.5 = (s32[8,16]{1,0:T(8,128)S(1)}, s32[8,16]{1,0:T(8,128)}, u32[]{:S(2)}) copy-start(s32[8,16]{1,0:T(8,128)} %hi.5) | copy-start | bytes 1540
  15.6 9.5 %collective-permute-start.2 = (bf16[18,64,128]{2,1,0:T(8,128)(2,1)S(1)}, bf16[18,64,128]{2,1,0:T(8,128)(2,1)S(1)}, u32[]{:S(2)}, u32[]{:S(2)}) collective-permute-start(bf16[18,64,128]{2,1,0:T(8,128)(2,1)S(1)} %pad_maximum_fusion), channel_id=1, source_target_pairs={{0,4},{4,8},{8,12},{12,16},{16,20},{20,24},{24,28},{28,32},{32,36}... | collective-permute-start | bytes 884744 | tf_op jit(solution)/shard_map/ppermute | solution.py:258
  16.9 8.2 %collective-permute-start.3 = (bf16[18,64,128]{2,1,0:T(8,128)(2,1)S(1)}, bf16[18,64,128]{2,1,0:T(8,128)(2,1)S(1)}, u32[]{:S(2)}, u32[]{:S(2)}) collective-permute-start(bf16[18,64,128]{2,1,0:T(8,128)(2,1)S(1)} %pad_maximum_fusion.1), channel_id=1, source_target_pairs={{4,0},{8,4},{12,8},{16,12},{20,16},{24,20},{28,24},{32,28},{36,32}... | collective-permute-start | bytes 884744 | tf_op jit(solution)/shard_map/ppermute | solution.py:259
  32.1 4.7 %collective-permute-start.4 = (bf16[4,128,256]{2,1,0:T(8,128)(2,1)S(1)}, bf16[4,128,256]{2,1,0:T(8,128)(2,1)S(1)}, u32[]{:S(2)}, u32[]{:S(2)}) collective-permute-start(bf16[4,128,256]{2,1,0:T(8,128)(2,1)S(1)} %get-tuple-element.40), channel_id=1, source_target_pairs={{0,4},{4,0},{8,12},{12,8},{16,20},{20,16},{24,28},{28,24},{32,36},... | collective-permute-start | bytes 786440 | tf_op jit(solution)/shard_map/ppermute | solution.py:271
  37.0 18.1 %collective-permute-start.5 = (bf16[2,128,512]{2,1,0:T(8,128)(2,1)S(1)}, bf16[2,128,512]{2,1,0:T(8,128)(2,1)S(1)}, u32[]{:S(2)}, u32[]{:S(2)}) collective-permute-start(bf16[2,128,512]{2,1,0:T(8,128)(2,1)S(1)} %slice.49), channel_id=1, source_target_pairs={{0,504},{4,12},{8,0},{12,20},{16,8},{20,28},{24,16},{28,36},{32,24... | collective-permute-start | bytes 786440 | tf_op jit(solution)/shard_map/ppermute | solution.py:276
  55.2 11.0 %collective-permute-start.6 = (bf16[2,128,512]{2,1,0:T(8,128)(2,1)S(1)}, bf16[2,128,512]{2,1,0:T(8,128)(2,1)S(1)}, u32[]{:S(2)}, u32[]{:S(2)}) collective-permute-start(bf16[2,128,512]{2,1,0:T(8,128)(2,1)S(1)} %pad_maximum_fusion.2), channel_id=1, source_target_pairs={{0,508},{4,8},{8,4},{12,16},{16,12},{20,24},{24,20},{28,32},{32,28... | collective-permute-start | bytes 786440 | tf_op jit(solution)/shard_map/ppermute | solution.py:277

commit v3 on v2

--- a/solution.py
+++ b/solution.py
@@ -103,7 +103,7 @@
         scratch_shapes=[pltpu.SemaphoreType.DMA((4,))],
         compiler_params=small_vmem(4),
         name="faces",
-    )(lo, hi, vox)
+    )(*(pltpu.with_memory_space_constraint(a, pltpu.HBM) for a in (lo, hi, vox)))
 
 
 def scene_rows(starts, columns, lo, hi, pad, w, d, cb, db, sel, cells):
@@ -261,9 +261,8 @@
 
     column = me // 2
     owners = lax.dynamic_index_in_dim(coarse_owner[:, 0, :], column, 0, keepdims=False)
-    offset = (owners - 2 * column + 3) % blk_n - 3
-    place = jnp.where(offset <= 0, offset + 3, 4 - offset)
-    slots = jnp.where((offset <= 0) == (core == 0), place, place + 4)
+    offset = (owners - 2 * column + 3) % blk_n
+    slots = (offset + 4 * core) % 8
 
     keep, give = outer_rows(
         shell_lo, shell_hi, slots, voxels, ylo, yhi, xlo, xhi, inner, tables
@@ -273,16 +272,16 @@
     whole = jnp.where(
         even, jnp.concatenate([keep, got], axis=2), jnp.concatenate([got, keep], axis=2)
     )
-    near = lax.ppermute(whole[0:2], "blk", ring(blk_n, lambda i: i + 2 if i % 2 else i - 2))
-    far = lax.ppermute(
-        jnp.concatenate([near[0:1], whole[2:3]]),
-        "blk",
-        ring(blk_n, lambda i: i + 1 if i % 2 else i - 1),
-    )
+
+    def mine(a, b):
+        return jnp.where(even, whole[a], whole[b])
+
+    one = lax.ppermute(mine(2, 1), "blk", ring(blk_n, lambda i: i + 1 if i % 2 else i - 1))
+    two = lax.ppermute(mine(1, 2), "blk", ring(blk_n, lambda i: i + 2 if i % 2 else i - 2))
+    three = lax.ppermute(mine(0, 3), "blk", ring(blk_n, lambda i: i + 3 if i % 2 else i - 3))
+    stay = mine(3, 0)
     result = jnp.where(
-        even,
-        jnp.stack([far[0], far[1], whole[3], near[1]]),
-        jnp.stack([near[1], whole[3], far[1], far[0]]),
+        even, jnp.stack([three, one, stay, two]), jnp.stack([two, stay, one, three])
     )
     return result[None, None]
 

time: 67.4 us -> 63.4 us (0.941)
  the two profiles are of different devices: /device:TPU:2 before, /device:TPU:1 now
where the time goes in v3:
time: 63.4 us; the launch traced here: 63.1 us
  starting transfers between devices  32.7 us (52%)
  Pallas kernels  16.8 us (26%)
  waiting for transfers between devices  11.8 us (19%)
  other arithmetic  1.37 us (2%)
    ppermute x1, starting transfers between devices, local(): lax.ppermute(mine(2, 1), 'blk', ring(blk_n, lambda i: i + 1 if i % 2 else...  11.3 us
    pallas_call x1, Pallas kernels, outer_rows(): pl.pallas_call(outer_kernel, out_shape=(half, half), in_specs=[smem] * 3...  7.01 us
    pallas_call x1, Pallas kernels, inner_rows(): pl.pallas_call(inner_kernel, out_shape=jax.ShapeDtypeStruct((256, 512), F...  6.83 us
    ppermute x1, waiting for transfers between devices, local(): lax.ppermute(mine(1, 2), 'blk', ring(blk_n, lambda i: i + 2 if i % 2 else...  6.39 us
    ppermute x1, starting transfers between devices, local(): lax.ppermute(jnp.concatenate([ylo[7:8], x_last, yhi[7:8]]), 'blk', ahead)  5.19 us
    ppermute x1, starting transfers between devices, local(): ylo = lax.ppermute(y_last, 'grp', up)  3.94 us
    ppermute x1, starting transfers between devices, local(): lax.ppermute(mine(0, 3), 'blk', ring(blk_n, lambda i: i + 3 if i % 2 else...  3.83 us
    ppermute x1, starting transfers between devices, local(): lax.ppermute(jnp.concatenate([ylo[0:1], x_first, yhi[0:1]]), 'blk', behind)  3.35 us
  transfers between devices with their start and end apart: 8, of which 4 were waited for; matrix products, arithmetic and copies ran while one was open for 1% of the time, Pallas kernels for 12%

profile of v3, /device:TPU:1, one launch (start us, length us, event | category | flops | bytes accessed | tf_op | source)
XLA Modules:
  0.0 63.1 jit_solution(224572329034697930)
XLA Ops:
  0.0 0.0 copy-start.6
  0.0 0.0 copy-start.7
  0.0 0.0 copy-start.5
  0.0 0.0 copy-start.4
  0.0 0.0 copy-start.3
  0.0 2.2 %faces.1 = (bf16[8,64,128]{2,1,0:T(8,128)(2,1)S(1)}, bf16[8,64,128]{2,1,0:T(8,128)(2,1)S(1)}, bf16[16,64,128]{2,1,0:T(8,128)(2,1)S(1)}, bf16[16,64,128]{2,1,0:T(8,128)(2,1)S(1)}) custom-call(s32[8,16]{1,0:T(8,128)} %lo.5, s32[8,16]{1,0:T(8,128)} %hi.5, bf16[8,16,64,128]{3,2,1,0:T(8,128)(2,1)} %vox.5), custom_call_target="tpu_custom_call" | custom-call | tf_op jit(solution)/shard_map/faces/pallas_call | solution.py:98
  2.2 3.9 %collective-permute-start = (bf16[8,64,128]{2,1,0:T(8,128)(2,1)S(1)}, bf16[8,64,128]{2,1,0:T(8,128)(2,1)S(1)}, u32[]{:S(2)}, u32[]{:S(2)}) collective-permute-start(bf16[8,64,128]{2,1,0:T(8,128)(2,1)S(1)} %get-tuple-element.23), channel_id=1, source_target_pairs={{0,1},{1,2},{2,3},{4,5},{5,6},{6,7},{8,9},{9,10},{10,11},{12,13},{... | collective-permute-start | bytes 393224 | tf_op jit(solution)/shard_map/ppermute | solution.py:251
  6.2 1.3 %collective-permute-start.1 = (bf16[8,64,128]{2,1,0:T(8,128)(2,1)S(1)}, bf16[8,64,128]{2,1,0:T(8,128)(2,1)S(1)}, u32[]{:S(2)}, u32[]{:S(2)}) collective-permute-start(bf16[8,64,128]{2,1,0:T(8,128)(2,1)S(1)} %get-tuple-element.24), channel_id=1, source_target_pairs={{1,0},{2,1},{3,2},{5,4},{6,5},{7,6},{9,8},{10,9},{11,10},{13,12},{... | collective-permute-start | bytes 393224 | tf_op jit(solution)/shard_map/ppermute | solution.py:252
  7.5 0.0 copy-done.6
  7.5 0.2 add_reduce_fusion
  7.7 0.0 copy-done.7
  7.7 0.1 broadcast_in_dim_tile.3.cb
  7.8 0.0 copy-done.5
  7.8 0.0 copy-done.4
  7.8 0.0 copy-done.3
  7.8 0.0 copy-start
  7.8 0.0 copy-start.1
  7.8 0.0 copy-start.2
  7.8 0.8 %prep.1 = (bf16[384,768]{1,0:T(8,128)(2,1)S(1)}, bf16[256,256]{1,0:T(8,128)(2,1)S(1)}, f32[128,128]{1,0:T(8,128)S(1)}, f32[128,128]{1,0:T(8,128)S(1)}, bf16[1024,512]{1,0:T(8,128)(2,1)S(1)}) custom-call(bf16[3,3,3,64,64]{4,3,2,1,0:T(8,128)(2,1)S(1)} %copy-done.3, f32[1,128]{1,0:T(1,128)S(1)} %broadcast_in_dim_tile.3.cb, bf16[8,64,128]{2,1,0:T(8,128)(2,1)S(1)} %copy-done.4, ...), custom_call_target="tpu_custom_call" | custom-call | flops 1000000000 | bytes 4000000 | tf_op jit(solution)/shard_map/prep/pallas_call | solution.py:44
  8.6 0.0 collective-permute-done.ylo
  8.6 3.2 %collective-permute-done.1.yhi = bf16[8,64,128]{2,1,0:T(8,128)(2,1)S(1)} collective-permute-done((bf16[8,64,128]{2,1,0:T(8,128)(2,1)S(1)}, bf16[8,64,128]{2,1,0:T(8,128)(2,1)S(1)}, u32[]{:S(2)}, u32[]{:S(2)}) %collective-permute-start.1) | collective-permute-done | bytes 131104 | tf_op jit(solution)/shard_map/ppermute | solution.py:252
  11.9 5.2 %collective-permute-start.2 = (bf16[18,64,128]{2,1,0:T(8,128)(2,1)S(1)}, bf16[18,64,128]{2,1,0:T(8,128)(2,1)S(1)}, u32[]{:S(2)}, u32[]{:S(2)}) collective-permute-start(bf16[18,64,128]{2,1,0:T(8,128)(2,1)S(1)} %pad_maximum_fusion), channel_id=1, source_target_pairs={{0,4},{4,8},{8,12},{12,16},{16,20},{20,24},{24,28},{28,32},{32,36}... | collective-permute-start | bytes 884744 | tf_op jit(solution)/shard_map/ppermute | solution.py:258
  17.2 3.4 %collective-permute-start.3 = (bf16[18,64,128]{2,1,0:T(8,128)(2,1)S(1)}, bf16[18,64,128]{2,1,0:T(8,128)(2,1)S(1)}, u32[]{:S(2)}, u32[]{:S(2)}) collective-permute-start(bf16[18,64,128]{2,1,0:T(8,128)(2,1)S(1)} %pad_maximum_fusion.1), channel_id=1, source_target_pairs={{4,0},{8,4},{12,8},{16,12},{20,16},{24,20},{28,24},{32,28},{36,32}... | collective-permute-start | bytes 884744 | tf_op jit(solution)/shard_map/ppermute | solution.py:259
  20.5 0.0 copy-done
  20.5 0.0 copy-done.1
  20.6 0.0 copy-done.2
  20.6 6.8 %inner.1 = f32[256,512]{1,0:T(8,128)S(1)} custom-call(s32[8,16]{1,0:T(8,128)S(1)} %copy-done.1, s32[8,16]{1,0:T(8,128)S(1)} %copy-done.2, bf16[8,16,64,128]{3,2,1,0:T(8,128)(2,1)S(1)} %copy-done, bf16[8,64,128]{2,1,0:T(8,128)(2,1)S(1)} %collective-permute-done.ylo, bf16[8,64,128]{2,1,0:T(8,128)(2,1)S(1)} %collective-permute-done.1.yhi, ...), custom_call_target="tpu_custom_call" | custom-call | flops 5000000000 | bytes 4000000 | tf_op jit(solution)/shard_map/inner/pallas_call | solution.py:207
  27.4 0.0 collective-permute-done.2.xlo
  27.4 0.0 collective-permute-done.3.xhi
  27.4 7.0 %outer.1 = (bf16[4,128,256]{2,1,0:T(8,128)(2,1)S(1)}, bf16[4,128,256]{2,1,0:T(8,128)(2,1)S(1)}) custom-call(s32[8,16]{1,0:T(8,128)S(1)} %copy-done.1, s32[8,16]{1,0:T(8,128)S(1)} %copy-done.2, s32[8]{0:T(128)S(1)} %and_select_fusion.slots, bf16[8,16,64,128]{3,2,1,0:T(8,128)(2,1)S(1)} %copy-done, bf16[8,64,128]{2,1,0:T(8,128)(2,1)S(1)} %collective-permute-done.ylo, ...), custom_call_target="tpu_custom_call" | custom-call | tf_op jit(solution)/shard_map/outer/pallas_call | solution.py:223
  34.4 1.9 %collective-permute-start.4 = (bf16[4,128,256]{2,1,0:T(8,128)(2,1)S(1)}, bf16[4,128,256]{2,1,0:T(8,128)(2,1)S(1)}, u32[]{:S(2)}, u32[]{:S(2)}) collective-permute-start(bf16[4,128,256]{2,1,0:T(8,128)(2,1)S(1)} %get-tuple-element.40), channel_id=1, source_target_pairs={{0,4},{4,0},{8,12},{12,8},{16,20},{20,16},{24,28},{28,24},{32,36},... | collective-permute-start | bytes 786440 | tf_op jit(solution)/shard_map/ppermute | solution.py:270
  36.4 1.5 %collective-permute-done.4 = bf16[4,128,256]{2,1,0:T(8,128)(2,1)S(1)} collective-permute-done((bf16[4,128,256]{2,1,0:T(8,128)(2,1)S(1)}, bf16[4,128,256]{2,1,0:T(8,128)(2,1)S(1)}, u32[]{:S(2)}, u32[]{:S(2)}) %collective-permute-start.4) | collective-permute-done | bytes 262176 | tf_op jit(solution)/shard_map/ppermute | solution.py:270
  37.9 0.1 maximum_select_fusion
  38.0 3.8 %collective-permute-start.5 = (bf16[128,512]{1,0:T(8,128)(2,1)S(1)}, bf16[128,512]{1,0:T(8,128)(2,1)S(1)}, u32[]{:S(2)}, u32[]{:S(2)}) collective-permute-start(bf16[128,512]{1,0:T(8,128)(2,1)S(1)} %get-tuple-element.41), channel_id=1, source_target_pairs={{0,500},{4,16},{8,508},{12,24},{16,4},{20,32},{24,12},{28,40},{32,... | collective-permute-start | bytes 393224 | tf_op jit(solution)/shard_map/ppermute | solution.py:281
  41.9 11.3 %collective-permute-start.6 = (bf16[128,512]{1,0:T(8,128)(2,1)S(1)}, bf16[128,512]{1,0:T(8,128)(2,1)S(1)}, u32[]{:S(2)}, u32[]{:S(2)}) collective-permute-start(bf16[128,512]{1,0:T(8,128)(2,1)S(1)} %get-tuple-element.42), channel_id=1, source_target_pairs={{0,508},{4,8},{8,4},{12,16},{16,12},{20,24},{24,20},{28,32},{32,28... | collective-permute-start | bytes 393224 | tf_op jit(solution)/shard_map/ppermute | solution.py:279
  53.1 1.9 %collective-permute-start.7 = (bf16[128,512]{1,0:T(8,128)(2,1)S(1)}, bf16[128,512]{1,0:T(8,128)(2,1)S(1)}, u32[]{:S(2)}, u32[]{:S(2)}) collective-permute-start(bf16[128,512]{1,0:T(8,128)(2,1)S(1)} %get-tuple-element.44), channel_id=1, source_target_pairs={{0,504},{4,12},{8,0},{12,20},{16,8},{20,28},{24,16},{28,36},{32,24... | collective-permute-start | bytes 393224 | tf_op jit(solution)/shard_map/ppermute | solution.py:280
  55.1 0.0 collective-permute-done.5
  55.1 0.7 %collective-permute-done.6 = bf16[128,512]{1,0:T(8,128)(2,1)S(1)} collective-permute-done((bf16[128,512]{1,0:T(8,128)(2,1)S(1)}, bf16[128,512]{1,0:T(8,128)(2,1)S(1)}, u32[]{:S(2)}, u32[]{:S(2)}) %collective-permute-start.6) | collective-permute-done | bytes 131104 | tf_op jit(solution)/shard_map/ppermute | solution.py:279
  55.8 6.4 %collective-permute-done.7 = bf16[128,512]{1,0:T(8,128)(2,1)S(1)} collective-permute-done((bf16[128,512]{1,0:T(8,128)(2,1)S(1)}, bf16[128,512]{1,0:T(8,128)(2,1)S(1)}, u32[]{:S(2)}, u32[]{:S(2)}) %collective-permute-start.7) | collective-permute-done | bytes 131104 | tf_op jit(solution)/shard_map/ppermute | solution.py:280
  62.2 0.9 %maximum_select_fusion.1 = bf16[1,1,4,128,512]{4,3,2,1,0:T(8,128)(2,1)} fusion(bf16[1,1,1,128,512]{4,3,2,1,0:T(8,128)(2,1)S(1)} %bitcast.15, bf16[1,1,1,128,512]{4,3,2,1,0:T(8,128)(2,1)S(1)} %get-tuple-element.43, bf16[1,1,1,128,512]{4,3,2,1,0:T(8,128)(2,1)S(1)} %bitcast.14, bf16[1,1,1,128,512]{4,3,2,1,0:T(8,128)(2,1)S(1)} %bitcast.13, pred[]{:T(512)S(6)} %eq.8), kind=kLoop, calls=%fused_computation.1 | loop fusion | flops 1835008 | bytes 1048577 | tf_op jit(solution)/shard_map/jit(_where)/select_n | solution.py:283
  (6 shorter events, 0.2 us)
Async XLA Ops:
  0.0 7.5 %copy-start.6 = (s32[64,1,8]{0,2,1:T(8,128)S(1)}, s32[64,1,8]{0,2,1:T(8,128)}, u32[]{:S(2)}) copy-start(s32[64,1,8]{0,2,1:T(8,128)} %param.15) | copy-start | bytes 6148
  0.0 7.7 %copy-start.7 = (f32[64]{0:T(128)S(1)}, f32[64]{0:T(128)}, u32[]{:S(2)}) copy-start(f32[64]{0:T(128)} %param.12) | copy-start | bytes 772
  0.0 7.8 %copy-start.5 = (f32[128]{0:T(128)S(1)}, f32[128]{0:T(128)}, u32[]{:S(2)}) copy-start(f32[128]{0:T(128)} %param.14) | copy-start | bytes 1540
  0.0 7.8 %copy-start.4 = (bf16[8,64,128]{2,1,0:T(8,128)(2,1)S(1)}, bf16[8,64,128]{2,1,0:T(8,128)(2,1)}, u32[]{:S(2)}) copy-start(bf16[8,64,128]{2,1,0:T(8,128)(2,1)} %dw.1) | copy-start | bytes 393220
  0.0 7.8 %copy-start.3 = (bf16[3,3,3,64,64]{4,3,2,1,0:T(8,128)(2,1)S(1)}, bf16[3,3,3,64,64]{4,3,2,1,0:T(8,128)(2,1)}, u32[]{:S(2)}) copy-start(bf16[3,3,3,64,64]{4,3,2,1,0:T(8,128)(2,1)} %cw.1) | copy-start | bytes 663556
  2.2 6.4 %collective-permute-start = (bf16[8,64,128]{2,1,0:T(8,128)(2,1)S(1)}, bf16[8,64,128]{2,1,0:T(8,128)(2,1)S(1)}, u32[]{:S(2)}, u32[]{:S(2)}) collective-permute-start(bf16[8,64,128]{2,1,0:T(8,128)(2,1)S(1)} %get-tuple-element.23), channel_id=1, source_target_pairs={{0,1},{1,2},{2,3},{4,5},{5,6},{6,7},{8,9},{9,10},{10,11},{12,13},{... | collective-permute-start | bytes 393224 | tf_op jit(solution)/shard_map/ppermute | solution.py:251
  6.2 5.7 %collective-permute-start.1 = (bf16[8,64,128]{2,1,0:T(8,128)(2,1)S(1)}, bf16[8,64,128]{2,1,0:T(8,128)(2,1)S(1)}, u32[]{:S(2)}, u32[]{:S(2)}) collective-permute-start(bf16[8,64,128]{2,1,0:T(8,128)(2,1)S(1)} %get-tuple-element.24), channel_id=1, source_target_pairs={{1,0},{2,1},{3,2},{5,4},{6,5},{7,6},{9,8},{10,9},{11,10},{13,12},{... | collective-permute-start | bytes 393224 | tf_op jit(solution)/shard_map/ppermute | solution.py:252
  7.8 12.7 %copy-start = (bf16[8,16,64,128]{3,2,1,0:T(8,128)(2,1)S(1)}, bf16[8,16,64,128]{3,2,1,0:T(8,128)(2,1)}, u32[]{:S(2)}) copy-start(bf16[8,16,64,128]{3,2,1,0:T(8,128)(2,1)} %vox.5) | copy-start | bytes 6291460
  7.8 12.7 %copy-start.1 = (s32[8,16]{1,0:T(8,128)S(1)}, s32[8,16]{1,0:T(8,128)}, u32[]{:S(2)}) copy-start(s32[8,16]{1,0:T(8,128)} %lo.5) | copy-start | bytes 1540
  7.8 12.7 %copy-start.2 = (s32[8,16]{1,0:T(8,128)S(1)}, s32[8,16]{1,0:T(8,128)}, u32[]{:S(2)}) copy-start(s32[8,16]{1,0:T(8,128)} %hi.5) | copy-start | bytes 1540
  11.9 15.5 %collective-permute-start.2 = (bf16[18,64,128]{2,1,0:T(8,128)(2,1)S(1)}, bf16[18,64,128]{2,1,0:T(8,128)(2,1)S(1)}, u32[]{:S(2)}, u32[]{:S(2)}) collective-permute-start(bf16[18,64,128]{2,1,0:T(8,128)(2,1)S(1)} %pad_maximum_fusion), channel_id=1, source_target_pairs={{0,4},{4,8},{8,12},{12,16},{16,20},{20,24},{24,28},{28,32},{32,36}... | collective-permute-start | bytes 884744 | tf_op jit(solution)/shard_map/ppermute | solution.py:258
  17.2 10.2 %collective-permute-start.3 = (bf16[18,64,128]{2,1,0:T(8,128)(2,1)S(1)}, bf16[18,64,128]{2,1,0:T(8,128)(2,1)S(1)}, u32[]{:S(2)}, u32[]{:S(2)}) collective-permute-start(bf16[18,64,128]{2,1,0:T(8,128)(2,1)S(1)} %pad_maximum_fusion.1), channel_id=1, source_target_pairs={{4,0},{8,4},{12,8},{16,12},{20,16},{24,20},{28,24},{32,28},{36,32}... | collective-permute-start | bytes 884744 | tf_op jit(solution)/shard_map/ppermute | solution.py:259
  34.4 3.4 %collective-permute-start.4 = (bf16[4,128,256]{2,1,0:T(8,128)(2,1)S(1)}, bf16[4,128,256]{2,1,0:T(8,128)(2,1)S(1)}, u32[]{:S(2)}, u32[]{:S(2)}) collective-permute-start(bf16[4,128,256]{2,1,0:T(8,128)(2,1)S(1)} %get-tuple-element.40), channel_id=1, source_target_pairs={{0,4},{4,0},{8,12},{12,8},{16,20},{20,16},{24,28},{28,24},{32,36},... | collective-permute-start | bytes 786440 | tf_op jit(solution)/shard_map/ppermute | solution.py:270
  38.0 17.0 %collective-permute-start.5 = (bf16[128,512]{1,0:T(8,128)(2,1)S(1)}, bf16[128,512]{1,0:T(8,128)(2,1)S(1)}, u32[]{:S(2)}, u32[]{:S(2)}) collective-permute-start(bf16[128,512]{1,0:T(8,128)(2,1)S(1)} %get-tuple-element.41), channel_id=1, source_target_pairs={{0,500},{4,16},{8,508},{12,24},{16,4},{20,32},{24,12},{28,40},{32,... | collective-permute-start | bytes 393224 | tf_op jit(solution)/shard_map/ppermute | solution.py:281
  41.9 13.9 %collective-permute-start.6 = (bf16[128,512]{1,0:T(8,128)(2,1)S(1)}, bf16[128,512]{1,0:T(8,128)(2,1)S(1)}, u32[]{:S(2)}, u32[]{:S(2)}) collective-permute-start(bf16[128,512]{1,0:T(8,128)(2,1)S(1)} %get-tuple-element.42), channel_id=1, source_target_pairs={{0,508},{4,8},{8,4},{12,16},{16,12},{20,24},{24,20},{28,32},{32,28... | collective-permute-start | bytes 393224 | tf_op jit(solution)/shard_map/ppermute | solution.py:279
  53.1 9.0 %collective-permute-start.7 = (bf16[128,512]{1,0:T(8,128)(2,1)S(1)}, bf16[128,512]{1,0:T(8,128)(2,1)S(1)}, u32[]{:S(2)}, u32[]{:S(2)}) collective-permute-start(bf16[128,512]{1,0:T(8,128)(2,1)S(1)} %get-tuple-element.44), channel_id=1, source_target_pairs={{0,504},{4,12},{8,0},{12,20},{16,8},{20,28},{24,16},{28,36},{32,24... | collective-permute-start | bytes 393224 | tf_op jit(solution)/shard_map/ppermute | solution.py:280

commit v4 on v3

--- a/solution.py
+++ b/solution.py
@@ -4,6 +4,7 @@
 from jax.experimental import pallas as pl
 from jax.experimental.pallas import tpu as pltpu
 from jax.sharding import PartitionSpec as P
+
 
 BF = jnp.bfloat16
 F32 = jnp.float32
@@ -106,7 +107,7 @@
     )(*(pltpu.with_memory_space_constraint(a, pltpu.HBM) for a in (lo, hi, vox)))
 
 
-def scene_rows(starts, columns, lo, hi, pad, w, d, cb, db, sel, cells):
+def scene_rows(starts, lo, hi, pad, w, d, cb, db, sel, cells):
     lane8 = lax.broadcasted_iota(jnp.int32, (8, 128), 1)
     lane = lax.broadcasted_iota(jnp.int32, (128, 128), 1)
 
@@ -170,7 +171,7 @@
         for y in range(16):
             pad[r, y + 1] = masked_column(vox[r + 1, y], lo, hi, r + 1, y)
 
-    out[...] = scene_rows(((0, 2), (2, 4)), None, lo, hi, pad, w, d, cb, db, sel, cells)
+    out[...] = scene_rows(((0, 2), (2, 4)), lo, hi, pad, w, d, cb, db, sel, cells)
 
 
 def outer_kernel(
@@ -190,7 +191,7 @@
             pad[r + 1, y + 1] = masked_column(vox[r, y], lo, hi, r, y)
             pad[r + 4, y + 1] = masked_column(vox[r + 5, y], lo, hi, r + 5, y)
 
-    ends = scene_rows(((0, 0), (4, 6)), None, lo, hi, pad, w, d, cb, db, sel, cells)
+    ends = scene_rows(((0, 0), (4, 6)), lo, hi, pad, w, d, cb, db, sel, cells)
     rows = (ends[0:128], inner[0:128], inner[128:256], ends[128:256])
     for pair in range(2):
         for level in range(8):
@@ -262,6 +263,8 @@
     column = me // 2
     owners = lax.dynamic_index_in_dim(coarse_owner[:, 0, :], column, 0, keepdims=False)
     offset = (owners - 2 * column + 3) % blk_n
+    ends = (offset == 0) | (offset == 7)
+    offset = jnp.where(ends & (column == 0), 7 - offset, offset)
     slots = (offset + 4 * core) % 8
 
     keep, give = outer_rows(
@@ -276,10 +279,20 @@
     def mine(a, b):
         return jnp.where(even, whole[a], whole[b])
 
-    one = lax.ppermute(mine(2, 1), "blk", ring(blk_n, lambda i: i + 1 if i % 2 else i - 1))
-    two = lax.ppermute(mine(1, 2), "blk", ring(blk_n, lambda i: i + 2 if i % 2 else i - 2))
-    three = lax.ppermute(mine(0, 3), "blk", ring(blk_n, lambda i: i + 3 if i % 2 else i - 3))
-    stay = mine(3, 0)
+    p_one, p_two, p_three, stay = mine(2, 1), mine(1, 2), mine(0, 3), mine(3, 0)
+    odds = range(1, blk_n, 2)
+    evens = range(0, blk_n, 2)
+    three_pairs = [(i, (i + 3) % blk_n) for i in odds if i > 1]
+    three_pairs += [(i, i - 3) for i in evens if i >= 4] + [(0, 4)]
+    two_pairs = [(i, (i + 2) % blk_n) for i in odds] + [(i, i - 2) for i in evens if i >= 2]
+    one_pairs = ring(blk_n, lambda i: i + 1 if i % 2 else i - 1)
+    rest_pairs = [(0, blk_n - 2), (1, blk_n - 3), (2, blk_n - 1)]
+    three = lax.ppermute(p_three, "blk", three_pairs)
+    two = lax.ppermute(p_two, "blk", two_pairs)
+    one = lax.ppermute(p_one, "blk", one_pairs)
+    rest = lax.ppermute(jnp.where(me == 0, p_two, p_three), "blk", rest_pairs)
+    three = jnp.where((me == blk_n - 1) | (me == blk_n - 3), rest, three)
+    two = jnp.where(me == blk_n - 2, rest, two)
     result = jnp.where(
         even, jnp.stack([three, one, stay, two]), jnp.stack([two, stay, one, three])
     )

time: 63.4 us -> 63.1 us (level)
  the two profiles are of different devices: /device:TPU:1 before, /device:TPU:2 now
where the time goes in v4:
time: 63.1 us; the launch traced here: 62.8 us
  starting transfers between devices  38.7 us (61%)
  Pallas kernels  16.8 us (27%)
  waiting for transfers between devices  5.39 us (9%)
  other arithmetic  1.43 us (2%)
    ppermute x1, starting transfers between devices, local(): rest = lax.ppermute(jnp.where(me == 0, p_two, p_three), 'blk', rest_pairs)  12.5 us
    ppermute x1, starting transfers between devices, local(): one = lax.ppermute(p_one, 'blk', one_pairs)  7.63 us
    pallas_call x1, Pallas kernels, outer_rows(): pl.pallas_call(outer_kernel, out_shape=(half, half), in_specs=[smem] * 3...  7.01 us
    pallas_call x1, Pallas kernels, inner_rows(): pl.pallas_call(inner_kernel, out_shape=jax.ShapeDtypeStruct((256, 512), F...  6.82 us
    ppermute x1, starting transfers between devices, local(): yhi = lax.ppermute(y_first, 'grp', down)  5.67 us
    ppermute x1, starting transfers between devices, local(): ylo = lax.ppermute(y_last, 'grp', up)  3.4 us
    ppermute x1, starting transfers between devices, local(): lax.ppermute(jnp.concatenate([ylo[7:8], x_last, yhi[7:8]]), 'blk', ahead)  3.05 us
    ppermute x1, waiting for transfers between devices, local(): one = lax.ppermute(p_one, 'blk', one_pairs)  2.57 us
  transfers between devices with their start and end apart: 9, of which 3 were waited for; matrix products, arithmetic and copies ran while one was open for 1% of the time, Pallas kernels for 12%

profile of v4, /device:TPU:2, one launch (start us, length us, event | category | flops | bytes accessed | tf_op | source)
XLA Modules:
  0.0 62.8 jit_solution(9076542696504482364)
XLA Ops:
  0.0 0.0 copy-start.6
  0.0 0.0 copy-start.7
  0.0 0.0 copy-start.5
  0.0 0.0 copy-start.3
  0.0 0.0 copy-start.4
  0.0 2.2 %faces.1 = (bf16[8,64,128]{2,1,0:T(8,128)(2,1)S(1)}, bf16[8,64,128]{2,1,0:T(8,128)(2,1)S(1)}, bf16[16,64,128]{2,1,0:T(8,128)(2,1)S(1)}, bf16[16,64,128]{2,1,0:T(8,128)(2,1)S(1)}) custom-call(s32[8,16]{1,0:T(8,128)} %lo.5, s32[8,16]{1,0:T(8,128)} %hi.5, bf16[8,16,64,128]{3,2,1,0:T(8,128)(2,1)} %vox.5), custom_call_target="tpu_custom_call" | custom-call | tf_op jit(solution)/shard_map/faces/pallas_call | solution.py:99
  2.2 3.4 %collective-permute-start = (bf16[8,64,128]{2,1,0:T(8,128)(2,1)S(1)}, bf16[8,64,128]{2,1,0:T(8,128)(2,1)S(1)}, u32[]{:S(2)}, u32[]{:S(2)}) collective-permute-start(bf16[8,64,128]{2,1,0:T(8,128)(2,1)S(1)} %get-tuple-element.23), channel_id=1, source_target_pairs={{0,1},{1,2},{2,3},{4,5},{5,6},{6,7},{8,9},{9,10},{10,11},{12,13},{... | collective-permute-start | bytes 393224 | tf_op jit(solution)/shard_map/ppermute | solution.py:252
  5.6 5.7 %collective-permute-start.1 = (bf16[8,64,128]{2,1,0:T(8,128)(2,1)S(1)}, bf16[8,64,128]{2,1,0:T(8,128)(2,1)S(1)}, u32[]{:S(2)}, u32[]{:S(2)}) collective-permute-start(bf16[8,64,128]{2,1,0:T(8,128)(2,1)S(1)} %get-tuple-element.24), channel_id=1, source_target_pairs={{1,0},{2,1},{3,2},{5,4},{6,5},{7,6},{9,8},{10,9},{11,10},{13,12},{... | collective-permute-start | bytes 393224 | tf_op jit(solution)/shard_map/ppermute | solution.py:253
  11.3 0.0 copy-done.6
  11.3 0.2 add_reduce_fusion
  11.5 0.0 copy-done.7
  11.6 0.1 broadcast_in_dim_tile.3.cb
  11.6 0.0 copy-done.5
  11.6 0.0 copy-done.3
  11.7 0.0 copy-done.4
  11.7 0.0 copy-start
  11.7 0.0 copy-start.1
  11.7 0.0 copy-start.2
  11.7 0.8 %prep.1 = (bf16[384,768]{1,0:T(8,128)(2,1)S(1)}, bf16[256,256]{1,0:T(8,128)(2,1)S(1)}, f32[128,128]{1,0:T(8,128)S(1)}, f32[128,128]{1,0:T(8,128)S(1)}, bf16[1024,512]{1,0:T(8,128)(2,1)S(1)}) custom-call(bf16[3,3,3,64,64]{4,3,2,1,0:T(8,128)(2,1)S(1)} %copy-done.3, f32[1,128]{1,0:T(1,128)S(1)} %broadcast_in_dim_tile.3.cb, bf16[8,64,128]{2,1,0:T(8,128)(2,1)S(1)} %copy-done.4, ...), custom_call_target="tpu_custom_call" | custom-call | flops 1000000000 | bytes 4000000 | tf_op jit(solution)/shard_map/prep/pallas_call | solution.py:45
  12.5 0.0 collective-permute-done.ylo
  12.5 1.3 %collective-permute-done.1.yhi = bf16[8,64,128]{2,1,0:T(8,128)(2,1)S(1)} collective-permute-done((bf16[8,64,128]{2,1,0:T(8,128)(2,1)S(1)}, bf16[8,64,128]{2,1,0:T(8,128)(2,1)S(1)}, u32[]{:S(2)}, u32[]{:S(2)}) %collective-permute-start.1) | collective-permute-done | bytes 131104 | tf_op jit(solution)/shard_map/ppermute | solution.py:253
  13.8 1.3 %collective-permute-start.3 = (bf16[18,64,128]{2,1,0:T(8,128)(2,1)S(1)}, bf16[18,64,128]{2,1,0:T(8,128)(2,1)S(1)}, u32[]{:S(2)}, u32[]{:S(2)}) collective-permute-start(bf16[18,64,128]{2,1,0:T(8,128)(2,1)S(1)} %pad_maximum_fusion.1), channel_id=1, source_target_pairs={{4,0},{8,4},{12,8},{16,12},{20,16},{24,20},{28,24},{32,28},{36,32}... | collective-permute-start | bytes 884744 | tf_op jit(solution)/shard_map/ppermute | solution.py:260
  15.2 3.0 %collective-permute-start.2 = (bf16[18,64,128]{2,1,0:T(8,128)(2,1)S(1)}, bf16[18,64,128]{2,1,0:T(8,128)(2,1)S(1)}, u32[]{:S(2)}, u32[]{:S(2)}) collective-permute-start(bf16[18,64,128]{2,1,0:T(8,128)(2,1)S(1)} %pad_maximum_fusion), channel_id=1, source_target_pairs={{0,4},{4,8},{8,12},{12,16},{16,20},{20,24},{24,28},{28,32},{32,36}... | collective-permute-start | bytes 884744 | tf_op jit(solution)/shard_map/ppermute | solution.py:259
  18.3 0.0 copy-done
  18.3 0.0 copy-done.1
  18.3 0.0 copy-done.2
  18.3 6.8 %inner.1 = f32[256,512]{1,0:T(8,128)S(1)} custom-call(s32[8,16]{1,0:T(8,128)S(1)} %copy-done.1, s32[8,16]{1,0:T(8,128)S(1)} %copy-done.2, bf16[8,16,64,128]{3,2,1,0:T(8,128)(2,1)S(1)} %copy-done, bf16[8,64,128]{2,1,0:T(8,128)(2,1)S(1)} %collective-permute-done.ylo, bf16[8,64,128]{2,1,0:T(8,128)(2,1)S(1)} %collective-permute-done.1.yhi, ...), custom_call_target="tpu_custom_call" | custom-call | flops 5000000000 | bytes 4000000 | tf_op jit(solution)/shard_map/inner/pallas_call | solution.py:208
  25.1 0.0 collective-permute-done.3.xhi
  25.1 0.0 collective-permute-done.2.xlo
  25.1 7.0 %outer.1 = (bf16[4,128,256]{2,1,0:T(8,128)(2,1)S(1)}, bf16[4,128,256]{2,1,0:T(8,128)(2,1)S(1)}) custom-call(s32[8,16]{1,0:T(8,128)S(1)} %copy-done.1, s32[8,16]{1,0:T(8,128)S(1)} %copy-done.2, s32[8]{0:T(128)S(1)} %and_select_fusion.slots, bf16[8,16,64,128]{3,2,1,0:T(8,128)(2,1)S(1)} %copy-done, bf16[8,64,128]{2,1,0:T(8,128)(2,1)S(1)} %collective-permute-done.ylo, ...), custom_call_target="tpu_custom_call" | custom-call | tf_op jit(solution)/shard_map/outer/pallas_call | solution.py:224
  32.2 1.9 %collective-permute-start.4 = (bf16[4,128,256]{2,1,0:T(8,128)(2,1)S(1)}, bf16[4,128,256]{2,1,0:T(8,128)(2,1)S(1)}, u32[]{:S(2)}, u32[]{:S(2)}) collective-permute-start(bf16[4,128,256]{2,1,0:T(8,128)(2,1)S(1)} %get-tuple-element.40), channel_id=1, source_target_pairs={{0,4},{4,0},{8,12},{12,8},{16,20},{20,16},{24,28},{28,24},{32,36},... | collective-permute-start | bytes 786440 | tf_op jit(solution)/shard_map/ppermute | solution.py:273
  34.1 1.5 %collective-permute-done.4 = bf16[4,128,256]{2,1,0:T(8,128)(2,1)S(1)} collective-permute-done((bf16[4,128,256]{2,1,0:T(8,128)(2,1)S(1)}, bf16[4,128,256]{2,1,0:T(8,128)(2,1)S(1)}, u32[]{:S(2)}, u32[]{:S(2)}) %collective-permute-start.4) | collective-permute-done | bytes 262176 | tf_op jit(solution)/shard_map/ppermute | solution.py:273
  35.6 0.1 maximum_select_fusion
  35.8 12.5 %collective-permute-start.5 = (bf16[128,512]{1,0:T(8,128)(2,1)S(1)}, bf16[128,512]{1,0:T(8,128)(2,1)S(1)}, u32[]{:S(2)}, u32[]{:S(2)}) collective-permute-start(bf16[128,512]{1,0:T(8,128)(2,1)S(1)} %get-tuple-element.41), channel_id=1, source_target_pairs={{0,504},{4,500},{8,508},{1,505},{5,501},{9,509},{2,506},{6,502},{1... | collective-permute-start | bytes 393224 | tf_op jit(solution)/shard_map/ppermute | solution.py:293
  48.3 1.9 %collective-permute-start.6 = (bf16[128,512]{1,0:T(8,128)(2,1)S(1)}, bf16[128,512]{1,0:T(8,128)(2,1)S(1)}, u32[]{:S(2)}, u32[]{:S(2)}) collective-permute-start(bf16[128,512]{1,0:T(8,128)(2,1)S(1)} %get-tuple-element.42), channel_id=1, source_target_pairs={{12,24},{20,32},{28,40},{36,48},{44,56},{52,64},{60,72},{68,80},{7... | collective-permute-start | bytes 393224 | tf_op jit(solution)/shard_map/ppermute | solution.py:290
  50.2 1.3 %collective-permute-start.8 = (bf16[128,512]{1,0:T(8,128)(2,1)S(1)}, bf16[128,512]{1,0:T(8,128)(2,1)S(1)}, u32[]{:S(2)}, u32[]{:S(2)}) collective-permute-start(bf16[128,512]{1,0:T(8,128)(2,1)S(1)} %get-tuple-element.43), channel_id=1, source_target_pairs={{4,12},{12,20},{20,28},{28,36},{36,44},{44,52},{52,60},{60,68},{68... | collective-permute-start | bytes 393224 | tf_op jit(solution)/shard_map/ppermute | solution.py:291
  51.6 7.6 %collective-permute-start.7 = (bf16[128,512]{1,0:T(8,128)(2,1)S(1)}, bf16[128,512]{1,0:T(8,128)(2,1)S(1)}, u32[]{:S(2)}, u32[]{:S(2)}) collective-permute-start(bf16[128,512]{1,0:T(8,128)(2,1)S(1)} %get-tuple-element.44), channel_id=1, source_target_pairs={{0,508},{4,8},{8,4},{12,16},{16,12},{20,24},{24,20},{28,32},{32,28... | collective-permute-start | bytes 393224 | tf_op jit(solution)/shard_map/ppermute | solution.py:292
  59.2 0.0 collective-permute-done.5
  59.2 0.0 collective-permute-done.6
  59.2 0.0 collective-permute-done.8
  59.3 2.6 %collective-permute-done.7 = bf16[128,512]{1,0:T(8,128)(2,1)S(1)} collective-permute-done((bf16[128,512]{1,0:T(8,128)(2,1)S(1)}, bf16[128,512]{1,0:T(8,128)(2,1)S(1)}, u32[]{:S(2)}, u32[]{:S(2)}) %collective-permute-start.7) | collective-permute-done | bytes 131104 | tf_op jit(solution)/shard_map/ppermute | solution.py:292
  61.8 0.9 %maximum_select_fusion.1 = bf16[1,1,4,128,512]{4,3,2,1,0:T(8,128)(2,1)} fusion(bf16[1,1,1,128,512]{4,3,2,1,0:T(8,128)(2,1)S(1)} %get-tuple-element.47, bf16[1,1,1,128,512]{4,3,2,1,0:T(8,128)(2,1)S(1)} %get-tuple-element.45, bf16[1,1,1,128,512]{4,3,2,1,0:T(8,128)(2,1)S(1)} %bitcast.17, bf16[1,1,1,128,512]{4,3,2,1,0:T(8,128)(2,1)S(1)} %get-tuple-element.46, ...), kind=kLoop, calls=%fused_computation.1 | loop fusion | flops 1835008 | bytes 1048577 | tf_op jit(solution)/shard_map/jit(_where)/select_n | solution.py:296
  (8 shorter events, 0.2 us)
Async XLA Ops:
  0.0 11.3 %copy-start.6 = (s32[64,1,8]{0,2,1:T(8,128)S(1)}, s32[64,1,8]{0,2,1:T(8,128)}, u32[]{:S(2)}) copy-start(s32[64,1,8]{0,2,1:T(8,128)} %param.15) | copy-start | bytes 6148
  0.0 11.5 %copy-start.7 = (f32[64]{0:T(128)S(1)}, f32[64]{0:T(128)}, u32[]{:S(2)}) copy-start(f32[64]{0:T(128)} %param.12) | copy-start | bytes 772
  0.0 11.6 %copy-start.5 = (f32[128]{0:T(128)S(1)}, f32[128]{0:T(128)}, u32[]{:S(2)}) copy-start(f32[128]{0:T(128)} %param.14) | copy-start | bytes 1540
  0.0 11.6 %copy-start.3 = (bf16[3,3,3,64,64]{4,3,2,1,0:T(8,128)(2,1)S(1)}, bf16[3,3,3,64,64]{4,3,2,1,0:T(8,128)(2,1)}, u32[]{:S(2)}) copy-start(bf16[3,3,3,64,64]{4,3,2,1,0:T(8,128)(2,1)} %cw.1) | copy-start | bytes 663556
  0.0 11.6 %copy-start.4 = (bf16[8,64,128]{2,1,0:T(8,128)(2,1)S(1)}, bf16[8,64,128]{2,1,0:T(8,128)(2,1)}, u32[]{:S(2)}) copy-start(bf16[8,64,128]{2,1,0:T(8,128)(2,1)} %dw.1) | copy-start | bytes 393220
  2.2 10.3 %collective-permute-start = (bf16[8,64,128]{2,1,0:T(8,128)(2,1)S(1)}, bf16[8,64,128]{2,1,0:T(8,128)(2,1)S(1)}, u32[]{:S(2)}, u32[]{:S(2)}) collective-permute-start(bf16[8,64,128]{2,1,0:T(8,128)(2,1)S(1)} %get-tuple-element.23), channel_id=1, source_target_pairs={{0,1},{1,2},{2,3},{4,5},{5,6},{6,7},{8,9},{9,10},{10,11},{12,13},{... | collective-permute-start | bytes 393224 | tf_op jit(solution)/shard_map/ppermute | solution.py:252
  5.6 8.2 %collective-permute-start.1 = (bf16[8,64,128]{2,1,0:T(8,128)(2,1)S(1)}, bf16[8,64,128]{2,1,0:T(8,128)(2,1)S(1)}, u32[]{:S(2)}, u32[]{:S(2)}) collective-permute-start(bf16[8,64,128]{2,1,0:T(8,128)(2,1)S(1)} %get-tuple-element.24), channel_id=1, source_target_pairs={{1,0},{2,1},{3,2},{5,4},{6,5},{7,6},{9,8},{10,9},{11,10},{13,12},{... | collective-permute-start | bytes 393224 | tf_op jit(solution)/shard_map/ppermute | solution.py:253
  11.7 6.6 %copy-start = (bf16[8,16,64,128]{3,2,1,0:T(8,128)(2,1)S(1)}, bf16[8,16,64,128]{3,2,1,0:T(8,128)(2,1)}, u32[]{:S(2)}) copy-start(bf16[8,16,64,128]{3,2,1,0:T(8,128)(2,1)} %vox.5) | copy-start | bytes 6291460
  11.7 6.6 %copy-start.1 = (s32[8,16]{1,0:T(8,128)S(1)}, s32[8,16]{1,0:T(8,128)}, u32[]{:S(2)}) copy-start(s32[8,16]{1,0:T(8,128)} %lo.5) | copy-start | bytes 1540
  11.7 6.6 %copy-start.2 = (s32[8,16]{1,0:T(8,128)S(1)}, s32[8,16]{1,0:T(8,128)}, u32[]{:S(2)}) copy-start(s32[8,16]{1,0:T(8,128)} %hi.5) | copy-start | bytes 1540
  13.8 11.3 %collective-permute-start.3 = (bf16[18,64,128]{2,1,0:T(8,128)(2,1)S(1)}, bf16[18,64,128]{2,1,0:T(8,128)(2,1)S(1)}, u32[]{:S(2)}, u32[]{:S(2)}) collective-permute-start(bf16[18,64,128]{2,1,0:T(8,128)(2,1)S(1)} %pad_maximum_fusion.1), channel_id=1, source_target_pairs={{4,0},{8,4},{12,8},{16,12},{20,16},{24,20},{28,24},{32,28},{36,32}... | collective-permute-start | bytes 884744 | tf_op jit(solution)/shard_map/ppermute | solution.py:260
  15.2 9.9 %collective-permute-start.2 = (bf16[18,64,128]{2,1,0:T(8,128)(2,1)S(1)}, bf16[18,64,128]{2,1,0:T(8,128)(2,1)S(1)}, u32[]{:S(2)}, u32[]{:S(2)}) collective-permute-start(bf16[18,64,128]{2,1,0:T(8,128)(2,1)S(1)} %pad_maximum_fusion), channel_id=1, source_target_pairs={{0,4},{4,8},{8,12},{12,16},{16,20},{20,24},{24,28},{28,32},{32,36}... | collective-permute-start | bytes 884744 | tf_op jit(solution)/shard_map/ppermute | solution.py:259
  32.2 3.4 %collective-permute-start.4 = (bf16[4,128,256]{2,1,0:T(8,128)(2,1)S(1)}, bf16[4,128,256]{2,1,0:T(8,128)(2,1)S(1)}, u32[]{:S(2)}, u32[]{:S(2)}) collective-permute-start(bf16[4,128,256]{2,1,0:T(8,128)(2,1)S(1)} %get-tuple-element.40), channel_id=1, source_target_pairs={{0,4},{4,0},{8,12},{12,8},{16,20},{20,16},{24,28},{28,24},{32,36},... | collective-permute-start | bytes 786440 | tf_op jit(solution)/shard_map/ppermute | solution.py:273
  35.8 23.4 %collective-permute-start.5 = (bf16[128,512]{1,0:T(8,128)(2,1)S(1)}, bf16[128,512]{1,0:T(8,128)(2,1)S(1)}, u32[]{:S(2)}, u32[]{:S(2)}) collective-permute-start(bf16[128,512]{1,0:T(8,128)(2,1)S(1)} %get-tuple-element.41), channel_id=1, source_target_pairs={{0,504},{4,500},{8,508},{1,505},{5,501},{9,509},{2,506},{6,502},{1... | collective-permute-start | bytes 393224 | tf_op jit(solution)/shard_map/ppermute | solution.py:293
  48.3 10.9 %collective-permute-start.6 = (bf16[128,512]{1,0:T(8,128)(2,1)S(1)}, bf16[128,512]{1,0:T(8,128)(2,1)S(1)}, u32[]{:S(2)}, u32[]{:S(2)}) collective-permute-start(bf16[128,512]{1,0:T(8,128)(2,1)S(1)} %get-tuple-element.42), channel_id=1, source_target_pairs={{12,24},{20,32},{28,40},{36,48},{44,56},{52,64},{60,72},{68,80},{7... | collective-permute-start | bytes 393224 | tf_op jit(solution)/shard_map/ppermute | solution.py:290
  50.2 9.0 %collective-permute-start.8 = (bf16[128,512]{1,0:T(8,128)(2,1)S(1)}, bf16[128,512]{1,0:T(8,128)(2,1)S(1)}, u32[]{:S(2)}, u32[]{:S(2)}) collective-permute-start(bf16[128,512]{1,0:T(8,128)(2,1)S(1)} %get-tuple-element.43), channel_id=1, source_target_pairs={{4,12},{12,20},{20,28},{28,36},{36,44},{44,52},{52,60},{60,68},{68... | collective-permute-start | bytes 393224 | tf_op jit(solution)/shard_map/ppermute | solution.py:291
  51.6 10.3 %collective-permute-start.7 = (bf16[128,512]{1,0:T(8,128)(2,1)S(1)}, bf16[128,512]{1,0:T(8,128)(2,1)S(1)}, u32[]{:S(2)}, u32[]{:S(2)}) collective-permute-start(bf16[128,512]{1,0:T(8,128)(2,1)S(1)} %get-tuple-element.44), channel_id=1, source_target_pairs={{0,508},{4,8},{8,4},{12,16},{16,12},{20,24},{24,20},{28,32},{32,28... | collective-permute-start | bytes 393224 | tf_op jit(solution)/shard_map/ppermute | solution.py:292

commit v5 on v3

--- a/solution.py
+++ b/solution.py
@@ -4,6 +4,7 @@
 from jax.experimental import pallas as pl
 from jax.experimental.pallas import tpu as pltpu
 from jax.sharding import PartitionSpec as P
+
 
 BF = jnp.bfloat16
 F32 = jnp.float32
@@ -106,7 +107,7 @@
     )(*(pltpu.with_memory_space_constraint(a, pltpu.HBM) for a in (lo, hi, vox)))
 
 
-def scene_rows(starts, columns, lo, hi, pad, w, d, cb, db, sel, cells):
+def scene_rows(starts, lo, hi, pad, w, d, cb, db, sel, cells):
     lane8 = lax.broadcasted_iota(jnp.int32, (8, 128), 1)
     lane = lax.broadcasted_iota(jnp.int32, (128, 128), 1)
 
@@ -139,8 +140,7 @@
 
     (row0, x0), (row1, x1) = starts
 
-    @pl.loop(0, 2)
-    def _(t):
+    for t in range(2):
         row = row0 + t * (row1 - row0)
         x = x0 + t * (x1 - x0)
         for ypp in range(4):
@@ -153,7 +153,7 @@
                 part = down[:, e * 128 : e * 128 + 128]
                 total = part[0:128] + pltpu.roll(part[128:256], 127, 1) + db[...]
                 total = total.reshape(16, 8, 128) * coarse_mask(x, q)[None]
-                cells[pl.ds(t * 128, 128), q * 128 : q * 128 + 128] = total.reshape(
+                cells[t * 128 : t * 128 + 128, q * 128 : q * 128 + 128] = total.reshape(
                     128, 128
                 ).astype(BF)
 
@@ -170,7 +170,7 @@
         for y in range(16):
             pad[r, y + 1] = masked_column(vox[r + 1, y], lo, hi, r + 1, y)
 
-    out[...] = scene_rows(((0, 2), (2, 4)), None, lo, hi, pad, w, d, cb, db, sel, cells)
+    out[...] = scene_rows(((0, 2), (2, 4)), lo, hi, pad, w, d, cb, db, sel, cells)
 
 
 def outer_kernel(
@@ -190,7 +190,7 @@
             pad[r + 1, y + 1] = masked_column(vox[r, y], lo, hi, r, y)
             pad[r + 4, y + 1] = masked_column(vox[r + 5, y], lo, hi, r + 5, y)
 
-    ends = scene_rows(((0, 0), (4, 6)), None, lo, hi, pad, w, d, cb, db, sel, cells)
+    ends = scene_rows(((0, 0), (4, 6)), lo, hi, pad, w, d, cb, db, sel, cells)
     rows = (ends[0:128], inner[0:128], inner[128:256], ends[128:256])
     for pair in range(2):
         for level in range(8):
@@ -276,9 +276,12 @@
     def mine(a, b):
         return jnp.where(even, whole[a], whole[b])
 
-    one = lax.ppermute(mine(2, 1), "blk", ring(blk_n, lambda i: i + 1 if i % 2 else i - 1))
-    two = lax.ppermute(mine(1, 2), "blk", ring(blk_n, lambda i: i + 2 if i % 2 else i - 2))
-    three = lax.ppermute(mine(0, 3), "blk", ring(blk_n, lambda i: i + 3 if i % 2 else i - 3))
+    pairs = ring(blk_n, lambda i: i + 1 if i % 2 else i - 1)
+    one = lax.ppermute(mine(2, 1), "blk", pairs)
+    pairs = ring(blk_n, lambda i: i + 3 if i % 2 else i - 3)
+    three = lax.ppermute(mine(0, 3), "blk", pairs)
+    pairs = ring(blk_n, lambda i: i + 2 if i % 2 else i - 2)
+    two = lax.ppermute(mine(1, 2), "blk", pairs)
     stay = mine(3, 0)
     result = jnp.where(
         even, jnp.stack([three, one, stay, two]), jnp.stack([two, stay, one, three])

time: 63.4 us -> 62.5 us (0.986)
  Pallas kernels: 16.8 us -> 15.9 us
where the time goes in v5:
time: 62.5 us; the launch traced here: 62.2 us
  starting transfers between devices  32.7 us (52%)
  Pallas kernels  15.9 us (25%)
  waiting for transfers between devices  11.8 us (19%)
  other arithmetic  1.37 us (2%)
    ppermute x1, starting transfers between devices, local(): one = lax.ppermute(mine(2, 1), 'blk', pairs)  11.3 us
    pallas_call x1, Pallas kernels, outer_rows(): pl.pallas_call(outer_kernel, out_shape=(half, half), in_specs=[smem] * 3...  6.54 us
    pallas_call x1, Pallas kernels, inner_rows(): pl.pallas_call(inner_kernel, out_shape=jax.ShapeDtypeStruct((256, 512), F...  6.42 us
    ppermute x1, waiting for transfers between devices, local(): two = lax.ppermute(mine(1, 2), 'blk', pairs)  6.39 us
    ppermute x1, starting transfers between devices, local(): lax.ppermute(jnp.concatenate([ylo[7:8], x_last, yhi[7:8]]), 'blk', ahead)  5.19 us
    ppermute x1, starting transfers between devices, local(): ylo = lax.ppermute(y_last, 'grp', up)  3.94 us
    ppermute x1, starting transfers between devices, local(): three = lax.ppermute(mine(0, 3), 'blk', pairs)  3.83 us
    ppermute x1, starting transfers between devices, local(): lax.ppermute(jnp.concatenate([ylo[0:1], x_first, yhi[0:1]]), 'blk', behind)  3.35 us
  transfers between devices with their start and end apart: 8, of which 4 were waited for; matrix products, arithmetic and copies ran while one was open for 1% of the time, Pallas kernels for 12%

profile of v5, /device:TPU:1, one launch (start us, length us, event | category | flops | bytes accessed | tf_op | source)
XLA Modules:
  0.0 62.2 jit_solution(8474130765767470823)
XLA Ops:
  0.0 0.0 copy-start.6
  0.0 0.0 copy-start.7
  0.0 0.0 copy-start.5
  0.0 0.0 copy-start.4
  0.0 0.0 copy-start.3
  0.0 2.2 %faces.1 = (bf16[8,64,128]{2,1,0:T(8,128)(2,1)S(1)}, bf16[8,64,128]{2,1,0:T(8,128)(2,1)S(1)}, bf16[16,64,128]{2,1,0:T(8,128)(2,1)S(1)}, bf16[16,64,128]{2,1,0:T(8,128)(2,1)S(1)}) custom-call(s32[8,16]{1,0:T(8,128)} %lo.5, s32[8,16]{1,0:T(8,128)} %hi.5, bf16[8,16,64,128]{3,2,1,0:T(8,128)(2,1)} %vox.5), custom_call_target="tpu_custom_call" | custom-call | tf_op jit(solution)/shard_map/faces/pallas_call | solution.py:99
  2.2 3.9 %collective-permute-start = (bf16[8,64,128]{2,1,0:T(8,128)(2,1)S(1)}, bf16[8,64,128]{2,1,0:T(8,128)(2,1)S(1)}, u32[]{:S(2)}, u32[]{:S(2)}) collective-permute-start(bf16[8,64,128]{2,1,0:T(8,128)(2,1)S(1)} %get-tuple-element.23), channel_id=1, source_target_pairs={{0,1},{1,2},{2,3},{4,5},{5,6},{6,7},{8,9},{9,10},{10,11},{12,13},{... | collective-permute-start | bytes 393224 | tf_op jit(solution)/shard_map/ppermute | solution.py:251
  6.2 1.3 %collective-permute-start.1 = (bf16[8,64,128]{2,1,0:T(8,128)(2,1)S(1)}, bf16[8,64,128]{2,1,0:T(8,128)(2,1)S(1)}, u32[]{:S(2)}, u32[]{:S(2)}) collective-permute-start(bf16[8,64,128]{2,1,0:T(8,128)(2,1)S(1)} %get-tuple-element.24), channel_id=1, source_target_pairs={{1,0},{2,1},{3,2},{5,4},{6,5},{7,6},{9,8},{10,9},{11,10},{13,12},{... | collective-permute-start | bytes 393224 | tf_op jit(solution)/shard_map/ppermute | solution.py:252
  7.5 0.0 copy-done.6
  7.5 0.2 add_reduce_fusion
  7.7 0.0 copy-done.7
  7.7 0.1 broadcast_in_dim_tile.3.cb
  7.8 0.0 copy-done.5
  7.8 0.0 copy-done.4
  7.8 0.0 copy-done.3
  7.8 0.0 copy-start
  7.8 0.0 copy-start.1
  7.8 0.0 copy-start.2
  7.8 0.8 %prep.1 = (bf16[384,768]{1,0:T(8,128)(2,1)S(1)}, bf16[256,256]{1,0:T(8,128)(2,1)S(1)}, f32[128,128]{1,0:T(8,128)S(1)}, f32[128,128]{1,0:T(8,128)S(1)}, bf16[1024,512]{1,0:T(8,128)(2,1)S(1)}) custom-call(bf16[3,3,3,64,64]{4,3,2,1,0:T(8,128)(2,1)S(1)} %copy-done.3, f32[1,128]{1,0:T(1,128)S(1)} %broadcast_in_dim_tile.3.cb, bf16[8,64,128]{2,1,0:T(8,128)(2,1)S(1)} %copy-done.4, ...), custom_call_target="tpu_custom_call" | custom-call | flops 1000000000 | bytes 4000000 | tf_op jit(solution)/shard_map/prep/pallas_call | solution.py:45
  8.6 0.0 collective-permute-done.ylo
  8.6 3.2 %collective-permute-done.1.yhi = bf16[8,64,128]{2,1,0:T(8,128)(2,1)S(1)} collective-permute-done((bf16[8,64,128]{2,1,0:T(8,128)(2,1)S(1)}, bf16[8,64,128]{2,1,0:T(8,128)(2,1)S(1)}, u32[]{:S(2)}, u32[]{:S(2)}) %collective-permute-start.1) | collective-permute-done | bytes 131104 | tf_op jit(solution)/shard_map/ppermute | solution.py:252
  11.9 5.2 %collective-permute-start.2 = (bf16[18,64,128]{2,1,0:T(8,128)(2,1)S(1)}, bf16[18,64,128]{2,1,0:T(8,128)(2,1)S(1)}, u32[]{:S(2)}, u32[]{:S(2)}) collective-permute-start(bf16[18,64,128]{2,1,0:T(8,128)(2,1)S(1)} %pad_maximum_fusion), channel_id=1, source_target_pairs={{0,4},{4,8},{8,12},{12,16},{16,20},{20,24},{24,28},{28,32},{32,36}... | collective-permute-start | bytes 884744 | tf_op jit(solution)/shard_map/ppermute | solution.py:258
  17.2 3.4 %collective-permute-start.3 = (bf16[18,64,128]{2,1,0:T(8,128)(2,1)S(1)}, bf16[18,64,128]{2,1,0:T(8,128)(2,1)S(1)}, u32[]{:S(2)}, u32[]{:S(2)}) collective-permute-start(bf16[18,64,128]{2,1,0:T(8,128)(2,1)S(1)} %pad_maximum_fusion.1), channel_id=1, source_target_pairs={{4,0},{8,4},{12,8},{16,12},{20,16},{24,20},{28,24},{32,28},{36,32}... | collective-permute-start | bytes 884744 | tf_op jit(solution)/shard_map/ppermute | solution.py:259
  20.5 0.0 copy-done
  20.5 0.0 copy-done.1
  20.6 0.0 copy-done.2
  20.6 6.4 %inner.1 = f32[256,512]{1,0:T(8,128)S(1)} custom-call(s32[8,16]{1,0:T(8,128)S(1)} %copy-done.1, s32[8,16]{1,0:T(8,128)S(1)} %copy-done.2, bf16[8,16,64,128]{3,2,1,0:T(8,128)(2,1)S(1)} %copy-done, bf16[8,64,128]{2,1,0:T(8,128)(2,1)S(1)} %collective-permute-done.ylo, bf16[8,64,128]{2,1,0:T(8,128)(2,1)S(1)} %collective-permute-done.1.yhi, ...), custom_call_target="tpu_custom_call" | custom-call | flops 5000000000 | bytes 4000000 | tf_op jit(solution)/shard_map/inner/pallas_call | solution.py:207
  27.0 0.0 collective-permute-done.2.xlo
  27.0 0.0 collective-permute-done.3.xhi
  27.0 6.5 %outer.1 = (bf16[4,128,256]{2,1,0:T(8,128)(2,1)S(1)}, bf16[4,128,256]{2,1,0:T(8,128)(2,1)S(1)}) custom-call(s32[8,16]{1,0:T(8,128)S(1)} %copy-done.1, s32[8,16]{1,0:T(8,128)S(1)} %copy-done.2, s32[8]{0:T(128)S(1)} %and_select_fusion.slots, bf16[8,16,64,128]{3,2,1,0:T(8,128)(2,1)S(1)} %copy-done, bf16[8,64,128]{2,1,0:T(8,128)(2,1)S(1)} %collective-permute-done.ylo, ...), custom_call_target="tpu_custom_call" | custom-call | tf_op jit(solution)/shard_map/outer/pallas_call | solution.py:223
  33.6 1.9 %collective-permute-start.4 = (bf16[4,128,256]{2,1,0:T(8,128)(2,1)S(1)}, bf16[4,128,256]{2,1,0:T(8,128)(2,1)S(1)}, u32[]{:S(2)}, u32[]{:S(2)}) collective-permute-start(bf16[4,128,256]{2,1,0:T(8,128)(2,1)S(1)} %get-tuple-element.40), channel_id=1, source_target_pairs={{0,4},{4,0},{8,12},{12,8},{16,20},{20,16},{24,28},{28,24},{32,36},... | collective-permute-start | bytes 786440 | tf_op jit(solution)/shard_map/ppermute | solution.py:270
  35.5 1.5 %collective-permute-done.4 = bf16[4,128,256]{2,1,0:T(8,128)(2,1)S(1)} collective-permute-done((bf16[4,128,256]{2,1,0:T(8,128)(2,1)S(1)}, bf16[4,128,256]{2,1,0:T(8,128)(2,1)S(1)}, u32[]{:S(2)}, u32[]{:S(2)}) %collective-permute-start.4) | collective-permute-done | bytes 262176 | tf_op jit(solution)/shard_map/ppermute | solution.py:270
  37.0 0.1 maximum_select_fusion
  37.2 3.8 %collective-permute-start.5 = (bf16[128,512]{1,0:T(8,128)(2,1)S(1)}, bf16[128,512]{1,0:T(8,128)(2,1)S(1)}, u32[]{:S(2)}, u32[]{:S(2)}) collective-permute-start(bf16[128,512]{1,0:T(8,128)(2,1)S(1)} %get-tuple-element.41), channel_id=1, source_target_pairs={{0,500},{4,16},{8,508},{12,24},{16,4},{20,32},{24,12},{28,40},{32,... | collective-permute-start | bytes 393224 | tf_op jit(solution)/shard_map/ppermute | solution.py:282
  41.0 11.3 %collective-permute-start.6 = (bf16[128,512]{1,0:T(8,128)(2,1)S(1)}, bf16[128,512]{1,0:T(8,128)(2,1)S(1)}, u32[]{:S(2)}, u32[]{:S(2)}) collective-permute-start(bf16[128,512]{1,0:T(8,128)(2,1)S(1)} %get-tuple-element.42), channel_id=1, source_target_pairs={{0,508},{4,8},{8,4},{12,16},{16,12},{20,24},{24,20},{28,32},{32,28... | collective-permute-start | bytes 393224 | tf_op jit(solution)/shard_map/ppermute | solution.py:280
  52.3 1.9 %collective-permute-start.7 = (bf16[128,512]{1,0:T(8,128)(2,1)S(1)}, bf16[128,512]{1,0:T(8,128)(2,1)S(1)}, u32[]{:S(2)}, u32[]{:S(2)}) collective-permute-start(bf16[128,512]{1,0:T(8,128)(2,1)S(1)} %get-tuple-element.44), channel_id=1, source_target_pairs={{0,504},{4,12},{8,0},{12,20},{16,8},{20,28},{24,16},{28,36},{32,24... | collective-permute-start | bytes 393224 | tf_op jit(solution)/shard_map/ppermute | solution.py:284
  54.2 0.0 collective-permute-done.5
  54.2 0.7 %collective-permute-done.6 = bf16[128,512]{1,0:T(8,128)(2,1)S(1)} collective-permute-done((bf16[128,512]{1,0:T(8,128)(2,1)S(1)}, bf16[128,512]{1,0:T(8,128)(2,1)S(1)}, u32[]{:S(2)}, u32[]{:S(2)}) %collective-permute-start.6) | collective-permute-done | bytes 131104 | tf_op jit(solution)/shard_map/ppermute | solution.py:280
  54.9 6.4 %collective-permute-done.7 = bf16[128,512]{1,0:T(8,128)(2,1)S(1)} collective-permute-done((bf16[128,512]{1,0:T(8,128)(2,1)S(1)}, bf16[128,512]{1,0:T(8,128)(2,1)S(1)}, u32[]{:S(2)}, u32[]{:S(2)}) %collective-permute-start.7) | collective-permute-done | bytes 131104 | tf_op jit(solution)/shard_map/ppermute | solution.py:284
  61.3 0.9 %maximum_select_fusion.1 = bf16[1,1,4,128,512]{4,3,2,1,0:T(8,128)(2,1)} fusion(bf16[1,1,1,128,512]{4,3,2,1,0:T(8,128)(2,1)S(1)} %bitcast.15, bf16[1,1,1,128,512]{4,3,2,1,0:T(8,128)(2,1)S(1)} %get-tuple-element.43, bf16[1,1,1,128,512]{4,3,2,1,0:T(8,128)(2,1)S(1)} %bitcast.14, bf16[1,1,1,128,512]{4,3,2,1,0:T(8,128)(2,1)S(1)} %bitcast.13, pred[]{:T(512)S(6)} %eq.8), kind=kLoop, calls=%fused_computation.1 | loop fusion | flops 1835008 | bytes 1048577 | tf_op jit(solution)/shard_map/jit(_where)/select_n | solution.py:286
  (6 shorter events, 0.2 us)
Async XLA Ops:
  0.0 7.5 %copy-start.6 = (s32[64,1,8]{0,2,1:T(8,128)S(1)}, s32[64,1,8]{0,2,1:T(8,128)}, u32[]{:S(2)}) copy-start(s32[64,1,8]{0,2,1:T(8,128)} %param.15) | copy-start | bytes 6148
  0.0 7.7 %copy-start.7 = (f32[64]{0:T(128)S(1)}, f32[64]{0:T(128)}, u32[]{:S(2)}) copy-start(f32[64]{0:T(128)} %param.12) | copy-start | bytes 772
  0.0 7.8 %copy-start.5 = (f32[128]{0:T(128)S(1)}, f32[128]{0:T(128)}, u32[]{:S(2)}) copy-start(f32[128]{0:T(128)} %param.14) | copy-start | bytes 1540
  0.0 7.8 %copy-start.4 = (bf16[8,64,128]{2,1,0:T(8,128)(2,1)S(1)}, bf16[8,64,128]{2,1,0:T(8,128)(2,1)}, u32[]{:S(2)}) copy-start(bf16[8,64,128]{2,1,0:T(8,128)(2,1)} %dw.1) | copy-start | bytes 393220
  0.0 7.8 %copy-start.3 = (bf16[3,3,3,64,64]{4,3,2,1,0:T(8,128)(2,1)S(1)}, bf16[3,3,3,64,64]{4,3,2,1,0:T(8,128)(2,1)}, u32[]{:S(2)}) copy-start(bf16[3,3,3,64,64]{4,3,2,1,0:T(8,128)(2,1)} %cw.1) | copy-start | bytes 663556
  2.2 6.4 %collective-permute-start = (bf16[8,64,128]{2,1,0:T(8,128)(2,1)S(1)}, bf16[8,64,128]{2,1,0:T(8,128)(2,1)S(1)}, u32[]{:S(2)}, u32[]{:S(2)}) collective-permute-start(bf16[8,64,128]{2,1,0:T(8,128)(2,1)S(1)} %get-tuple-element.23), channel_id=1, source_target_pairs={{0,1},{1,2},{2,3},{4,5},{5,6},{6,7},{8,9},{9,10},{10,11},{12,13},{... | collective-permute-start | bytes 393224 | tf_op jit(solution)/shard_map/ppermute | solution.py:251
  6.2 5.7 %collective-permute-start.1 = (bf16[8,64,128]{2,1,0:T(8,128)(2,1)S(1)}, bf16[8,64,128]{2,1,0:T(8,128)(2,1)S(1)}, u32[]{:S(2)}, u32[]{:S(2)}) collective-permute-start(bf16[8,64,128]{2,1,0:T(8,128)(2,1)S(1)} %get-tuple-element.24), channel_id=1, source_target_pairs={{1,0},{2,1},{3,2},{5,4},{6,5},{7,6},{9,8},{10,9},{11,10},{13,12},{... | collective-permute-start | bytes 393224 | tf_op jit(solution)/shard_map/ppermute | solution.py:252
  7.8 12.7 %copy-start = (bf16[8,16,64,128]{3,2,1,0:T(8,128)(2,1)S(1)}, bf16[8,16,64,128]{3,2,1,0:T(8,128)(2,1)}, u32[]{:S(2)}) copy-start(bf16[8,16,64,128]{3,2,1,0:T(8,128)(2,1)} %vox.5) | copy-start | bytes 6291460
  7.8 12.7 %copy-start.1 = (s32[8,16]{1,0:T(8,128)S(1)}, s32[8,16]{1,0:T(8,128)}, u32[]{:S(2)}) copy-start(s32[8,16]{1,0:T(8,128)} %lo.5) | copy-start | bytes 1540
  7.8 12.7 %copy-start.2 = (s32[8,16]{1,0:T(8,128)S(1)}, s32[8,16]{1,0:T(8,128)}, u32[]{:S(2)}) copy-start(s32[8,16]{1,0:T(8,128)} %hi.5) | copy-start | bytes 1540
  11.9 15.1 %collective-permute-start.2 = (bf16[18,64,128]{2,1,0:T(8,128)(2,1)S(1)}, bf16[18,64,128]{2,1,0:T(8,128)(2,1)S(1)}, u32[]{:S(2)}, u32[]{:S(2)}) collective-permute-start(bf16[18,64,128]{2,1,0:T(8,128)(2,1)S(1)} %pad_maximum_fusion), channel_id=1, source_target_pairs={{0,4},{4,8},{8,12},{12,16},{16,20},{20,24},{24,28},{28,32},{32,36}... | collective-permute-start | bytes 884744 | tf_op jit(solution)/shard_map/ppermute | solution.py:258
  17.2 9.8 %collective-permute-start.3 = (bf16[18,64,128]{2,1,0:T(8,128)(2,1)S(1)}, bf16[18,64,128]{2,1,0:T(8,128)(2,1)S(1)}, u32[]{:S(2)}, u32[]{:S(2)}) collective-permute-start(bf16[18,64,128]{2,1,0:T(8,128)(2,1)S(1)} %pad_maximum_fusion.1), channel_id=1, source_target_pairs={{4,0},{8,4},{12,8},{16,12},{20,16},{24,20},{28,24},{32,28},{36,32}... | collective-permute-start | bytes 884744 | tf_op jit(solution)/shard_map/ppermute | solution.py:259
  33.6 3.4 %collective-permute-start.4 = (bf16[4,128,256]{2,1,0:T(8,128)(2,1)S(1)}, bf16[4,128,256]{2,1,0:T(8,128)(2,1)S(1)}, u32[]{:S(2)}, u32[]{:S(2)}) collective-permute-start(bf16[4,128,256]{2,1,0:T(8,128)(2,1)S(1)} %get-tuple-element.40), channel_id=1, source_target_pairs={{0,4},{4,0},{8,12},{12,8},{16,20},{20,16},{24,28},{28,24},{32,36},... | collective-permute-start | bytes 786440 | tf_op jit(solution)/shard_map/ppermute | solution.py:270
  37.2 17.0 %collective-permute-start.5 = (bf16[128,512]{1,0:T(8,128)(2,1)S(1)}, bf16[128,512]{1,0:T(8,128)(2,1)S(1)}, u32[]{:S(2)}, u32[]{:S(2)}) collective-permute-start(bf16[128,512]{1,0:T(8,128)(2,1)S(1)} %get-tuple-element.41), channel_id=1, source_target_pairs={{0,500},{4,16},{8,508},{12,24},{16,4},{20,32},{24,12},{28,40},{32,... | collective-permute-start | bytes 393224 | tf_op jit(solution)/shard_map/ppermute | solution.py:282
  41.0 13.9 %collective-permute-start.6 = (bf16[128,512]{1,0:T(8,128)(2,1)S(1)}, bf16[128,512]{1,0:T(8,128)(2,1)S(1)}, u32[]{:S(2)}, u32[]{:S(2)}) collective-permute-start(bf16[128,512]{1,0:T(8,128)(2,1)S(1)} %get-tuple-element.42), channel_id=1, source_target_pairs={{0,508},{4,8},{8,4},{12,16},{16,12},{20,24},{24,20},{28,32},{32,28... | collective-permute-start | bytes 393224 | tf_op jit(solution)/shard_map/ppermute | solution.py:280
  52.3 9.0 %collective-permute-start.7 = (bf16[128,512]{1,0:T(8,128)(2,1)S(1)}, bf16[128,512]{1,0:T(8,128)(2,1)S(1)}, u32[]{:S(2)}, u32[]{:S(2)}) collective-permute-start(bf16[128,512]{1,0:T(8,128)(2,1)S(1)} %get-tuple-element.44), channel_id=1, source_target_pairs={{0,504},{4,12},{8,0},{12,20},{16,8},{20,28},{24,16},{28,36},{32,24... | collective-permute-start | bytes 393224 | tf_op jit(solution)/shard_map/ppermute | solution.py:284

commit v6 on v5

--- a/solution.py
+++ b/solution.py
@@ -72,26 +72,31 @@
     return (column.reshape(4, 16, 128) * mask[None]).reshape(64, 128)
 
 
-def faces_kernel(lo, hi, vox, y_first, y_last, x_first, x_last, sems):
-    copies = [
-        pltpu.make_async_copy(vox.at[:, 0], y_first, sems.at[0]),
-        pltpu.make_async_copy(vox.at[:, 15], y_last, sems.at[1]),
-        pltpu.make_async_copy(vox.at[0], x_first, sems.at[2]),
-        pltpu.make_async_copy(vox.at[7], x_last, sems.at[3]),
+def faces_kernel(side, lo, hi, vox, y_one, y_two, x_one, x_two, sems):
+    core, odd = side[0] & 1, side[0] >> 1
+    y_at = (jnp.where(odd == 1, 0, 15), jnp.where(odd == 1, 15, 0))
+    x_at = (jnp.where(core == 1, 0, 7), jnp.where(core == 1, 7, 0))
+    y_copies = [
+        pltpu.make_async_copy(vox.at[:, y_at[k]], ref, sems.at[k])
+        for k, ref in enumerate((y_one, y_two))
     ]
-    for copy in copies:
+    x_copies = [
+        pltpu.make_async_copy(vox.at[x_at[k]], ref, sems.at[2 + k])
+        for k, ref in enumerate((x_one, x_two))
+    ]
+    for copy in y_copies + x_copies:
         copy.start()
-    for copy, ref, y in ((copies[0], y_first, 0), (copies[1], y_last, 15)):
+    for copy, ref, y in zip(y_copies, (y_one, y_two), y_at):
         copy.wait()
         for x in range(8):
             ref[x] = masked_column(ref[x], lo, hi, x, y)
-    for copy, ref, x in ((copies[2], x_first, 0), (copies[3], x_last, 7)):
+    for copy, ref, x in zip(x_copies, (x_one, x_two), x_at):
         copy.wait()
         for y in range(16):
             ref[y] = masked_column(ref[y], lo, hi, x, y)
 
 
-def faces(lo, hi, vox):
+def faces(side, lo, hi, vox):
     y_face = jax.ShapeDtypeStruct((8, 64, 128), BF)
     x_face = jax.ShapeDtypeStruct((16, 64, 128), BF)
     smem = pl.BlockSpec(memory_space=SMEM)
@@ -99,12 +104,12 @@
     return pl.pallas_call(
         faces_kernel,
         out_shape=(y_face, y_face, x_face, x_face),
-        in_specs=[smem, smem, pl.BlockSpec(memory_space=pltpu.HBM)],
+        in_specs=[smem] * 3 + [pl.BlockSpec(memory_space=pltpu.HBM)],
         out_specs=(vmem,) * 4,
         scratch_shapes=[pltpu.SemaphoreType.DMA((4,))],
         compiler_params=small_vmem(4),
         name="faces",
-    )(*(pltpu.with_memory_space_constraint(a, pltpu.HBM) for a in (lo, hi, vox)))
+    )(side, *(pltpu.with_memory_space_constraint(a, pltpu.HBM) for a in (lo, hi, vox)))
 
 
 def scene_rows(starts, lo, hi, pad, w, d, cb, db, sel, cells):
@@ -160,10 +165,12 @@
     return jnp.dot(cells[...], sel[...], preferred_element_type=F32)
 
 
-def inner_kernel(lo, hi, vox, ylo, yhi, w, d, cb, db, sel, out, pad, cells):
+def inner_kernel(side, lo, hi, vox, y_one, y_two, w, d, cb, db, sel, out, pad, cells):
+    odd = side[0] >> 1
+    one_at, two_at = 17 * (1 - odd), 17 * odd
     for r in range(6):
-        pad[r, 0] = ylo[r + 1]
-        pad[r, 17] = yhi[r + 1]
+        pad[r, one_at] = y_one[r + 1]
+        pad[r, two_at] = y_two[r + 1]
 
     @pl.loop(0, 6)
     def _(r):
@@ -174,15 +181,17 @@
 
 
 def outer_kernel(
-    lo, hi, slots, vox, ylo, yhi, xlo, xhi, inner, w, d, cb, db, sel, keep, give, pad, cells, pieces
+    side, lo, hi, slots, vox, y_one, y_two, x_one, x_two, inner, w, d, cb, db, sel, keep, give, pad, cells, pieces
 ):
-    pad[0] = xlo[...]
-    pad[7] = xhi[...]
+    core, odd = side[0] & 1, side[0] >> 1
+    one_at, two_at = 17 * (1 - odd), 17 * odd
+    pad[7 * (1 - core)] = x_one[...]
+    pad[7 * core] = x_two[...]
     for r in range(3):
-        pad[r + 1, 0] = ylo[r]
-        pad[r + 1, 17] = yhi[r]
-        pad[r + 4, 0] = ylo[r + 5]
-        pad[r + 4, 17] = yhi[r + 5]
+        pad[r + 1, one_at] = y_one[r]
+        pad[r + 1, two_at] = y_two[r]
+        pad[r + 4, one_at] = y_one[r + 5]
+        pad[r + 4, two_at] = y_two[r + 5]
 
     @pl.loop(0, 3)
     def _(r):
@@ -201,29 +210,29 @@
     give[...] = pieces[4:8]
 
 
-def inner_rows(lo, hi, vox, ylo, yhi, tables):
+def inner_rows(side, lo, hi, vox, y_one, y_two, tables):
     smem = pl.BlockSpec(memory_space=SMEM)
     vmem = pl.BlockSpec(memory_space=VMEM)
     return pl.pallas_call(
         inner_kernel,
         out_shape=jax.ShapeDtypeStruct((256, 512), F32),
-        in_specs=[smem] * 2 + [vmem] * 8,
+        in_specs=[smem] * 3 + [vmem] * 8,
         out_specs=vmem,
         scratch_shapes=[VMEM((6, 18, 64, 128), BF), VMEM((256, 1024), BF)],
         compiler_params=small_vmem(12),
         cost_estimate=pl.CostEstimate(flops=5 * 10**9, bytes_accessed=4 * 10**6, transcendentals=0),
         name="inner",
-    )(lo, hi, vox, ylo, yhi, *tables)
-
-
-def outer_rows(lo, hi, slots, vox, ylo, yhi, xlo, xhi, inner, tables):
+    )(side, lo, hi, vox, y_one, y_two, *tables)
+
+
+def outer_rows(side, lo, hi, slots, vox, y_one, y_two, x_one, x_two, inner, tables):
     half = jax.ShapeDtypeStruct((4, 128, 256), BF)
     smem = pl.BlockSpec(memory_space=SMEM)
     vmem = pl.BlockSpec(memory_space=VMEM)
     return pl.pallas_call(
         outer_kernel,
         out_shape=(half, half),
-        in_specs=[smem] * 3 + [vmem] * 11,
+        in_specs=[smem] * 4 + [vmem] * 11,
         out_specs=(vmem, vmem),
         scratch_shapes=[
             VMEM((8, 18, 64, 128), BF),
@@ -232,7 +241,7 @@
         ],
         compiler_params=small_vmem(12),
         name="outer",
-    )(lo, hi, slots, vox, ylo, yhi, xlo, xhi, inner, *tables)
+    )(side, lo, hi, slots, vox, y_one, y_two, x_one, x_two, inner, *tables)
 
 
 def ring(count, step):
@@ -245,19 +254,29 @@
     me = lax.axis_index("blk")
     core = me % 2
 
-    up = [(i, i + 1) for i in range(grp_n - 1)]
-    down = [(b, a) for a, b in up]
-    y_first, y_last, x_first, x_last = faces(shell_lo, shell_hi, voxels)
-    ylo = lax.ppermute(y_last, "grp", up)
-    yhi = lax.ppermute(y_first, "grp", down)
+    grp_odd = lax.axis_index("grp") % 2
+    side = (core + 2 * grp_odd).astype(jnp.int32).reshape(1)
+
+    def swaps(count, first):
+        lower = range(first, count - 1, 2)
+        return [(i, i + 1) for i in lower] + [(i + 1, i) for i in lower]
+
+    y_one, y_two, x_one, x_two = faces(side, shell_lo, shell_hi, voxels)
+    y_one = lax.ppermute(y_one, "grp", swaps(grp_n, 0))
+    y_two = lax.ppermute(y_two, "grp", swaps(grp_n, 1))
     tables = prep(conv_weight, conv_bias, down_weight, down_bias)
-    ylo, yhi, tables = lax.optimization_barrier((ylo, yhi, tables))
-
-    ahead = [(i, i + 1) for i in range(blk_n - 1)]
-    behind = [(b, a) for a, b in ahead]
-    xlo = lax.ppermute(jnp.concatenate([ylo[7:8], x_last, yhi[7:8]]), "blk", ahead)
-    xhi = lax.ppermute(jnp.concatenate([ylo[0:1], x_first, yhi[0:1]]), "blk", behind)
-    inner = inner_rows(shell_lo, shell_hi, voxels, ylo, yhi, tables)
+    y_one, y_two, tables = lax.optimization_barrier((y_one, y_two, tables))
+
+    def x_message(face, last_row):
+        ones = jnp.where(last_row, y_one[7:8], y_one[0:1])
+        twos = jnp.where(last_row, y_two[7:8], y_two[0:1])
+        low = jnp.where(grp_odd == 1, ones, twos)
+        high = jnp.where(grp_odd == 1, twos, ones)
+        return jnp.concatenate([low, face, high])
+
+    x_one = lax.ppermute(x_message(x_one, core == 0), "blk", swaps(blk_n, 0))
+    x_two = lax.ppermute(x_message(x_two, core == 1), "blk", swaps(blk_n, 1))
+    inner = inner_rows(side, shell_lo, shell_hi, voxels, y_one, y_two, tables)
 
     column = me // 2
     owners = lax.dynamic_index_in_dim(coarse_owner[:, 0, :], column, 0, keepdims=False)
@@ -265,7 +284,7 @@
     slots = (offset + 4 * core) % 8
 
     keep, give = outer_rows(
-        shell_lo, shell_hi, slots, voxels, ylo, yhi, xlo, xhi, inner, tables
+        side, shell_lo, shell_hi, slots, voxels, y_one, y_two, x_one, x_two, inner, tables
     )
     got = lax.ppermute(give, "blk", ring(blk_n, lambda i: i ^ 1))
     even = core == 0

time: 62.5 us -> 60.5 us (0.968)
  the two profiles are of different devices: /device:TPU:1 before, /device:TPU:5 now
where the time goes in v6:
time: 60.5 us; the launch traced here: 60.2 us
  starting transfers between devices  31.3 us (52%)
  Pallas kernels  15.8 us (26%)
  waiting for transfers between devices  11.3 us (19%)
  other arithmetic  1.38 us (2%)
    ppermute x1, starting transfers between devices, local(): one = lax.ppermute(mine(2, 1), 'blk', pairs)  11.1 us
    ppermute x1, starting transfers between devices, local(): x_one = lax.ppermute(x_message(x_one, core == 0), 'blk', swaps(blk_n, 0))  7.2 us
    pallas_call x1, Pallas kernels, outer_rows(): pl.pallas_call(outer_kernel, out_shape=(half, half), in_specs=[smem] * 4...  6.5 us
    ppermute x1, waiting for transfers between devices, local(): two = lax.ppermute(mine(1, 2), 'blk', pairs)  6.43 us
    pallas_call x1, Pallas kernels, inner_rows(): pl.pallas_call(inner_kernel, out_shape=jax.ShapeDtypeStruct((256, 512), F...  6.38 us
    ppermute x1, starting transfers between devices, local(): y_one = lax.ppermute(y_one, 'grp', swaps(grp_n, 0))  2.83 us
    ppermute x1, starting transfers between devices, local(): three = lax.ppermute(mine(0, 3), 'blk', pairs)  2.55 us
    ppermute x1, waiting for transfers between devices, local(): y_two = lax.ppermute(y_two, 'grp', swaps(grp_n, 1))  2.27 us
  transfers between devices with their start and end apart: 8, of which 5 were waited for; matrix products, arithmetic and copies ran while one was open for 1% of the time, Pallas kernels for 12%

profile of v6, /device:TPU:5, one launch (start us, length us, event | category | flops | bytes accessed | tf_op | source)
XLA Modules:
  0.0 60.2 jit_solution(4064157762908751395)
XLA Ops:
  0.0 0.0 copy-start.6
  0.0 0.0 copy-start.7
  0.0 0.0 copy-start.5
  0.0 0.0 copy-start.4
  0.0 0.0 copy-start.3
  0.1 2.2 %faces.1 = (bf16[8,64,128]{2,1,0:T(8,128)(2,1)S(1)}, bf16[8,64,128]{2,1,0:T(8,128)(2,1)S(1)}, bf16[16,64,128]{2,1,0:T(8,128)(2,1)S(1)}, bf16[16,64,128]{2,1,0:T(8,128)(2,1)S(1)}) custom-call(s32[1]{0:T(128)} %bitcast.side, s32[8,16]{1,0:T(8,128)} %lo.5, s32[8,16]{1,0:T(8,128)} %hi.5, bf16[8,16,64,128]{3,2,1,0:T(8,128)(2,1)} %vox.5), custom_call_target="tpu_custom_call" | custom-call | tf_op jit(solution)/shard_map/faces/pallas_call | solution.py:104
  2.2 2.8 %collective-permute-start = (bf16[8,64,128]{2,1,0:T(8,128)(2,1)S(1)}, bf16[8,64,128]{2,1,0:T(8,128)(2,1)S(1)}, u32[]{:S(2)}, u32[]{:S(2)}) collective-permute-start(bf16[8,64,128]{2,1,0:T(8,128)(2,1)S(1)} %get-tuple-element.23), channel_id=1, source_target_pairs={{0,1},{2,3},{1,0},{3,2},{4,5},{6,7},{5,4},{7,6},{8,9},{10,11},{9,8... | collective-permute-start | bytes 393224 | tf_op jit(solution)/shard_map/ppermute | solution.py:265
  5.1 1.9 %collective-permute-start.1 = (bf16[8,64,128]{2,1,0:T(8,128)(2,1)S(1)}, bf16[8,64,128]{2,1,0:T(8,128)(2,1)S(1)}, u32[]{:S(2)}, u32[]{:S(2)}) collective-permute-start(bf16[8,64,128]{2,1,0:T(8,128)(2,1)S(1)} %get-tuple-element.24), channel_id=1, source_target_pairs={{1,2},{2,1},{5,6},{6,5},{9,10},{10,9},{13,14},{14,13},{17,18},{18,... | collective-permute-start | bytes 393224 | tf_op jit(solution)/shard_map/ppermute | solution.py:266
  7.0 0.0 copy-done.6
  7.0 0.2 add_reduce_fusion
  7.2 0.0 copy-done.7
  7.3 0.1 broadcast_in_dim_tile.3.cb
  7.3 0.0 copy-done.5
  7.4 0.0 copy-done.4
  7.4 0.0 copy-done.3
  7.4 0.0 copy-start
  7.4 0.0 copy-start.1
  7.4 0.0 copy-start.2
  7.4 0.8 %prep.1 = (bf16[384,768]{1,0:T(8,128)(2,1)S(1)}, bf16[256,256]{1,0:T(8,128)(2,1)S(1)}, f32[128,128]{1,0:T(8,128)S(1)}, f32[128,128]{1,0:T(8,128)S(1)}, bf16[1024,512]{1,0:T(8,128)(2,1)S(1)}) custom-call(bf16[3,3,3,64,64]{4,3,2,1,0:T(8,128)(2,1)S(1)} %copy-done.3, f32[1,128]{1,0:T(1,128)S(1)} %broadcast_in_dim_tile.3.cb, bf16[8,64,128]{2,1,0:T(8,128)(2,1)S(1)} %copy-done.4, ...), custom_call_target="tpu_custom_call" | custom-call | flops 1000000000 | bytes 4000000 | tf_op jit(solution)/shard_map/prep/pallas_call | solution.py:45
  8.2 0.3 collective-permute-done.y_one
  8.5 2.3 %collective-permute-done.1.y_two = bf16[8,64,128]{2,1,0:T(8,128)(2,1)S(1)} collective-permute-done((bf16[8,64,128]{2,1,0:T(8,128)(2,1)S(1)}, bf16[8,64,128]{2,1,0:T(8,128)(2,1)S(1)}, u32[]{:S(2)}, u32[]{:S(2)}) %collective-permute-start.1) | collective-permute-done | bytes 131104 | tf_op jit(solution)/shard_map/ppermute | solution.py:266
  10.8 7.2 %collective-permute-start.2 = (bf16[18,64,128]{2,1,0:T(8,128)(2,1)S(1)}, bf16[18,64,128]{2,1,0:T(8,128)(2,1)S(1)}, u32[]{:S(2)}, u32[]{:S(2)}) collective-permute-start(bf16[18,64,128]{2,1,0:T(8,128)(2,1)S(1)} %pad_maximum_fusion), channel_id=1, source_target_pairs={{0,4},{8,12},{16,20},{24,28},{32,36},{40,44},{48,52},{56,60},{64,6... | collective-permute-start | bytes 884744 | tf_op jit(solution)/shard_map/ppermute | solution.py:277
  18.1 1.9 %collective-permute-start.3 = (bf16[18,64,128]{2,1,0:T(8,128)(2,1)S(1)}, bf16[18,64,128]{2,1,0:T(8,128)(2,1)S(1)}, u32[]{:S(2)}, u32[]{:S(2)}) collective-permute-start(bf16[18,64,128]{2,1,0:T(8,128)(2,1)S(1)} %pad_maximum_fusion.1), channel_id=1, source_target_pairs={{4,8},{12,16},{20,24},{28,32},{36,40},{44,48},{52,56},{60,64},{68,... | collective-permute-start | bytes 884744 | tf_op jit(solution)/shard_map/ppermute | solution.py:278
  20.0 0.0 copy-done
  20.0 0.0 copy-done.1
  20.1 0.0 copy-done.2
  20.1 6.4 %inner.1 = f32[256,512]{1,0:T(8,128)S(1)} custom-call(s32[1]{0:T(128)} %bitcast.side, s32[8,16]{1,0:T(8,128)S(1)} %copy-done.1, s32[8,16]{1,0:T(8,128)S(1)} %copy-done.2, bf16[8,16,64,128]{3,2,1,0:T(8,128)(2,1)S(1)} %copy-done, bf16[8,64,128]{2,1,0:T(8,128)(2,1)S(1)} %collective-permute-done.y_one, bf16[8,64,128]{2,1,0:T(8,128)(2,1)S(1)} %collective-permute-done.1.y_two, ...), custom_call_target="tpu_custom_call" | custom-call | flops 5000000000 | bytes 4000000 | tf_op jit(solution)/shard_map/inner/pallas_call | solution.py:216
  26.4 0.0 collective-permute-done.2.x_one
  26.5 0.0 collective-permute-done.3.x_two
  26.5 6.5 %outer.1 = (bf16[4,128,256]{2,1,0:T(8,128)(2,1)S(1)}, bf16[4,128,256]{2,1,0:T(8,128)(2,1)S(1)}) custom-call(s32[1]{0:T(128)} %bitcast.side, s32[8,16]{1,0:T(8,128)S(1)} %copy-done.1, s32[8,16]{1,0:T(8,128)S(1)} %copy-done.2, s32[8]{0:T(128)S(1)} %and_select_fusion.slots, bf16[8,16,64,128]{3,2,1,0:T(8,128)(2,1)S(1)} %copy-done, ...), custom_call_target="tpu_custom_call" | custom-call | tf_op jit(solution)/shard_map/outer/pallas_call | solution.py:232
  33.0 1.9 %collective-permute-start.4 = (bf16[4,128,256]{2,1,0:T(8,128)(2,1)S(1)}, bf16[4,128,256]{2,1,0:T(8,128)(2,1)S(1)}, u32[]{:S(2)}, u32[]{:S(2)}) collective-permute-start(bf16[4,128,256]{2,1,0:T(8,128)(2,1)S(1)} %get-tuple-element.40), channel_id=1, source_target_pairs={{0,4},{4,0},{8,12},{12,8},{16,20},{20,16},{24,28},{28,24},{32,36},... | collective-permute-start | bytes 786440 | tf_op jit(solution)/shard_map/ppermute | solution.py:289
  34.9 1.5 %collective-permute-done.4 = bf16[4,128,256]{2,1,0:T(8,128)(2,1)S(1)} collective-permute-done((bf16[4,128,256]{2,1,0:T(8,128)(2,1)S(1)}, bf16[4,128,256]{2,1,0:T(8,128)(2,1)S(1)}, u32[]{:S(2)}, u32[]{:S(2)}) %collective-permute-start.4) | collective-permute-done | bytes 262176 | tf_op jit(solution)/shard_map/ppermute | solution.py:289
  36.4 0.1 maximum_select_fusion
  36.6 2.6 %collective-permute-start.5 = (bf16[128,512]{1,0:T(8,128)(2,1)S(1)}, bf16[128,512]{1,0:T(8,128)(2,1)S(1)}, u32[]{:S(2)}, u32[]{:S(2)}) collective-permute-start(bf16[128,512]{1,0:T(8,128)(2,1)S(1)} %get-tuple-element.41), channel_id=1, source_target_pairs={{0,500},{4,16},{8,508},{12,24},{16,4},{20,32},{24,12},{28,40},{32,... | collective-permute-start | bytes 393224 | tf_op jit(solution)/shard_map/ppermute | solution.py:301
  39.1 11.1 %collective-permute-start.6 = (bf16[128,512]{1,0:T(8,128)(2,1)S(1)}, bf16[128,512]{1,0:T(8,128)(2,1)S(1)}, u32[]{:S(2)}, u32[]{:S(2)}) collective-permute-start(bf16[128,512]{1,0:T(8,128)(2,1)S(1)} %get-tuple-element.42), channel_id=1, source_target_pairs={{0,508},{4,8},{8,4},{12,16},{16,12},{20,24},{24,20},{28,32},{32,28... | collective-permute-start | bytes 393224 | tf_op jit(solution)/shard_map/ppermute | solution.py:299
  50.2 1.9 %collective-permute-start.7 = (bf16[128,512]{1,0:T(8,128)(2,1)S(1)}, bf16[128,512]{1,0:T(8,128)(2,1)S(1)}, u32[]{:S(2)}, u32[]{:S(2)}) collective-permute-start(bf16[128,512]{1,0:T(8,128)(2,1)S(1)} %get-tuple-element.44), channel_id=1, source_target_pairs={{0,504},{4,12},{8,0},{12,20},{16,8},{20,28},{24,16},{28,36},{32,24... | collective-permute-start | bytes 393224 | tf_op jit(solution)/shard_map/ppermute | solution.py:303
  52.1 0.0 collective-permute-done.5
  52.2 0.7 %collective-permute-done.6 = bf16[128,512]{1,0:T(8,128)(2,1)S(1)} collective-permute-done((bf16[128,512]{1,0:T(8,128)(2,1)S(1)}, bf16[128,512]{1,0:T(8,128)(2,1)S(1)}, u32[]{:S(2)}, u32[]{:S(2)}) %collective-permute-start.6) | collective-permute-done | bytes 131104 | tf_op jit(solution)/shard_map/ppermute | solution.py:299
  52.9 6.4 %collective-permute-done.7 = bf16[128,512]{1,0:T(8,128)(2,1)S(1)} collective-permute-done((bf16[128,512]{1,0:T(8,128)(2,1)S(1)}, bf16[128,512]{1,0:T(8,128)(2,1)S(1)}, u32[]{:S(2)}, u32[]{:S(2)}) %collective-permute-start.7) | collective-permute-done | bytes 131104 | tf_op jit(solution)/shard_map/ppermute | solution.py:303
  59.3 0.9 %maximum_select_fusion.1 = bf16[1,1,4,128,512]{4,3,2,1,0:T(8,128)(2,1)} fusion(bf16[1,1,1,128,512]{4,3,2,1,0:T(8,128)(2,1)S(1)} %bitcast.16, bf16[1,1,1,128,512]{4,3,2,1,0:T(8,128)(2,1)S(1)} %get-tuple-element.43, bf16[1,1,1,128,512]{4,3,2,1,0:T(8,128)(2,1)S(1)} %bitcast.15, bf16[1,1,1,128,512]{4,3,2,1,0:T(8,128)(2,1)S(1)} %bitcast.14, pred[]{:T(512)S(6)} %eq.19), kind=kLoop, calls=%fused_computation.1 | loop fusion | flops 1835008 | bytes 1048577 | tf_op jit(solution)/shard_map/jit(_where)/select_n | solution.py:305
  (6 shorter events, 0.2 us)
Async XLA Ops:
  0.0 7.0 %copy-start.6 = (s32[64,1,8]{0,2,1:T(8,128)S(1)}, s32[64,1,8]{0,2,1:T(8,128)}, u32[]{:S(2)}) copy-start(s32[64,1,8]{0,2,1:T(8,128)} %param.15) | copy-start | bytes 6148
  0.0 7.2 %copy-start.7 = (f32[64]{0:T(128)S(1)}, f32[64]{0:T(128)}, u32[]{:S(2)}) copy-start(f32[64]{0:T(128)} %param.12) | copy-start | bytes 772
  0.0 7.3 %copy-start.5 = (f32[128]{0:T(128)S(1)}, f32[128]{0:T(128)}, u32[]{:S(2)}) copy-start(f32[128]{0:T(128)} %param.14) | copy-start | bytes 1540
  0.0 7.3 %copy-start.4 = (bf16[8,64,128]{2,1,0:T(8,128)(2,1)S(1)}, bf16[8,64,128]{2,1,0:T(8,128)(2,1)}, u32[]{:S(2)}) copy-start(bf16[8,64,128]{2,1,0:T(8,128)(2,1)} %dw.1) | copy-start | bytes 393220
  0.0 7.3 %copy-start.3 = (bf16[3,3,3,64,64]{4,3,2,1,0:T(8,128)(2,1)S(1)}, bf16[3,3,3,64,64]{4,3,2,1,0:T(8,128)(2,1)}, u32[]{:S(2)}) copy-start(bf16[3,3,3,64,64]{4,3,2,1,0:T(8,128)(2,1)} %cw.1) | copy-start | bytes 663556
  2.2 6.3 %collective-permute-start = (bf16[8,64,128]{2,1,0:T(8,128)(2,1)S(1)}, bf16[8,64,128]{2,1,0:T(8,128)(2,1)S(1)}, u32[]{:S(2)}, u32[]{:S(2)}) collective-permute-start(bf16[8,64,128]{2,1,0:T(8,128)(2,1)S(1)} %get-tuple-element.23), channel_id=1, source_target_pairs={{0,1},{2,3},{1,0},{3,2},{4,5},{6,7},{5,4},{7,6},{8,9},{10,11},{9,8... | collective-permute-start | bytes 393224 | tf_op jit(solution)/shard_map/ppermute | solution.py:265
  5.1 5.7 %collective-permute-start.1 = (bf16[8,64,128]{2,1,0:T(8,128)(2,1)S(1)}, bf16[8,64,128]{2,1,0:T(8,128)(2,1)S(1)}, u32[]{:S(2)}, u32[]{:S(2)}) collective-permute-start(bf16[8,64,128]{2,1,0:T(8,128)(2,1)S(1)} %get-tuple-element.24), channel_id=1, source_target_pairs={{1,2},{2,1},{5,6},{6,5},{9,10},{10,9},{13,14},{14,13},{17,18},{18,... | collective-permute-start | bytes 393224 | tf_op jit(solution)/shard_map/ppermute | solution.py:266
  7.4 12.7 %copy-start = (bf16[8,16,64,128]{3,2,1,0:T(8,128)(2,1)S(1)}, bf16[8,16,64,128]{3,2,1,0:T(8,128)(2,1)}, u32[]{:S(2)}) copy-start(bf16[8,16,64,128]{3,2,1,0:T(8,128)(2,1)} %vox.5) | copy-start | bytes 6291460
  7.4 12.7 %copy-start.1 = (s32[8,16]{1,0:T(8,128)S(1)}, s32[8,16]{1,0:T(8,128)}, u32[]{:S(2)}) copy-start(s32[8,16]{1,0:T(8,128)} %lo.5) | copy-start | bytes 1540
  7.4 12.7 %copy-start.2 = (s32[8,16]{1,0:T(8,128)S(1)}, s32[8,16]{1,0:T(8,128)}, u32[]{:S(2)}) copy-start(s32[8,16]{1,0:T(8,128)} %hi.5) | copy-start | bytes 1540
  10.8 15.6 %collective-permute-start.2 = (bf16[18,64,128]{2,1,0:T(8,128)(2,1)S(1)}, bf16[18,64,128]{2,1,0:T(8,128)(2,1)S(1)}, u32[]{:S(2)}, u32[]{:S(2)}) collective-permute-start(bf16[18,64,128]{2,1,0:T(8,128)(2,1)S(1)} %pad_maximum_fusion), channel_id=1, source_target_pairs={{0,4},{8,12},{16,20},{24,28},{32,36},{40,44},{48,52},{56,60},{64,6... | collective-permute-start | bytes 884744 | tf_op jit(solution)/shard_map/ppermute | solution.py:277
  18.1 8.4 %collective-permute-start.3 = (bf16[18,64,128]{2,1,0:T(8,128)(2,1)S(1)}, bf16[18,64,128]{2,1,0:T(8,128)(2,1)S(1)}, u32[]{:S(2)}, u32[]{:S(2)}) collective-permute-start(bf16[18,64,128]{2,1,0:T(8,128)(2,1)S(1)} %pad_maximum_fusion.1), channel_id=1, source_target_pairs={{4,8},{12,16},{20,24},{28,32},{36,40},{44,48},{52,56},{60,64},{68,... | collective-permute-start | bytes 884744 | tf_op jit(solution)/shard_map/ppermute | solution.py:278
  33.0 3.4 %collective-permute-start.4 = (bf16[4,128,256]{2,1,0:T(8,128)(2,1)S(1)}, bf16[4,128,256]{2,1,0:T(8,128)(2,1)S(1)}, u32[]{:S(2)}, u32[]{:S(2)}) collective-permute-start(bf16[4,128,256]{2,1,0:T(8,128)(2,1)S(1)} %get-tuple-element.40), channel_id=1, source_target_pairs={{0,4},{4,0},{8,12},{12,8},{16,20},{20,16},{24,28},{28,24},{32,36},... | collective-permute-start | bytes 786440 | tf_op jit(solution)/shard_map/ppermute | solution.py:289
  36.6 15.6 %collective-permute-start.5 = (bf16[128,512]{1,0:T(8,128)(2,1)S(1)}, bf16[128,512]{1,0:T(8,128)(2,1)S(1)}, u32[]{:S(2)}, u32[]{:S(2)}) collective-permute-start(bf16[128,512]{1,0:T(8,128)(2,1)S(1)} %get-tuple-element.41), channel_id=1, source_target_pairs={{0,500},{4,16},{8,508},{12,24},{16,4},{20,32},{24,12},{28,40},{32,... | collective-permute-start | bytes 393224 | tf_op jit(solution)/shard_map/ppermute | solution.py:301
  39.1 13.7 %collective-permute-start.6 = (bf16[128,512]{1,0:T(8,128)(2,1)S(1)}, bf16[128,512]{1,0:T(8,128)(2,1)S(1)}, u32[]{:S(2)}, u32[]{:S(2)}) collective-permute-start(bf16[128,512]{1,0:T(8,128)(2,1)S(1)} %get-tuple-element.42), channel_id=1, source_target_pairs={{0,508},{4,8},{8,4},{12,16},{16,12},{20,24},{24,20},{28,32},{32,28... | collective-permute-start | bytes 393224 | tf_op jit(solution)/shard_map/ppermute | solution.py:299
  50.2 9.1 %collective-permute-start.7 = (bf16[128,512]{1,0:T(8,128)(2,1)S(1)}, bf16[128,512]{1,0:T(8,128)(2,1)S(1)}, u32[]{:S(2)}, u32[]{:S(2)}) collective-permute-start(bf16[128,512]{1,0:T(8,128)(2,1)S(1)} %get-tuple-element.44), channel_id=1, source_target_pairs={{0,504},{4,12},{8,0},{12,20},{16,8},{20,28},{24,16},{28,36},{32,24... | collective-permute-start | bytes 393224 | tf_op jit(solution)/shard_map/ppermute | solution.py:303

commit v7 on v6

--- a/solution.py
+++ b/solution.py
@@ -16,7 +16,27 @@
     return pltpu.CompilerParams(vmem_limit_bytes=mib * 1024 * 1024)
 
 
-def prep_kernel(cw, cb, dw, db, w_out, d_out, cb_out, db_out, sel_out):
+def occupancy(lo, hi, x, y):
+    lane = lax.broadcasted_iota(jnp.int32, (8, 128), 1)
+    return jnp.where((lane >= lo[x, y]) & (lane < hi[x, y]), 1.0, 0.0)
+
+
+def masked_column(column, lo, hi, x, y):
+    mask = jnp.concatenate([occupancy(lo, hi, x, y)] * 2, axis=0).astype(BF)
+    return (column.reshape(4, 16, 128) * mask[None]).reshape(64, 128)
+
+
+def prep_kernel(
+    side, lo, hi, vox, cw, cb, dw, db, x_one, x_two, w_out, d_out, cb_out, db_out, sel_out, sems
+):
+    core = side[0] & 1
+    x_at = (jnp.where(core == 1, 0, 7), jnp.where(core == 1, 7, 0))
+    copies = [
+        pltpu.make_async_copy(vox.at[x_at[k]], ref, sems.at[k])
+        for k, ref in enumerate((x_one, x_two))
+    ]
+    for copy in copies:
+        copy.start()
     zero = jnp.zeros((64, 64), F32)
     for dx in range(3):
         for dz in range(3):
@@ -39,22 +59,36 @@
         lane = lax.broadcasted_iota(jnp.int32, (128, 512), 1)
         want = jnp.where(((lane >> 3) & 7) == q, 16 * (lane >> 6) + 2 * (lane & 7), -1)
         sel_out[q * 128 : q * 128 + 128, :] = jnp.where(z == want, 1.0, 0.0).astype(BF)
-
-
-def prep(conv_weight, conv_bias, down_weight, down_bias):
+    for copy, ref, x in zip(copies, (x_one, x_two), x_at):
+        copy.wait()
+        for y in range(16):
+            ref[y] = masked_column(ref[y], lo, hi, x, y)
+
+
+def prep(side, lo, hi, vox, conv_weight, conv_bias, down_weight, down_bias):
+    smem = pl.BlockSpec(memory_space=SMEM)
+    vmem = pl.BlockSpec(memory_space=VMEM)
+    x_face = jax.ShapeDtypeStruct((16, 64, 128), BF)
     return pl.pallas_call(
         prep_kernel,
         out_shape=(
+            x_face,
+            x_face,
             jax.ShapeDtypeStruct((384, 768), BF),
             jax.ShapeDtypeStruct((256, 256), BF),
             jax.ShapeDtypeStruct((128, 128), F32),
             jax.ShapeDtypeStruct((128, 128), F32),
             jax.ShapeDtypeStruct((1024, 512), BF),
         ),
+        in_specs=[smem] * 3 + [pl.BlockSpec(memory_space=pltpu.HBM)] + [vmem] * 4,
+        out_specs=(vmem,) * 7,
+        scratch_shapes=[pltpu.SemaphoreType.DMA((2,))],
         compiler_params=small_vmem(8),
         cost_estimate=pl.CostEstimate(flops=10**9, bytes_accessed=4 * 10**6, transcendentals=0),
         name="prep",
     )(
+        side,
+        *in_place(lo, hi, vox),
         conv_weight,
         jnp.tile(conv_bias, 2)[None],
         down_weight,
@@ -62,54 +96,38 @@
     )
 
 
-def occupancy(lo, hi, x, y):
-    lane = lax.broadcasted_iota(jnp.int32, (8, 128), 1)
-    return jnp.where((lane >= lo[x, y]) & (lane < hi[x, y]), 1.0, 0.0)
-
-
-def masked_column(column, lo, hi, x, y):
-    mask = jnp.concatenate([occupancy(lo, hi, x, y)] * 2, axis=0).astype(BF)
-    return (column.reshape(4, 16, 128) * mask[None]).reshape(64, 128)
-
-
-def faces_kernel(side, lo, hi, vox, y_one, y_two, x_one, x_two, sems):
-    core, odd = side[0] & 1, side[0] >> 1
+def faces_kernel(side, lo, hi, vox, y_one, y_two, sems):
+    odd = side[0] >> 1
     y_at = (jnp.where(odd == 1, 0, 15), jnp.where(odd == 1, 15, 0))
-    x_at = (jnp.where(core == 1, 0, 7), jnp.where(core == 1, 7, 0))
-    y_copies = [
+    copies = [
         pltpu.make_async_copy(vox.at[:, y_at[k]], ref, sems.at[k])
         for k, ref in enumerate((y_one, y_two))
     ]
-    x_copies = [
-        pltpu.make_async_copy(vox.at[x_at[k]], ref, sems.at[2 + k])
-        for k, ref in enumerate((x_one, x_two))
-    ]
-    for copy in y_copies + x_copies:
+    for copy in copies:
         copy.start()
-    for copy, ref, y in zip(y_copies, (y_one, y_two), y_at):
+    for copy, ref, y in zip(copies, (y_one, y_two), y_at):
         copy.wait()
         for x in range(8):
             ref[x] = masked_column(ref[x], lo, hi, x, y)
-    for copy, ref, x in zip(x_copies, (x_one, x_two), x_at):
-        copy.wait()
-        for y in range(16):
-            ref[y] = masked_column(ref[y], lo, hi, x, y)
+
+
+def in_place(*arrays):
+    return tuple(pltpu.with_memory_space_constraint(a, pltpu.HBM) for a in arrays)
 
 
 def faces(side, lo, hi, vox):
     y_face = jax.ShapeDtypeStruct((8, 64, 128), BF)
-    x_face = jax.ShapeDtypeStruct((16, 64, 128), BF)
     smem = pl.BlockSpec(memory_space=SMEM)
     vmem = pl.BlockSpec(memory_space=VMEM)
     return pl.pallas_call(
         faces_kernel,
-        out_shape=(y_face, y_face, x_face, x_face),
+        out_shape=(y_face, y_face),
         in_specs=[smem] * 3 + [pl.BlockSpec(memory_space=pltpu.HBM)],
-        out_specs=(vmem,) * 4,
-        scratch_shapes=[pltpu.SemaphoreType.DMA((4,))],
+        out_specs=(vmem, vmem),
+        scratch_shapes=[pltpu.SemaphoreType.DMA((2,))],
         compiler_params=small_vmem(4),
         name="faces",
-    )(side, *(pltpu.with_memory_space_constraint(a, pltpu.HBM) for a in (lo, hi, vox)))
+    )(side, *in_place(lo, hi, vox))
 
 
 def scene_rows(starts, lo, hi, pad, w, d, cb, db, sel, cells):
@@ -261,11 +279,13 @@
         lower = range(first, count - 1, 2)
         return [(i, i + 1) for i in lower] + [(i + 1, i) for i in lower]
 
-    y_one, y_two, x_one, x_two = faces(side, shell_lo, shell_hi, voxels)
+    y_one, y_two = faces(side, shell_lo, shell_hi, voxels)
     y_one = lax.ppermute(y_one, "grp", swaps(grp_n, 0))
     y_two = lax.ppermute(y_two, "grp", swaps(grp_n, 1))
-    tables = prep(conv_weight, conv_bias, down_weight, down_bias)
-    y_one, y_two, tables = lax.optimization_barrier((y_one, y_two, tables))
+    x_one, x_two, *tables = prep(
+        side, shell_lo, shell_hi, voxels, conv_weight, conv_bias, down_weight, down_bias
+    )
+    y_one, y_two, tables = lax.optimization_barrier((y_one, y_two, tuple(tables)))
 
     def x_message(face, last_row):
         ones = jnp.where(last_row, y_one[7:8], y_one[0:1])

time: 60.5 us -> 60.3 us (level)
  waiting for transfers between devices: 11.3 us -> 9.7 us
  Pallas kernels: 15.8 us -> 17.1 us
    pallas_call x2, Pallas kernels: 2.94 us -> 4.24 us  [the longest x1 2.3 us: prep(): pl.pallas_call(prep_kernel, out_shape=(x_face, x_face, jax.ShapeDtypeStru...]
    ppermute x1, waiting for transfers between devices: 2.27 us -> 1.07 us  [local(): y_two = lax.ppermute(y_two, 'grp', swaps(grp_n, 1))]
  transfers between devices with their start and end apart: 8 -> 8, of which waited for: 5 -> 4; matrix products, arithmetic and copies ran while one was open for 1% -> 1% of each run, Pallas kernels for 12% -> 14%
where the time goes in v7:
time: 60.3 us; the launch traced here: 60 us
  starting transfers between devices  31.3 us (52%)
  Pallas kernels  17.1 us (28%)
  waiting for transfers between devices  9.7 us (16%)
  other arithmetic  1.38 us (2%)
    ppermute x1, starting transfers between devices, local(): one = lax.ppermute(mine(2, 1), 'blk', pairs)  11.1 us
    ppermute x1, starting transfers between devices, local(): x_one = lax.ppermute(x_message(x_one, core == 0), 'blk', swaps(blk_n, 0))  7.2 us
    pallas_call x1, Pallas kernels, outer_rows(): pl.pallas_call(outer_kernel, out_shape=(half, half), in_specs=[smem] * 4...  6.5 us
    ppermute x1, waiting for transfers between devices, local(): two = lax.ppermute(mine(1, 2), 'blk', pairs)  6.43 us
    pallas_call x1, Pallas kernels, inner_rows(): pl.pallas_call(inner_kernel, out_shape=jax.ShapeDtypeStruct((256, 512), F...  6.38 us
    ppermute x1, starting transfers between devices, local(): y_one = lax.ppermute(y_one, 'grp', swaps(grp_n, 0))  2.83 us
    ppermute x1, starting transfers between devices, local(): three = lax.ppermute(mine(0, 3), 'blk', pairs)  2.55 us
    pallas_call x1, Pallas kernels, prep(): pl.pallas_call(prep_kernel, out_shape=(x_face, x_face, jax.ShapeDtypeStru...  2.3 us
  transfers between devices with their start and end apart: 8, of which 4 were waited for; matrix products, arithmetic and copies ran while one was open for 1% of the time, Pallas kernels for 14%

profile of v7, /device:TPU:5, one launch (start us, length us, event | category | flops | bytes accessed | tf_op | source)
XLA Modules:
  0.0 60.0 jit_solution(15536385776947662547)
XLA Ops:
  0.0 0.0 copy-start.6
  0.0 0.0 copy-start.7
  0.0 0.0 copy-start.5
  0.0 0.0 copy-start.4
  0.0 0.0 copy-start.3
  0.1 1.9 %faces.1 = (bf16[8,64,128]{2,1,0:T(8,128)(2,1)S(1)}, bf16[8,64,128]{2,1,0:T(8,128)(2,1)S(1)}) custom-call(s32[1]{0:T(128)} %bitcast.side, s32[8,16]{1,0:T(8,128)} %lo.7, s32[8,16]{1,0:T(8,128)} %hi.7, bf16[8,16,64,128]{3,2,1,0:T(8,128)(2,1)} %vox.7), custom_call_target="tpu_custom_call" | custom-call | tf_op jit(solution)/shard_map/faces/pallas_call | solution.py:122
  2.0 2.8 %collective-permute-start = (bf16[8,64,128]{2,1,0:T(8,128)(2,1)S(1)}, bf16[8,64,128]{2,1,0:T(8,128)(2,1)S(1)}, u32[]{:S(2)}, u32[]{:S(2)}) collective-permute-start(bf16[8,64,128]{2,1,0:T(8,128)(2,1)S(1)} %get-tuple-element.23), channel_id=1, source_target_pairs={{0,1},{2,3},{1,0},{3,2},{4,5},{6,7},{5,4},{7,6},{8,9},{10,11},{9,8... | collective-permute-start | bytes 393224 | tf_op jit(solution)/shard_map/ppermute | solution.py:283
  4.8 1.9 %collective-permute-start.1 = (bf16[8,64,128]{2,1,0:T(8,128)(2,1)S(1)}, bf16[8,64,128]{2,1,0:T(8,128)(2,1)S(1)}, u32[]{:S(2)}, u32[]{:S(2)}) collective-permute-start(bf16[8,64,128]{2,1,0:T(8,128)(2,1)S(1)} %get-tuple-element.24), channel_id=1, source_target_pairs={{1,2},{2,1},{5,6},{6,5},{9,10},{10,9},{13,14},{14,13},{17,18},{18,... | collective-permute-start | bytes 393224 | tf_op jit(solution)/shard_map/ppermute | solution.py:284
  6.8 0.0 copy-done.6
  6.8 0.2 add_reduce_fusion
  7.0 0.0 copy-done.7
  7.0 0.1 broadcast_in_dim_tile.3.cb
  7.1 0.0 copy-done.5
  7.1 0.0 copy-done.4
  7.1 0.0 copy-done.3
  7.1 0.0 copy-start
  7.1 0.0 copy-start.1
  7.1 0.0 copy-start.2
  7.2 2.3 %prep.1 = (bf16[16,64,128]{2,1,0:T(8,128)(2,1)S(1)}, bf16[16,64,128]{2,1,0:T(8,128)(2,1)S(1)}, bf16[384,768]{1,0:T(8,128)(2,1)S(1)}, bf16[256,256]{1,0:T(8,128)(...) custom-call(s32[1]{0:T(128)} %bitcast.side, s32[8,16]{1,0:T(8,128)} %lo.7, ...), custom_call_target="tpu_custom_call" | custom-call | flops 1000000000 | bytes 4000000 | tf_op jit(solution)/shard_map/prep/pallas_call | solution.py:72
  9.5 0.0 collective-permute-done.y_one
  9.5 1.1 %collective-permute-done.1.y_two = bf16[8,64,128]{2,1,0:T(8,128)(2,1)S(1)} collective-permute-done((bf16[8,64,128]{2,1,0:T(8,128)(2,1)S(1)}, bf16[8,64,128]{2,1,0:T(8,128)(2,1)S(1)}, u32[]{:S(2)}, u32[]{:S(2)}) %collective-permute-start.1) | collective-permute-done | bytes 131104 | tf_op jit(solution)/shard_map/ppermute | solution.py:284
  10.6 7.2 %collective-permute-start.2 = (bf16[18,64,128]{2,1,0:T(8,128)(2,1)S(1)}, bf16[18,64,128]{2,1,0:T(8,128)(2,1)S(1)}, u32[]{:S(2)}, u32[]{:S(2)}) collective-permute-start(bf16[18,64,128]{2,1,0:T(8,128)(2,1)S(1)} %pad_maximum_fusion), channel_id=1, source_target_pairs={{0,4},{8,12},{16,20},{24,28},{32,36},{40,44},{48,52},{56,60},{64,6... | collective-permute-start | bytes 884744 | tf_op jit(solution)/shard_map/ppermute | solution.py:297
  17.9 1.9 %collective-permute-start.3 = (bf16[18,64,128]{2,1,0:T(8,128)(2,1)S(1)}, bf16[18,64,128]{2,1,0:T(8,128)(2,1)S(1)}, u32[]{:S(2)}, u32[]{:S(2)}) collective-permute-start(bf16[18,64,128]{2,1,0:T(8,128)(2,1)S(1)} %pad_maximum_fusion.1), channel_id=1, source_target_pairs={{4,8},{12,16},{20,24},{28,32},{36,40},{44,48},{52,56},{60,64},{68,... | collective-permute-start | bytes 884744 | tf_op jit(solution)/shard_map/ppermute | solution.py:298
  19.8 0.0 copy-done
  19.8 0.0 copy-done.1
  19.8 0.0 copy-done.2
  19.8 6.4 %inner.1 = f32[256,512]{1,0:T(8,128)S(1)} custom-call(s32[1]{0:T(128)} %bitcast.side, s32[8,16]{1,0:T(8,128)S(1)} %copy-done.1, s32[8,16]{1,0:T(8,128)S(1)} %copy-done.2, bf16[8,16,64,128]{3,2,1,0:T(8,128)(2,1)S(1)} %copy-done, bf16[8,64,128]{2,1,0:T(8,128)(2,1)S(1)} %collective-permute-done.y_one, bf16[8,64,128]{2,1,0:T(8,128)(2,1)S(1)} %collective-permute-done.1.y_two, ...), custom_call_target="tpu_custom_call" | custom-call | flops 5000000000 | bytes 4000000 | tf_op jit(solution)/shard_map/inner/pallas_call | solution.py:234
  26.2 0.0 collective-permute-done.2.x_one
  26.2 0.0 collective-permute-done.3.x_two
  26.2 6.5 %outer.1 = (bf16[4,128,256]{2,1,0:T(8,128)(2,1)S(1)}, bf16[4,128,256]{2,1,0:T(8,128)(2,1)S(1)}) custom-call(s32[1]{0:T(128)} %bitcast.side, s32[8,16]{1,0:T(8,128)S(1)} %copy-done.1, s32[8,16]{1,0:T(8,128)S(1)} %copy-done.2, s32[8]{0:T(128)S(1)} %and_select_fusion.slots, bf16[8,16,64,128]{3,2,1,0:T(8,128)(2,1)S(1)} %copy-done, ...), custom_call_target="tpu_custom_call" | custom-call | tf_op jit(solution)/shard_map/outer/pallas_call | solution.py:250
  32.7 1.9 %collective-permute-start.4 = (bf16[4,128,256]{2,1,0:T(8,128)(2,1)S(1)}, bf16[4,128,256]{2,1,0:T(8,128)(2,1)S(1)}, u32[]{:S(2)}, u32[]{:S(2)}) collective-permute-start(bf16[4,128,256]{2,1,0:T(8,128)(2,1)S(1)} %get-tuple-element.40), channel_id=1, source_target_pairs={{0,4},{4,0},{8,12},{12,8},{16,20},{20,16},{24,28},{28,24},{32,36},... | collective-permute-start | bytes 786440 | tf_op jit(solution)/shard_map/ppermute | solution.py:309
  34.7 1.5 %collective-permute-done.4 = bf16[4,128,256]{2,1,0:T(8,128)(2,1)S(1)} collective-permute-done((bf16[4,128,256]{2,1,0:T(8,128)(2,1)S(1)}, bf16[4,128,256]{2,1,0:T(8,128)(2,1)S(1)}, u32[]{:S(2)}, u32[]{:S(2)}) %collective-permute-start.4) | collective-permute-done | bytes 262176 | tf_op jit(solution)/shard_map/ppermute | solution.py:309
  36.2 0.1 maximum_select_fusion
  36.3 2.5 %collective-permute-start.5 = (bf16[128,512]{1,0:T(8,128)(2,1)S(1)}, bf16[128,512]{1,0:T(8,128)(2,1)S(1)}, u32[]{:S(2)}, u32[]{:S(2)}) collective-permute-start(bf16[128,512]{1,0:T(8,128)(2,1)S(1)} %get-tuple-element.41), channel_id=1, source_target_pairs={{0,500},{4,16},{8,508},{12,24},{16,4},{20,32},{24,12},{28,40},{32,... | collective-permute-start | bytes 393224 | tf_op jit(solution)/shard_map/ppermute | solution.py:321
  38.9 11.1 %collective-permute-start.6 = (bf16[128,512]{1,0:T(8,128)(2,1)S(1)}, bf16[128,512]{1,0:T(8,128)(2,1)S(1)}, u32[]{:S(2)}, u32[]{:S(2)}) collective-permute-start(bf16[128,512]{1,0:T(8,128)(2,1)S(1)} %get-tuple-element.42), channel_id=1, source_target_pairs={{0,508},{4,8},{8,4},{12,16},{16,12},{20,24},{24,20},{28,32},{32,28... | collective-permute-start | bytes 393224 | tf_op jit(solution)/shard_map/ppermute | solution.py:319
  50.0 1.9 %collective-permute-start.7 = (bf16[128,512]{1,0:T(8,128)(2,1)S(1)}, bf16[128,512]{1,0:T(8,128)(2,1)S(1)}, u32[]{:S(2)}, u32[]{:S(2)}) collective-permute-start(bf16[128,512]{1,0:T(8,128)(2,1)S(1)} %get-tuple-element.44), channel_id=1, source_target_pairs={{0,504},{4,12},{8,0},{12,20},{16,8},{20,28},{24,16},{28,36},{32,24... | collective-permute-start | bytes 393224 | tf_op jit(solution)/shard_map/ppermute | solution.py:323
  51.9 0.0 collective-permute-done.5
  51.9 0.7 %collective-permute-done.6 = bf16[128,512]{1,0:T(8,128)(2,1)S(1)} collective-permute-done((bf16[128,512]{1,0:T(8,128)(2,1)S(1)}, bf16[128,512]{1,0:T(8,128)(2,1)S(1)}, u32[]{:S(2)}, u32[]{:S(2)}) %collective-permute-start.6) | collective-permute-done | bytes 131104 | tf_op jit(solution)/shard_map/ppermute | solution.py:319
  52.6 6.4 %collective-permute-done.7 = bf16[128,512]{1,0:T(8,128)(2,1)S(1)} collective-permute-done((bf16[128,512]{1,0:T(8,128)(2,1)S(1)}, bf16[128,512]{1,0:T(8,128)(2,1)S(1)}, u32[]{:S(2)}, u32[]{:S(2)}) %collective-permute-start.7) | collective-permute-done | bytes 131104 | tf_op jit(solution)/shard_map/ppermute | solution.py:323
  59.0 0.9 %maximum_select_fusion.1 = bf16[1,1,4,128,512]{4,3,2,1,0:T(8,128)(2,1)} fusion(bf16[1,1,1,128,512]{4,3,2,1,0:T(8,128)(2,1)S(1)} %bitcast.16, bf16[1,1,1,128,512]{4,3,2,1,0:T(8,128)(2,1)S(1)} %get-tuple-element.43, bf16[1,1,1,128,512]{4,3,2,1,0:T(8,128)(2,1)S(1)} %bitcast.15, bf16[1,1,1,128,512]{4,3,2,1,0:T(8,128)(2,1)S(1)} %bitcast.14, pred[]{:T(512)S(6)} %eq.19), kind=kLoop, calls=%fused_computation.1 | loop fusion | flops 1835008 | bytes 1048577 | tf_op jit(solution)/shard_map/jit(_where)/select_n | solution.py:325
  (6 shorter events, 0.2 us)
Async XLA Ops:
  0.0 6.8 %copy-start.6 = (s32[64,1,8]{0,2,1:T(8,128)S(1)}, s32[64,1,8]{0,2,1:T(8,128)}, u32[]{:S(2)}) copy-start(s32[64,1,8]{0,2,1:T(8,128)} %param.15) | copy-start | bytes 6148
  0.0 7.0 %copy-start.7 = (f32[64]{0:T(128)S(1)}, f32[64]{0:T(128)}, u32[]{:S(2)}) copy-start(f32[64]{0:T(128)} %param.12) | copy-start | bytes 772
  0.0 7.1 %copy-start.5 = (f32[128]{0:T(128)S(1)}, f32[128]{0:T(128)}, u32[]{:S(2)}) copy-start(f32[128]{0:T(128)} %param.14) | copy-start | bytes 1540
  0.0 7.1 %copy-start.4 = (bf16[8,64,128]{2,1,0:T(8,128)(2,1)S(1)}, bf16[8,64,128]{2,1,0:T(8,128)(2,1)}, u32[]{:S(2)}) copy-start(bf16[8,64,128]{2,1,0:T(8,128)(2,1)} %dw.1) | copy-start | bytes 393220
  0.0 7.1 %copy-start.3 = (bf16[3,3,3,64,64]{4,3,2,1,0:T(8,128)(2,1)S(1)}, bf16[3,3,3,64,64]{4,3,2,1,0:T(8,128)(2,1)}, u32[]{:S(2)}) copy-start(bf16[3,3,3,64,64]{4,3,2,1,0:T(8,128)(2,1)} %cw.1) | copy-start | bytes 663556
  2.0 7.5 %collective-permute-start = (bf16[8,64,128]{2,1,0:T(8,128)(2,1)S(1)}, bf16[8,64,128]{2,1,0:T(8,128)(2,1)S(1)}, u32[]{:S(2)}, u32[]{:S(2)}) collective-permute-start(bf16[8,64,128]{2,1,0:T(8,128)(2,1)S(1)} %get-tuple-element.23), channel_id=1, source_target_pairs={{0,1},{2,3},{1,0},{3,2},{4,5},{6,7},{5,4},{7,6},{8,9},{10,11},{9,8... | collective-permute-start | bytes 393224 | tf_op jit(solution)/shard_map/ppermute | solution.py:283
  4.8 5.7 %collective-permute-start.1 = (bf16[8,64,128]{2,1,0:T(8,128)(2,1)S(1)}, bf16[8,64,128]{2,1,0:T(8,128)(2,1)S(1)}, u32[]{:S(2)}, u32[]{:S(2)}) collective-permute-start(bf16[8,64,128]{2,1,0:T(8,128)(2,1)S(1)} %get-tuple-element.24), channel_id=1, source_target_pairs={{1,2},{2,1},{5,6},{6,5},{9,10},{10,9},{13,14},{14,13},{17,18},{18,... | collective-permute-start | bytes 393224 | tf_op jit(solution)/shard_map/ppermute | solution.py:284
  7.1 12.7 %copy-start = (bf16[8,16,64,128]{3,2,1,0:T(8,128)(2,1)S(1)}, bf16[8,16,64,128]{3,2,1,0:T(8,128)(2,1)}, u32[]{:S(2)}) copy-start(bf16[8,16,64,128]{3,2,1,0:T(8,128)(2,1)} %vox.7) | copy-start | bytes 6291460
  7.1 12.7 %copy-start.1 = (s32[8,16]{1,0:T(8,128)S(1)}, s32[8,16]{1,0:T(8,128)}, u32[]{:S(2)}) copy-start(s32[8,16]{1,0:T(8,128)} %lo.7) | copy-start | bytes 1540
  7.1 12.7 %copy-start.2 = (s32[8,16]{1,0:T(8,128)S(1)}, s32[8,16]{1,0:T(8,128)}, u32[]{:S(2)}) copy-start(s32[8,16]{1,0:T(8,128)} %hi.7) | copy-start | bytes 1540
  10.6 15.6 %collective-permute-start.2 = (bf16[18,64,128]{2,1,0:T(8,128)(2,1)S(1)}, bf16[18,64,128]{2,1,0:T(8,128)(2,1)S(1)}, u32[]{:S(2)}, u32[]{:S(2)}) collective-permute-start(bf16[18,64,128]{2,1,0:T(8,128)(2,1)S(1)} %pad_maximum_fusion), channel_id=1, source_target_pairs={{0,4},{8,12},{16,20},{24,28},{32,36},{40,44},{48,52},{56,60},{64,6... | collective-permute-start | bytes 884744 | tf_op jit(solution)/shard_map/ppermute | solution.py:297
  17.9 8.4 %collective-permute-start.3 = (bf16[18,64,128]{2,1,0:T(8,128)(2,1)S(1)}, bf16[18,64,128]{2,1,0:T(8,128)(2,1)S(1)}, u32[]{:S(2)}, u32[]{:S(2)}) collective-permute-start(bf16[18,64,128]{2,1,0:T(8,128)(2,1)S(1)} %pad_maximum_fusion.1), channel_id=1, source_target_pairs={{4,8},{12,16},{20,24},{28,32},{36,40},{44,48},{52,56},{60,64},{68,... | collective-permute-start | bytes 884744 | tf_op jit(solution)/shard_map/ppermute | solution.py:298
  32.7 3.4 %collective-permute-start.4 = (bf16[4,128,256]{2,1,0:T(8,128)(2,1)S(1)}, bf16[4,128,256]{2,1,0:T(8,128)(2,1)S(1)}, u32[]{:S(2)}, u32[]{:S(2)}) collective-permute-start(bf16[4,128,256]{2,1,0:T(8,128)(2,1)S(1)} %get-tuple-element.40), channel_id=1, source_target_pairs={{0,4},{4,0},{8,12},{12,8},{16,20},{20,16},{24,28},{28,24},{32,36},... | collective-permute-start | bytes 786440 | tf_op jit(solution)/shard_map/ppermute | solution.py:309
  36.3 15.6 %collective-permute-start.5 = (bf16[128,512]{1,0:T(8,128)(2,1)S(1)}, bf16[128,512]{1,0:T(8,128)(2,1)S(1)}, u32[]{:S(2)}, u32[]{:S(2)}) collective-permute-start(bf16[128,512]{1,0:T(8,128)(2,1)S(1)} %get-tuple-element.41), channel_id=1, source_target_pairs={{0,500},{4,16},{8,508},{12,24},{16,4},{20,32},{24,12},{28,40},{32,... | collective-permute-start | bytes 393224 | tf_op jit(solution)/shard_map/ppermute | solution.py:321
  38.9 13.7 %collective-permute-start.6 = (bf16[128,512]{1,0:T(8,128)(2,1)S(1)}, bf16[128,512]{1,0:T(8,128)(2,1)S(1)}, u32[]{:S(2)}, u32[]{:S(2)}) collective-permute-start(bf16[128,512]{1,0:T(8,128)(2,1)S(1)} %get-tuple-element.42), channel_id=1, source_target_pairs={{0,508},{4,8},{8,4},{12,16},{16,12},{20,24},{24,20},{28,32},{32,28... | collective-permute-start | bytes 393224 | tf_op jit(solution)/shard_map/ppermute | solution.py:319
  50.0 9.1 %collective-permute-start.7 = (bf16[128,512]{1,0:T(8,128)(2,1)S(1)}, bf16[128,512]{1,0:T(8,128)(2,1)S(1)}, u32[]{:S(2)}, u32[]{:S(2)}) collective-permute-start(bf16[128,512]{1,0:T(8,128)(2,1)S(1)} %get-tuple-element.44), channel_id=1, source_target_pairs={{0,504},{4,12},{8,0},{12,20},{16,8},{20,28},{24,16},{28,36},{32,24... | collective-permute-start | bytes 393224 | tf_op jit(solution)/shard_map/ppermute | solution.py:323

commit v8 on v7

--- a/solution.py
+++ b/solution.py
@@ -96,16 +96,20 @@
     )
 
 
-def faces_kernel(side, lo, hi, vox, y_one, y_two, sems):
-    odd = side[0] >> 1
-    y_at = (jnp.where(odd == 1, 0, 15), jnp.where(odd == 1, 15, 0))
+def faces_kernel(lo_all, hi_all, vox, y_first, y_last, lo, hi, sems):
+    bounds = [
+        pltpu.make_async_copy(lo_all, lo, sems.at[0]),
+        pltpu.make_async_copy(hi_all, hi, sems.at[1]),
+    ]
     copies = [
-        pltpu.make_async_copy(vox.at[:, y_at[k]], ref, sems.at[k])
-        for k, ref in enumerate((y_one, y_two))
+        pltpu.make_async_copy(vox.at[:, 0], y_first, sems.at[2]),
+        pltpu.make_async_copy(vox.at[:, 15], y_last, sems.at[3]),
     ]
-    for copy in copies:
+    for copy in bounds + copies:
         copy.start()
-    for copy, ref, y in zip(copies, (y_one, y_two), y_at):
+    for copy in bounds:
+        copy.wait()
+    for copy, ref, y in zip(copies, (y_first, y_last), (0, 15)):
         copy.wait()
         for x in range(8):
             ref[x] = masked_column(ref[x], lo, hi, x, y)
@@ -115,19 +119,22 @@
     return tuple(pltpu.with_memory_space_constraint(a, pltpu.HBM) for a in arrays)
 
 
-def faces(side, lo, hi, vox):
+def faces(lo, hi, vox):
     y_face = jax.ShapeDtypeStruct((8, 64, 128), BF)
-    smem = pl.BlockSpec(memory_space=SMEM)
     vmem = pl.BlockSpec(memory_space=VMEM)
     return pl.pallas_call(
         faces_kernel,
         out_shape=(y_face, y_face),
-        in_specs=[smem] * 3 + [pl.BlockSpec(memory_space=pltpu.HBM)],
+        in_specs=[pl.BlockSpec(memory_space=pltpu.HBM)] * 3,
         out_specs=(vmem, vmem),
-        scratch_shapes=[pltpu.SemaphoreType.DMA((2,))],
+        scratch_shapes=[
+            SMEM((8, 16), jnp.int32),
+            SMEM((8, 16), jnp.int32),
+            pltpu.SemaphoreType.DMA((4,)),
+        ],
         compiler_params=small_vmem(4),
         name="faces",
-    )(side, *in_place(lo, hi, vox))
+    )(*in_place(lo, hi, vox))
 
 
 def scene_rows(starts, lo, hi, pad, w, d, cb, db, sel, cells):
@@ -279,7 +286,9 @@
         lower = range(first, count - 1, 2)
         return [(i, i + 1) for i in lower] + [(i + 1, i) for i in lower]
 
-    y_one, y_two = faces(side, shell_lo, shell_hi, voxels)
+    y_first, y_last = faces(shell_lo, shell_hi, voxels)
+    y_one = jnp.where(grp_odd == 1, y_first, y_last)
+    y_two = jnp.where(grp_odd == 1, y_last, y_first)
     y_one = lax.ppermute(y_one, "grp", swaps(grp_n, 0))
     y_two = lax.ppermute(y_two, "grp", swaps(grp_n, 1))
     x_one, x_two, *tables = prep(

time: 60.3 us -> 60.4 us (level)
  the two profiles are of different devices: /device:TPU:5 before, /device:TPU:1 now
where the time goes in v8:
time: 60.4 us; the launch traced here: 60 us
  starting transfers between devices  33.2 us (55%)
  Pallas kernels  16.3 us (27%)
  waiting for transfers between devices  8.64 us (14%)
  other arithmetic  1.41 us (2%)
    ppermute x1, starting transfers between devices, local(): one = lax.ppermute(mine(2, 1), 'blk', pairs)  11.1 us
    pallas_call x1, Pallas kernels, outer_rows(): pl.pallas_call(outer_kernel, out_shape=(half, half), in_specs=[smem] * 4...  6.5 us
    ppermute x1, starting transfers between devices, local(): x_one = lax.ppermute(x_message(x_one, core == 0), 'blk', swaps(blk_n, 0))  6.46 us
    ppermute x1, waiting for transfers between devices, local(): two = lax.ppermute(mine(1, 2), 'blk', pairs)  6.43 us
    ppermute x1, starting transfers between devices, local(): y_one = lax.ppermute(y_one, 'grp', swaps(grp_n, 0))  6.39 us
    pallas_call x1, Pallas kernels, inner_rows(): pl.pallas_call(inner_kernel, out_shape=jax.ShapeDtypeStruct((256, 512), F...  6.38 us
    ppermute x1, starting transfers between devices, local(): three = lax.ppermute(mine(0, 3), 'blk', pairs)  2.88 us
    pallas_call x1, Pallas kernels, prep(): pl.pallas_call(prep_kernel, out_shape=(x_face, x_face, jax.ShapeDtypeStru...  2.3 us
  transfers between devices with their start and end apart: 8, of which 3 were waited for; matrix products, arithmetic and copies ran while one was open for 1% of the time, Pallas kernels for 14%

profile of v8, /device:TPU:1, one launch (start us, length us, event | category | flops | bytes accessed | tf_op | source)
XLA Modules:
  0.0 60.0 jit_solution(10460524141433594378)
XLA Ops:
  0.0 0.0 copy-start.6
  0.0 0.0 copy-start.7
  0.0 0.0 copy-start.5
  0.0 0.0 copy-start.4
  0.0 0.0 copy-start.3
  0.0 1.1 %faces.1 = (bf16[8,64,128]{2,1,0:T(8,128)(2,1)S(1)}, bf16[8,64,128]{2,1,0:T(8,128)(2,1)S(1)}) custom-call(s32[8,16]{1,0:T(8,128)} %lo.5, s32[8,16]{1,0:T(8,128)} %hi.5, bf16[8,16,64,128]{3,2,1,0:T(8,128)(2,1)} %vox.7), custom_call_target="tpu_custom_call" | custom-call | tf_op jit(solution)/shard_map/faces/pallas_call | solution.py:125
  1.2 0.7 %collective-permute-start.1 = (bf16[8,64,128]{2,1,0:T(8,128)(2,1)S(1)}, bf16[8,64,128]{2,1,0:T(8,128)(2,1)S(1)}, u32[]{:S(2)}, u32[]{:S(2)}) collective-permute-start(bf16[8,64,128]{2,1,0:T(8,128)(2,1)S(1)} %get-tuple-element.49), channel_id=1, source_target_pairs={{1,2},{2,1},{5,6},{6,5},{9,10},{10,9},{13,14},{14,13},{17,18},{18,... | collective-permute-start | bytes 393224 | tf_op jit(solution)/shard_map/ppermute | solution.py:293
  1.9 6.4 %collective-permute-start = (bf16[8,64,128]{2,1,0:T(8,128)(2,1)S(1)}, bf16[8,64,128]{2,1,0:T(8,128)(2,1)S(1)}, u32[]{:S(2)}, u32[]{:S(2)}) collective-permute-start(bf16[8,64,128]{2,1,0:T(8,128)(2,1)S(1)} %get-tuple-element.50), channel_id=1, source_target_pairs={{0,1},{2,3},{1,0},{3,2},{4,5},{6,7},{5,4},{7,6},{8,9},{10,11},{9,8... | collective-permute-start | bytes 393224 | tf_op jit(solution)/shard_map/ppermute | solution.py:292
  8.3 0.0 copy-done.6
  8.3 0.2 add_reduce_fusion
  8.5 0.0 copy-done.7
  8.5 0.1 broadcast_in_dim_tile.3.cb
  8.6 0.0 copy-done.5
  8.6 0.0 copy-done.4
  8.6 0.0 copy-done.3
  8.6 0.0 copy-start
  8.6 0.0 copy-start.1
  8.7 0.0 copy-start.2
  8.7 2.3 %prep.1 = (bf16[16,64,128]{2,1,0:T(8,128)(2,1)S(1)}, bf16[16,64,128]{2,1,0:T(8,128)(2,1)S(1)}, bf16[384,768]{1,0:T(8,128)(2,1)S(1)}, bf16[256,256]{1,0:T(8,128)(...) custom-call(s32[1]{0:T(128)} %bitcast.side, s32[8,16]{1,0:T(8,128)} %lo.5, ...), custom_call_target="tpu_custom_call" | custom-call | flops 1000000000 | bytes 4000000 | tf_op jit(solution)/shard_map/prep/pallas_call | solution.py:72
  11.0 0.0 collective-permute-done.1.y_two
  11.0 0.0 collective-permute-done.y_one
  11.1 6.5 %collective-permute-start.2 = (bf16[18,64,128]{2,1,0:T(8,128)(2,1)S(1)}, bf16[18,64,128]{2,1,0:T(8,128)(2,1)S(1)}, u32[]{:S(2)}, u32[]{:S(2)}) collective-permute-start(bf16[18,64,128]{2,1,0:T(8,128)(2,1)S(1)} %pad_maximum_fusion), channel_id=1, source_target_pairs={{0,4},{8,12},{16,20},{24,28},{32,36},{40,44},{48,52},{56,60},{64,6... | collective-permute-start | bytes 884744 | tf_op jit(solution)/shard_map/ppermute | solution.py:306
  17.6 1.9 %collective-permute-start.3 = (bf16[18,64,128]{2,1,0:T(8,128)(2,1)S(1)}, bf16[18,64,128]{2,1,0:T(8,128)(2,1)S(1)}, u32[]{:S(2)}, u32[]{:S(2)}) collective-permute-start(bf16[18,64,128]{2,1,0:T(8,128)(2,1)S(1)} %pad_maximum_fusion.1), channel_id=1, source_target_pairs={{4,8},{12,16},{20,24},{28,32},{36,40},{44,48},{52,56},{60,64},{68,... | collective-permute-start | bytes 884744 | tf_op jit(solution)/shard_map/ppermute | solution.py:307
  19.5 0.0 copy-done
  19.5 0.0 copy-done.1
  19.5 0.0 copy-done.2
  19.5 6.4 %inner.1 = f32[256,512]{1,0:T(8,128)S(1)} custom-call(s32[1]{0:T(128)} %bitcast.side, s32[8,16]{1,0:T(8,128)S(1)} %copy-done.1, s32[8,16]{1,0:T(8,128)S(1)} %copy-done.2, bf16[8,16,64,128]{3,2,1,0:T(8,128)(2,1)S(1)} %copy-done, bf16[8,64,128]{2,1,0:T(8,128)(2,1)S(1)} %collective-permute-done.y_one, bf16[8,64,128]{2,1,0:T(8,128)(2,1)S(1)} %collective-permute-done.1.y_two, ...), custom_call_target="tpu_custom_call" | custom-call | flops 5000000000 | bytes 4000000 | tf_op jit(solution)/shard_map/inner/pallas_call | solution.py:241
  25.9 0.0 collective-permute-done.2.x_one
  25.9 0.0 collective-permute-done.3.x_two
  26.0 6.5 %outer.1 = (bf16[4,128,256]{2,1,0:T(8,128)(2,1)S(1)}, bf16[4,128,256]{2,1,0:T(8,128)(2,1)S(1)}) custom-call(s32[1]{0:T(128)} %bitcast.side, s32[8,16]{1,0:T(8,128)S(1)} %copy-done.1, s32[8,16]{1,0:T(8,128)S(1)} %copy-done.2, s32[8]{0:T(128)S(1)} %and_select_fusion.slots, bf16[8,16,64,128]{3,2,1,0:T(8,128)(2,1)S(1)} %copy-done, ...), custom_call_target="tpu_custom_call" | custom-call | tf_op jit(solution)/shard_map/outer/pallas_call | solution.py:257
  32.5 1.9 %collective-permute-start.4 = (bf16[4,128,256]{2,1,0:T(8,128)(2,1)S(1)}, bf16[4,128,256]{2,1,0:T(8,128)(2,1)S(1)}, u32[]{:S(2)}, u32[]{:S(2)}) collective-permute-start(bf16[4,128,256]{2,1,0:T(8,128)(2,1)S(1)} %get-tuple-element.40), channel_id=1, source_target_pairs={{0,4},{4,0},{8,12},{12,8},{16,20},{20,16},{24,28},{28,24},{32,36},... | collective-permute-start | bytes 786440 | tf_op jit(solution)/shard_map/ppermute | solution.py:318
  34.4 1.5 %collective-permute-done.4 = bf16[4,128,256]{2,1,0:T(8,128)(2,1)S(1)} collective-permute-done((bf16[4,128,256]{2,1,0:T(8,128)(2,1)S(1)}, bf16[4,128,256]{2,1,0:T(8,128)(2,1)S(1)}, u32[]{:S(2)}, u32[]{:S(2)}) %collective-permute-start.4) | collective-permute-done | bytes 262176 | tf_op jit(solution)/shard_map/ppermute | solution.py:318
  35.9 0.1 maximum_select_fusion
  36.1 2.9 %collective-permute-start.5 = (bf16[128,512]{1,0:T(8,128)(2,1)S(1)}, bf16[128,512]{1,0:T(8,128)(2,1)S(1)}, u32[]{:S(2)}, u32[]{:S(2)}) collective-permute-start(bf16[128,512]{1,0:T(8,128)(2,1)S(1)} %get-tuple-element.41), channel_id=1, source_target_pairs={{0,500},{4,16},{8,508},{12,24},{16,4},{20,32},{24,12},{28,40},{32,... | collective-permute-start | bytes 393224 | tf_op jit(solution)/shard_map/ppermute | solution.py:330
  39.0 11.1 %collective-permute-start.6 = (bf16[128,512]{1,0:T(8,128)(2,1)S(1)}, bf16[128,512]{1,0:T(8,128)(2,1)S(1)}, u32[]{:S(2)}, u32[]{:S(2)}) collective-permute-start(bf16[128,512]{1,0:T(8,128)(2,1)S(1)} %get-tuple-element.42), channel_id=1, source_target_pairs={{0,508},{4,8},{8,4},{12,16},{16,12},{20,24},{24,20},{28,32},{32,28... | collective-permute-start | bytes 393224 | tf_op jit(solution)/shard_map/ppermute | solution.py:328
  50.0 1.9 %collective-permute-start.7 = (bf16[128,512]{1,0:T(8,128)(2,1)S(1)}, bf16[128,512]{1,0:T(8,128)(2,1)S(1)}, u32[]{:S(2)}, u32[]{:S(2)}) collective-permute-start(bf16[128,512]{1,0:T(8,128)(2,1)S(1)} %get-tuple-element.44), channel_id=1, source_target_pairs={{0,504},{4,12},{8,0},{12,20},{16,8},{20,28},{24,16},{28,36},{32,24... | collective-permute-start | bytes 393224 | tf_op jit(solution)/shard_map/ppermute | solution.py:332
  52.0 0.0 collective-permute-done.5
  52.0 0.7 %collective-permute-done.6 = bf16[128,512]{1,0:T(8,128)(2,1)S(1)} collective-permute-done((bf16[128,512]{1,0:T(8,128)(2,1)S(1)}, bf16[128,512]{1,0:T(8,128)(2,1)S(1)}, u32[]{:S(2)}, u32[]{:S(2)}) %collective-permute-start.6) | collective-permute-done | bytes 131104 | tf_op jit(solution)/shard_map/ppermute | solution.py:328
  52.7 6.4 %collective-permute-done.7 = bf16[128,512]{1,0:T(8,128)(2,1)S(1)} collective-permute-done((bf16[128,512]{1,0:T(8,128)(2,1)S(1)}, bf16[128,512]{1,0:T(8,128)(2,1)S(1)}, u32[]{:S(2)}, u32[]{:S(2)}) %collective-permute-start.7) | collective-permute-done | bytes 131104 | tf_op jit(solution)/shard_map/ppermute | solution.py:332
  59.1 0.9 %maximum_select_fusion.1 = bf16[1,1,4,128,512]{4,3,2,1,0:T(8,128)(2,1)} fusion(bf16[1,1,1,128,512]{4,3,2,1,0:T(8,128)(2,1)S(1)} %bitcast.16, bf16[1,1,1,128,512]{4,3,2,1,0:T(8,128)(2,1)S(1)} %get-tuple-element.43, bf16[1,1,1,128,512]{4,3,2,1,0:T(8,128)(2,1)S(1)} %bitcast.15, bf16[1,1,1,128,512]{4,3,2,1,0:T(8,128)(2,1)S(1)} %bitcast.14, pred[]{:T(512)S(6)} %eq.12), kind=kLoop, calls=%fused_computation.1 | loop fusion | flops 1835008 | bytes 1048577 | tf_op jit(solution)/shard_map/jit(_where)/select_n | solution.py:334
  (7 shorter events, 0.2 us)
Async XLA Ops:
  0.0 8.3 %copy-start.6 = (s32[64,1,8]{0,2,1:T(8,128)S(1)}, s32[64,1,8]{0,2,1:T(8,128)}, u32[]{:S(2)}) copy-start(s32[64,1,8]{0,2,1:T(8,128)} %param.15) | copy-start | bytes 6148
  0.0 8.5 %copy-start.7 = (f32[64]{0:T(128)S(1)}, f32[64]{0:T(128)}, u32[]{:S(2)}) copy-start(f32[64]{0:T(128)} %param.12) | copy-start | bytes 772
  0.0 8.6 %copy-start.5 = (f32[128]{0:T(128)S(1)}, f32[128]{0:T(128)}, u32[]{:S(2)}) copy-start(f32[128]{0:T(128)} %param.14) | copy-start | bytes 1540
  0.0 8.6 %copy-start.4 = (bf16[8,64,128]{2,1,0:T(8,128)(2,1)S(1)}, bf16[8,64,128]{2,1,0:T(8,128)(2,1)}, u32[]{:S(2)}) copy-start(bf16[8,64,128]{2,1,0:T(8,128)(2,1)} %dw.1) | copy-start | bytes 393220
  0.0 8.6 %copy-start.3 = (bf16[3,3,3,64,64]{4,3,2,1,0:T(8,128)(2,1)S(1)}, bf16[3,3,3,64,64]{4,3,2,1,0:T(8,128)(2,1)}, u32[]{:S(2)}) copy-start(bf16[3,3,3,64,64]{4,3,2,1,0:T(8,128)(2,1)} %cw.1) | copy-start | bytes 663556
  1.2 9.8 %collective-permute-start.1 = (bf16[8,64,128]{2,1,0:T(8,128)(2,1)S(1)}, bf16[8,64,128]{2,1,0:T(8,128)(2,1)S(1)}, u32[]{:S(2)}, u32[]{:S(2)}) collective-permute-start(bf16[8,64,128]{2,1,0:T(8,128)(2,1)S(1)} %get-tuple-element.49), channel_id=1, source_target_pairs={{1,2},{2,1},{5,6},{6,5},{9,10},{10,9},{13,14},{14,13},{17,18},{18,... | collective-permute-start | bytes 393224 | tf_op jit(solution)/shard_map/ppermute | solution.py:293
  1.9 9.1 %collective-permute-start = (bf16[8,64,128]{2,1,0:T(8,128)(2,1)S(1)}, bf16[8,64,128]{2,1,0:T(8,128)(2,1)S(1)}, u32[]{:S(2)}, u32[]{:S(2)}) collective-permute-start(bf16[8,64,128]{2,1,0:T(8,128)(2,1)S(1)} %get-tuple-element.50), channel_id=1, source_target_pairs={{0,1},{2,3},{1,0},{3,2},{4,5},{6,7},{5,4},{7,6},{8,9},{10,11},{9,8... | collective-permute-start | bytes 393224 | tf_op jit(solution)/shard_map/ppermute | solution.py:292
  8.6 10.9 %copy-start = (bf16[8,16,64,128]{3,2,1,0:T(8,128)(2,1)S(1)}, bf16[8,16,64,128]{3,2,1,0:T(8,128)(2,1)}, u32[]{:S(2)}) copy-start(bf16[8,16,64,128]{3,2,1,0:T(8,128)(2,1)} %vox.7) | copy-start | bytes 6291460
  8.6 10.9 %copy-start.1 = (s32[8,16]{1,0:T(8,128)S(1)}, s32[8,16]{1,0:T(8,128)}, u32[]{:S(2)}) copy-start(s32[8,16]{1,0:T(8,128)} %lo.5) | copy-start | bytes 1540
  8.7 10.9 %copy-start.2 = (s32[8,16]{1,0:T(8,128)S(1)}, s32[8,16]{1,0:T(8,128)}, u32[]{:S(2)}) copy-start(s32[8,16]{1,0:T(8,128)} %hi.5) | copy-start | bytes 1540
  11.1 14.9 %collective-permute-start.2 = (bf16[18,64,128]{2,1,0:T(8,128)(2,1)S(1)}, bf16[18,64,128]{2,1,0:T(8,128)(2,1)S(1)}, u32[]{:S(2)}, u32[]{:S(2)}) collective-permute-start(bf16[18,64,128]{2,1,0:T(8,128)(2,1)S(1)} %pad_maximum_fusion), channel_id=1, source_target_pairs={{0,4},{8,12},{16,20},{24,28},{32,36},{40,44},{48,52},{56,60},{64,6... | collective-permute-start | bytes 884744 | tf_op jit(solution)/shard_map/ppermute | solution.py:306
  17.6 8.4 %collective-permute-start.3 = (bf16[18,64,128]{2,1,0:T(8,128)(2,1)S(1)}, bf16[18,64,128]{2,1,0:T(8,128)(2,1)S(1)}, u32[]{:S(2)}, u32[]{:S(2)}) collective-permute-start(bf16[18,64,128]{2,1,0:T(8,128)(2,1)S(1)} %pad_maximum_fusion.1), channel_id=1, source_target_pairs={{4,8},{12,16},{20,24},{28,32},{36,40},{44,48},{52,56},{60,64},{68,... | collective-permute-start | bytes 884744 | tf_op jit(solution)/shard_map/ppermute | solution.py:307
  32.5 3.4 %collective-permute-start.4 = (bf16[4,128,256]{2,1,0:T(8,128)(2,1)S(1)}, bf16[4,128,256]{2,1,0:T(8,128)(2,1)S(1)}, u32[]{:S(2)}, u32[]{:S(2)}) collective-permute-start(bf16[4,128,256]{2,1,0:T(8,128)(2,1)S(1)} %get-tuple-element.40), channel_id=1, source_target_pairs={{0,4},{4,0},{8,12},{12,8},{16,20},{20,16},{24,28},{28,24},{32,36},... | collective-permute-start | bytes 786440 | tf_op jit(solution)/shard_map/ppermute | solution.py:318
  36.1 15.9 %collective-permute-start.5 = (bf16[128,512]{1,0:T(8,128)(2,1)S(1)}, bf16[128,512]{1,0:T(8,128)(2,1)S(1)}, u32[]{:S(2)}, u32[]{:S(2)}) collective-permute-start(bf16[128,512]{1,0:T(8,128)(2,1)S(1)} %get-tuple-element.41), channel_id=1, source_target_pairs={{0,500},{4,16},{8,508},{12,24},{16,4},{20,32},{24,12},{28,40},{32,... | collective-permute-start | bytes 393224 | tf_op jit(solution)/shard_map/ppermute | solution.py:330
  39.0 13.7 %collective-permute-start.6 = (bf16[128,512]{1,0:T(8,128)(2,1)S(1)}, bf16[128,512]{1,0:T(8,128)(2,1)S(1)}, u32[]{:S(2)}, u32[]{:S(2)}) collective-permute-start(bf16[128,512]{1,0:T(8,128)(2,1)S(1)} %get-tuple-element.42), channel_id=1, source_target_pairs={{0,508},{4,8},{8,4},{12,16},{16,12},{20,24},{24,20},{28,32},{32,28... | collective-permute-start | bytes 393224 | tf_op jit(solution)/shard_map/ppermute | solution.py:328
  50.0 9.1 %collective-permute-start.7 = (bf16[128,512]{1,0:T(8,128)(2,1)S(1)}, bf16[128,512]{1,0:T(8,128)(2,1)S(1)}, u32[]{:S(2)}, u32[]{:S(2)}) collective-permute-start(bf16[128,512]{1,0:T(8,128)(2,1)S(1)} %get-tuple-element.44), channel_id=1, source_target_pairs={{0,504},{4,12},{8,0},{12,20},{16,8},{20,28},{24,16},{28,36},{32,24... | collective-permute-start | bytes 393224 | tf_op jit(solution)/shard_map/ppermute | solution.py:332

commit v9 on v8

--- a/solution.py
+++ b/solution.py
@@ -190,12 +190,34 @@
     return jnp.dot(cells[...], sel[...], preferred_element_type=F32)
 
 
-def inner_kernel(side, lo, hi, vox, y_one, y_two, w, d, cb, db, sel, out, pad, cells):
+def fetch_bounds(lo_all, hi_all, lo, hi, sems):
+    copies = [
+        pltpu.make_async_copy(lo_all, lo, sems.at[0]),
+        pltpu.make_async_copy(hi_all, hi, sems.at[1]),
+    ]
+    for copy in copies:
+        copy.start()
+    return copies
+
+
+BOUNDS = [
+    SMEM((8, 16), jnp.int32),
+    SMEM((8, 16), jnp.int32),
+    pltpu.SemaphoreType.DMA((2,)),
+]
+
+
+def inner_kernel(
+    side, lo_all, hi_all, vox, y_one, y_two, w, d, cb, db, sel, out, pad, cells, lo, hi, sems
+):
+    bounds = fetch_bounds(lo_all, hi_all, lo, hi, sems)
     odd = side[0] >> 1
     one_at, two_at = 17 * (1 - odd), 17 * odd
     for r in range(6):
         pad[r, one_at] = y_one[r + 1]
         pad[r, two_at] = y_two[r + 1]
+    for copy in bounds:
+        copy.wait()
 
     @pl.loop(0, 6)
     def _(r):
@@ -206,8 +228,10 @@
 
 
 def outer_kernel(
-    side, lo, hi, slots, vox, y_one, y_two, x_one, x_two, inner, w, d, cb, db, sel, keep, give, pad, cells, pieces
+    side, lo_all, hi_all, slots, vox, y_one, y_two, x_one, x_two, inner, w, d, cb, db, sel,
+    keep, give, pad, cells, pieces, lo, hi, sems
 ):
+    bounds = fetch_bounds(lo_all, hi_all, lo, hi, sems)
     core, odd = side[0] & 1, side[0] >> 1
     one_at, two_at = 17 * (1 - odd), 17 * odd
     pad[7 * (1 - core)] = x_one[...]
@@ -217,6 +241,8 @@
         pad[r + 1, two_at] = y_two[r]
         pad[r + 4, one_at] = y_one[r + 5]
         pad[r + 4, two_at] = y_two[r + 5]
+    for copy in bounds:
+        copy.wait()
 
     @pl.loop(0, 3)
     def _(r):
@@ -241,9 +267,9 @@
     return pl.pallas_call(
         inner_kernel,
         out_shape=jax.ShapeDtypeStruct((256, 512), F32),
-        in_specs=[smem] * 3 + [vmem] * 8,
+        in_specs=[smem] + [pl.BlockSpec(memory_space=pl.ANY)] * 2 + [vmem] * 8,
         out_specs=vmem,
-        scratch_shapes=[VMEM((6, 18, 64, 128), BF), VMEM((256, 1024), BF)],
+        scratch_shapes=[VMEM((6, 18, 64, 128), BF), VMEM((256, 1024), BF), *BOUNDS],
         compiler_params=small_vmem(12),
         cost_estimate=pl.CostEstimate(flops=5 * 10**9, bytes_accessed=4 * 10**6, transcendentals=0),
         name="inner",
@@ -257,12 +283,13 @@
     return pl.pallas_call(
         outer_kernel,
         out_shape=(half, half),
-        in_specs=[smem] * 4 + [vmem] * 11,
+        in_specs=[smem] + [pl.BlockSpec(memory_space=pl.ANY)] * 2 + [smem] + [vmem] * 11,
         out_specs=(vmem, vmem),
         scratch_shapes=[
             VMEM((8, 18, 64, 128), BF),
             VMEM((256, 1024), BF),
             VMEM((8, 128, 256), BF),
+            *BOUNDS,
         ],
         compiler_params=small_vmem(12),
         name="outer",

time: 60.4 us -> 60.8 us (level)
  no operation moved by 1% of the time
where the time goes in v9:
time: 60.8 us; the launch traced here: 60.5 us
  starting transfers between devices  33.2 us (55%)
  Pallas kernels  16.8 us (28%)
  waiting for transfers between devices  8.64 us (14%)
  other arithmetic  1.41 us (2%)
    ppermute x1, starting transfers between devices, local(): one = lax.ppermute(mine(2, 1), 'blk', pairs)  11.1 us
    pallas_call x1, Pallas kernels, outer_rows(): pl.pallas_call(outer_kernel, out_shape=(half, half), in_specs=[smem] + [p...  6.98 us
    ppermute x1, starting transfers between devices, local(): x_one = lax.ppermute(x_message(x_one, core == 0), 'blk', swaps(blk_n, 0))  6.46 us
    ppermute x1, waiting for transfers between devices, local(): two = lax.ppermute(mine(1, 2), 'blk', pairs)  6.43 us
    ppermute x1, starting transfers between devices, local(): y_one = lax.ppermute(y_one, 'grp', swaps(grp_n, 0))  6.39 us
    pallas_call x1, Pallas kernels, inner_rows(): pl.pallas_call(inner_kernel, out_shape=jax.ShapeDtypeStruct((256, 512), F...  6.37 us
    ppermute x1, starting transfers between devices, local(): three = lax.ppermute(mine(0, 3), 'blk', pairs)  2.88 us
    pallas_call x1, Pallas kernels, prep(): pl.pallas_call(prep_kernel, out_shape=(x_face, x_face, jax.ShapeDtypeStru...  2.3 us
  transfers between devices with their start and end apart: 8, of which 3 were waited for; matrix products, arithmetic and copies ran while one was open for 1% of the time, Pallas kernels for 14%

profile of v9, /device:TPU:1, one launch (start us, length us, event | category | flops | bytes accessed | tf_op | source)
XLA Modules:
  0.0 60.5 jit_solution(12249542603675303505)
XLA Ops:
  0.0 0.0 copy-start.6
  0.0 0.0 copy-start.7
  0.0 0.0 copy-start.5
  0.0 0.0 copy-start.4
  0.0 0.0 copy-start.3
  0.0 1.1 %faces.1 = (bf16[8,64,128]{2,1,0:T(8,128)(2,1)S(1)}, bf16[8,64,128]{2,1,0:T(8,128)(2,1)S(1)}) custom-call(s32[8,16]{1,0:T(8,128)} %lo_all.5, s32[8,16]{1,0:T(8,128)} %hi_all.5, bf16[8,16,64,128]{3,2,1,0:T(8,128)(2,1)} %vox.7), custom_call_target="tpu_custom_call" | custom-call | tf_op jit(solution)/shard_map/faces/pallas_call | solution.py:125
  1.2 0.7 %collective-permute-start.1 = (bf16[8,64,128]{2,1,0:T(8,128)(2,1)S(1)}, bf16[8,64,128]{2,1,0:T(8,128)(2,1)S(1)}, u32[]{:S(2)}, u32[]{:S(2)}) collective-permute-start(bf16[8,64,128]{2,1,0:T(8,128)(2,1)S(1)} %get-tuple-element.49), channel_id=1, source_target_pairs={{1,2},{2,1},{5,6},{6,5},{9,10},{10,9},{13,14},{14,13},{17,18},{18,... | collective-permute-start | bytes 393224 | tf_op jit(solution)/shard_map/ppermute | solution.py:320
  1.9 6.4 %collective-permute-start = (bf16[8,64,128]{2,1,0:T(8,128)(2,1)S(1)}, bf16[8,64,128]{2,1,0:T(8,128)(2,1)S(1)}, u32[]{:S(2)}, u32[]{:S(2)}) collective-permute-start(bf16[8,64,128]{2,1,0:T(8,128)(2,1)S(1)} %get-tuple-element.50), channel_id=1, source_target_pairs={{0,1},{2,3},{1,0},{3,2},{4,5},{6,7},{5,4},{7,6},{8,9},{10,11},{9,8... | collective-permute-start | bytes 393224 | tf_op jit(solution)/shard_map/ppermute | solution.py:319
  8.3 0.0 copy-done.6
  8.3 0.2 add_reduce_fusion
  8.5 0.0 copy-done.7
  8.5 0.1 broadcast_in_dim_tile.3.cb
  8.6 0.0 copy-done.5
  8.6 0.0 copy-done.4
  8.6 0.0 copy-done.3
  8.6 0.0 copy-start
  8.6 0.0 copy-start.1
  8.7 0.0 copy-start.2
  8.7 2.3 %prep.1 = (bf16[16,64,128]{2,1,0:T(8,128)(2,1)S(1)}, bf16[16,64,128]{2,1,0:T(8,128)(2,1)S(1)}, bf16[384,768]{1,0:T(8,128)(2,1)S(1)}, bf16[256,256]{1,0:T(8,128)(...) custom-call(s32[1]{0:T(128)} %bitcast.side, s32[8,16]{1,0:T(8,128)} %lo_all.5, ...), custom_call_target="tpu_custom_call" | custom-call | flops 1000000000 | bytes 4000000 | tf_op jit(solution)/shard_map/prep/pallas_call | solution.py:72
  11.0 0.0 collective-permute-done.1.y_two
  11.0 0.0 collective-permute-done.y_one
  11.1 6.5 %collective-permute-start.2 = (bf16[18,64,128]{2,1,0:T(8,128)(2,1)S(1)}, bf16[18,64,128]{2,1,0:T(8,128)(2,1)S(1)}, u32[]{:S(2)}, u32[]{:S(2)}) collective-permute-start(bf16[18,64,128]{2,1,0:T(8,128)(2,1)S(1)} %pad_maximum_fusion), channel_id=1, source_target_pairs={{0,4},{8,12},{16,20},{24,28},{32,36},{40,44},{48,52},{56,60},{64,6... | collective-permute-start | bytes 884744 | tf_op jit(solution)/shard_map/ppermute | solution.py:333
  17.6 1.9 %collective-permute-start.3 = (bf16[18,64,128]{2,1,0:T(8,128)(2,1)S(1)}, bf16[18,64,128]{2,1,0:T(8,128)(2,1)S(1)}, u32[]{:S(2)}, u32[]{:S(2)}) collective-permute-start(bf16[18,64,128]{2,1,0:T(8,128)(2,1)S(1)} %pad_maximum_fusion.1), channel_id=1, source_target_pairs={{4,8},{12,16},{20,24},{28,32},{36,40},{44,48},{52,56},{60,64},{68,... | collective-permute-start | bytes 884744 | tf_op jit(solution)/shard_map/ppermute | solution.py:334
  19.5 0.0 copy-done
  19.5 0.0 copy-done.1
  19.5 0.0 copy-done.2
  19.5 6.4 %inner.1 = f32[256,512]{1,0:T(8,128)S(1)} custom-call(s32[1]{0:T(128)} %bitcast.side, s32[8,16]{1,0:T(8,128)S(1)} %copy-done.1, s32[8,16]{1,0:T(8,128)S(1)} %copy-done.2, bf16[8,16,64,128]{3,2,1,0:T(8,128)(2,1)S(1)} %copy-done, bf16[8,64,128]{2,1,0:T(8,128)(2,1)S(1)} %collective-permute-done.y_one, bf16[8,64,128]{2,1,0:T(8,128)(2,1)S(1)} %collective-permute-done.1.y_two, ...), custom_call_target="tpu_custom_call" | custom-call | flops 5000000000 | bytes 4000000 | tf_op jit(solution)/shard_map/inner/pallas_call | solution.py:267
  25.9 0.0 collective-permute-done.2.x_one
  25.9 0.0 collective-permute-done.3.x_two
  26.0 7.0 %outer.1 = (bf16[4,128,256]{2,1,0:T(8,128)(2,1)S(1)}, bf16[4,128,256]{2,1,0:T(8,128)(2,1)S(1)}) custom-call(s32[1]{0:T(128)} %bitcast.side, s32[8,16]{1,0:T(8,128)S(1)} %copy-done.1, s32[8,16]{1,0:T(8,128)S(1)} %copy-done.2, s32[8]{0:T(128)S(1)} %and_select_fusion.slots, bf16[8,16,64,128]{3,2,1,0:T(8,128)(2,1)S(1)} %copy-done, ...), custom_call_target="tpu_custom_call" | custom-call | tf_op jit(solution)/shard_map/outer/pallas_call | solution.py:283
  32.9 1.9 %collective-permute-start.4 = (bf16[4,128,256]{2,1,0:T(8,128)(2,1)S(1)}, bf16[4,128,256]{2,1,0:T(8,128)(2,1)S(1)}, u32[]{:S(2)}, u32[]{:S(2)}) collective-permute-start(bf16[4,128,256]{2,1,0:T(8,128)(2,1)S(1)} %get-tuple-element.40), channel_id=1, source_target_pairs={{0,4},{4,0},{8,12},{12,8},{16,20},{20,16},{24,28},{28,24},{32,36},... | collective-permute-start | bytes 786440 | tf_op jit(solution)/shard_map/ppermute | solution.py:345
  34.9 1.5 %collective-permute-done.4 = bf16[4,128,256]{2,1,0:T(8,128)(2,1)S(1)} collective-permute-done((bf16[4,128,256]{2,1,0:T(8,128)(2,1)S(1)}, bf16[4,128,256]{2,1,0:T(8,128)(2,1)S(1)}, u32[]{:S(2)}, u32[]{:S(2)}) %collective-permute-start.4) | collective-permute-done | bytes 262176 | tf_op jit(solution)/shard_map/ppermute | solution.py:345
  36.4 0.1 maximum_select_fusion
  36.5 2.9 %collective-permute-start.5 = (bf16[128,512]{1,0:T(8,128)(2,1)S(1)}, bf16[128,512]{1,0:T(8,128)(2,1)S(1)}, u32[]{:S(2)}, u32[]{:S(2)}) collective-permute-start(bf16[128,512]{1,0:T(8,128)(2,1)S(1)} %get-tuple-element.41), channel_id=1, source_target_pairs={{0,500},{4,16},{8,508},{12,24},{16,4},{20,32},{24,12},{28,40},{32,... | collective-permute-start | bytes 393224 | tf_op jit(solution)/shard_map/ppermute | solution.py:357
  39.4 11.1 %collective-permute-start.6 = (bf16[128,512]{1,0:T(8,128)(2,1)S(1)}, bf16[128,512]{1,0:T(8,128)(2,1)S(1)}, u32[]{:S(2)}, u32[]{:S(2)}) collective-permute-start(bf16[128,512]{1,0:T(8,128)(2,1)S(1)} %get-tuple-element.42), channel_id=1, source_target_pairs={{0,508},{4,8},{8,4},{12,16},{16,12},{20,24},{24,20},{28,32},{32,28... | collective-permute-start | bytes 393224 | tf_op jit(solution)/shard_map/ppermute | solution.py:355
  50.5 1.9 %collective-permute-start.7 = (bf16[128,512]{1,0:T(8,128)(2,1)S(1)}, bf16[128,512]{1,0:T(8,128)(2,1)S(1)}, u32[]{:S(2)}, u32[]{:S(2)}) collective-permute-start(bf16[128,512]{1,0:T(8,128)(2,1)S(1)} %get-tuple-element.44), channel_id=1, source_target_pairs={{0,504},{4,12},{8,0},{12,20},{16,8},{20,28},{24,16},{28,36},{32,24... | collective-permute-start | bytes 393224 | tf_op jit(solution)/shard_map/ppermute | solution.py:359
  52.5 0.0 collective-permute-done.5
  52.5 0.7 %collective-permute-done.6 = bf16[128,512]{1,0:T(8,128)(2,1)S(1)} collective-permute-done((bf16[128,512]{1,0:T(8,128)(2,1)S(1)}, bf16[128,512]{1,0:T(8,128)(2,1)S(1)}, u32[]{:S(2)}, u32[]{:S(2)}) %collective-permute-start.6) | collective-permute-done | bytes 131104 | tf_op jit(solution)/shard_map/ppermute | solution.py:355
  53.2 6.4 %collective-permute-done.7 = bf16[128,512]{1,0:T(8,128)(2,1)S(1)} collective-permute-done((bf16[128,512]{1,0:T(8,128)(2,1)S(1)}, bf16[128,512]{1,0:T(8,128)(2,1)S(1)}, u32[]{:S(2)}, u32[]{:S(2)}) %collective-permute-start.7) | collective-permute-done | bytes 131104 | tf_op jit(solution)/shard_map/ppermute | solution.py:359
  59.6 0.9 %maximum_select_fusion.1 = bf16[1,1,4,128,512]{4,3,2,1,0:T(8,128)(2,1)} fusion(bf16[1,1,1,128,512]{4,3,2,1,0:T(8,128)(2,1)S(1)} %bitcast.16, bf16[1,1,1,128,512]{4,3,2,1,0:T(8,128)(2,1)S(1)} %get-tuple-element.43, bf16[1,1,1,128,512]{4,3,2,1,0:T(8,128)(2,1)S(1)} %bitcast.15, bf16[1,1,1,128,512]{4,3,2,1,0:T(8,128)(2,1)S(1)} %bitcast.14, pred[]{:T(512)S(6)} %eq.12), kind=kLoop, calls=%fused_computation.1 | loop fusion | flops 1835008 | bytes 1048577 | tf_op jit(solution)/shard_map/jit(_where)/select_n | solution.py:361
  (7 shorter events, 0.2 us)
Async XLA Ops:
  0.0 8.3 %copy-start.6 = (s32[64,1,8]{0,2,1:T(8,128)S(1)}, s32[64,1,8]{0,2,1:T(8,128)}, u32[]{:S(2)}) copy-start(s32[64,1,8]{0,2,1:T(8,128)} %param.15) | copy-start | bytes 6148
  0.0 8.5 %copy-start.7 = (f32[64]{0:T(128)S(1)}, f32[64]{0:T(128)}, u32[]{:S(2)}) copy-start(f32[64]{0:T(128)} %param.12) | copy-start | bytes 772
  0.0 8.6 %copy-start.5 = (f32[128]{0:T(128)S(1)}, f32[128]{0:T(128)}, u32[]{:S(2)}) copy-start(f32[128]{0:T(128)} %param.14) | copy-start | bytes 1540
  0.0 8.6 %copy-start.4 = (bf16[8,64,128]{2,1,0:T(8,128)(2,1)S(1)}, bf16[8,64,128]{2,1,0:T(8,128)(2,1)}, u32[]{:S(2)}) copy-start(bf16[8,64,128]{2,1,0:T(8,128)(2,1)} %dw.1) | copy-start | bytes 393220
  0.0 8.6 %copy-start.3 = (bf16[3,3,3,64,64]{4,3,2,1,0:T(8,128)(2,1)S(1)}, bf16[3,3,3,64,64]{4,3,2,1,0:T(8,128)(2,1)}, u32[]{:S(2)}) copy-start(bf16[3,3,3,64,64]{4,3,2,1,0:T(8,128)(2,1)} %cw.1) | copy-start | bytes 663556
  1.2 9.8 %collective-permute-start.1 = (bf16[8,64,128]{2,1,0:T(8,128)(2,1)S(1)}, bf16[8,64,128]{2,1,0:T(8,128)(2,1)S(1)}, u32[]{:S(2)}, u32[]{:S(2)}) collective-permute-start(bf16[8,64,128]{2,1,0:T(8,128)(2,1)S(1)} %get-tuple-element.49), channel_id=1, source_target_pairs={{1,2},{2,1},{5,6},{6,5},{9,10},{10,9},{13,14},{14,13},{17,18},{18,... | collective-permute-start | bytes 393224 | tf_op jit(solution)/shard_map/ppermute | solution.py:320
  1.9 9.1 %collective-permute-start = (bf16[8,64,128]{2,1,0:T(8,128)(2,1)S(1)}, bf16[8,64,128]{2,1,0:T(8,128)(2,1)S(1)}, u32[]{:S(2)}, u32[]{:S(2)}) collective-permute-start(bf16[8,64,128]{2,1,0:T(8,128)(2,1)S(1)} %get-tuple-element.50), channel_id=1, source_target_pairs={{0,1},{2,3},{1,0},{3,2},{4,5},{6,7},{5,4},{7,6},{8,9},{10,11},{9,8... | collective-permute-start | bytes 393224 | tf_op jit(solution)/shard_map/ppermute | solution.py:319
  8.6 10.9 %copy-start = (bf16[8,16,64,128]{3,2,1,0:T(8,128)(2,1)S(1)}, bf16[8,16,64,128]{3,2,1,0:T(8,128)(2,1)}, u32[]{:S(2)}) copy-start(bf16[8,16,64,128]{3,2,1,0:T(8,128)(2,1)} %vox.7) | copy-start | bytes 6291460
  8.6 10.9 %copy-start.1 = (s32[8,16]{1,0:T(8,128)S(1)}, s32[8,16]{1,0:T(8,128)}, u32[]{:S(2)}) copy-start(s32[8,16]{1,0:T(8,128)} %lo_all.5) | copy-start | bytes 1540
  8.7 10.9 %copy-start.2 = (s32[8,16]{1,0:T(8,128)S(1)}, s32[8,16]{1,0:T(8,128)}, u32[]{:S(2)}) copy-start(s32[8,16]{1,0:T(8,128)} %hi_all.5) | copy-start | bytes 1540
  11.1 14.9 %collective-permute-start.2 = (bf16[18,64,128]{2,1,0:T(8,128)(2,1)S(1)}, bf16[18,64,128]{2,1,0:T(8,128)(2,1)S(1)}, u32[]{:S(2)}, u32[]{:S(2)}) collective-permute-start(bf16[18,64,128]{2,1,0:T(8,128)(2,1)S(1)} %pad_maximum_fusion), channel_id=1, source_target_pairs={{0,4},{8,12},{16,20},{24,28},{32,36},{40,44},{48,52},{56,60},{64,6... | collective-permute-start | bytes 884744 | tf_op jit(solution)/shard_map/ppermute | solution.py:333
  17.6 8.4 %collective-permute-start.3 = (bf16[18,64,128]{2,1,0:T(8,128)(2,1)S(1)}, bf16[18,64,128]{2,1,0:T(8,128)(2,1)S(1)}, u32[]{:S(2)}, u32[]{:S(2)}) collective-permute-start(bf16[18,64,128]{2,1,0:T(8,128)(2,1)S(1)} %pad_maximum_fusion.1), channel_id=1, source_target_pairs={{4,8},{12,16},{20,24},{28,32},{36,40},{44,48},{52,56},{60,64},{68,... | collective-permute-start | bytes 884744 | tf_op jit(solution)/shard_map/ppermute | solution.py:334
  32.9 3.4 %collective-permute-start.4 = (bf16[4,128,256]{2,1,0:T(8,128)(2,1)S(1)}, bf16[4,128,256]{2,1,0:T(8,128)(2,1)S(1)}, u32[]{:S(2)}, u32[]{:S(2)}) collective-permute-start(bf16[4,128,256]{2,1,0:T(8,128)(2,1)S(1)} %get-tuple-element.40), channel_id=1, source_target_pairs={{0,4},{4,0},{8,12},{12,8},{16,20},{20,16},{24,28},{28,24},{32,36},... | collective-permute-start | bytes 786440 | tf_op jit(solution)/shard_map/ppermute | solution.py:345
  36.5 15.9 %collective-permute-start.5 = (bf16[128,512]{1,0:T(8,128)(2,1)S(1)}, bf16[128,512]{1,0:T(8,128)(2,1)S(1)}, u32[]{:S(2)}, u32[]{:S(2)}) collective-permute-start(bf16[128,512]{1,0:T(8,128)(2,1)S(1)} %get-tuple-element.41), channel_id=1, source_target_pairs={{0,500},{4,16},{8,508},{12,24},{16,4},{20,32},{24,12},{28,40},{32,... | collective-permute-start | bytes 393224 | tf_op jit(solution)/shard_map/ppermute | solution.py:357
  39.4 13.7 %collective-permute-start.6 = (bf16[128,512]{1,0:T(8,128)(2,1)S(1)}, bf16[128,512]{1,0:T(8,128)(2,1)S(1)}, u32[]{:S(2)}, u32[]{:S(2)}) collective-permute-start(bf16[128,512]{1,0:T(8,128)(2,1)S(1)} %get-tuple-element.42), channel_id=1, source_target_pairs={{0,508},{4,8},{8,4},{12,16},{16,12},{20,24},{24,20},{28,32},{32,28... | collective-permute-start | bytes 393224 | tf_op jit(solution)/shard_map/ppermute | solution.py:355
  50.5 9.1 %collective-permute-start.7 = (bf16[128,512]{1,0:T(8,128)(2,1)S(1)}, bf16[128,512]{1,0:T(8,128)(2,1)S(1)}, u32[]{:S(2)}, u32[]{:S(2)}) collective-permute-start(bf16[128,512]{1,0:T(8,128)(2,1)S(1)} %get-tuple-element.44), channel_id=1, source_target_pairs={{0,504},{4,12},{8,0},{12,20},{16,8},{20,28},{24,16},{28,36},{32,24... | collective-permute-start | bytes 393224 | tf_op jit(solution)/shard_map/ppermute | solution.py:359
